TPU v7x, 128 devices: a whole 4x4x4 slice. The times are simulated.
128 devices in a mesh: grp: 8 (over x, core), dev: 16 (over y, z).
Axes of the slice: x: 4, y: 4, z: 4, core: 2. Of those that a mesh axis runs over, the one named last changes fastest.
Arguments:
- ref_pos: float32 [3, 1048576], P(None, ('grp', 'dev')), may hold values from -4 to 4
- displacement: float32 [3, 1048576], P(None, ('grp', 'dev')), may hold values from -0.6 to 0.6
- velocity: float32 [3, 1048576], P(None, ('grp', 'dev')), may hold values from -6 to 6
- node_mass: float32 [1048576], P(('grp', 'dev')), may hold values from 0.5 to 2
- elem_nodes: int32 [4, 1048576], P(None, ('grp', 'dev')), may hold values from 0 to 8191
- elem_part: int32 [1048576], P(('grp', 'dev')), may hold values from 0 to 511, as said below
- elem_scale: float32 [1048576], P(('grp', 'dev')), may hold values from 0.5 to 2
- part_stiff: float32 [512], P(('grp', 'dev')), may hold values from 1 to 100
- shared: int32 [2, 262144], P(None, ('grp', 'dev')), may hold values from 0 to 8191, as said below
- seg_node: int32 [8192, 128], P(('grp', 'dev')), may hold values from 0 to 8191
- seg_mask: int32 [8192, 128], P(('grp', 'dev')), may hold values 0 or 1
- send_blk: int32 [128, 128, 5], P(('grp', 'dev')), may hold values from 0 to 63
- pair_a: int32 [65536], P(('grp', 'dev')), may hold values from 0 to 63
- pair_slot: int32 [65536], P(('grp', 'dev')), may hold values from 0 to 639
- pair_mask: int32 [65536], P(('grp', 'dev')), may hold values from 0 to 1, as said below
Outputs:
- new_displace: float32 [3, 1048576], P(None, ('grp', 'dev'))
- new_velocity: float32 [3, 1048576], P(None, ('grp', 'dev'))
Inputs may be any that keep to these rules, and one draw needn't show every extreme that they name: `elem_part`: the elements of device d belong to parts d * 4 to (d + 1) * 4 - 1. `shared`: the 4096 entries of one device are different nodes; row 1 of device k and row 0 of device k + 1 of the same group name the same physical nodes, entry by entry. `pair_mask`: in each device's 512 pair slots the live ones come first; each device has 128 or more live, and some device has all 512 live.
All inputs are finite; a program needn't handle non-finite values. No bound on the sum of `seg_mask` on one device may be relied on, other than what follows from the above.
Results may differ from a plain program's by a relative error of at most 0.000062.
Values sent between devices are 32-bit elements; how exact they have to be, the bound alone decides.
No kernel may reach another device: no remote copies, remote signals or barrier semaphores. Data moves between devices by JAX's collectives and lax.ppermute only.
A program may use at most 128 MiB of HBM per device.

v0:
```python
import math

import jax
import jax.numpy as jnp
from jax import lax
from jax.sharding import PartitionSpec as P

SPRINGS = ((0, 1, 1.0), (1, 2, 1.0), (2, 3, 1.0), (3, 0, 1.0), (0, 2, 0.5), (1, 3, 0.5))
COURANT = 0.5
EXACT = lax.Precision.HIGHEST


def in_one_piece(arrays, axis, split_dim, concat_dim, along):
    columns = [a.reshape(*a.shape[:along], -1) for a in arrays]
    both = jnp.concatenate(columns, axis=along)
    filled, at, gathered = (
        lax.all_to_all(both, axis, split_axis=split_dim, concat_axis=concat_dim, tiled=True),
        0,
        [],
    )
    for a, column in zip(arrays, columns):
        piece = filled[..., at : at + column.shape[along]]
        gathered.append(piece.reshape(*piece.shape[:along], *a.shape[along:]))
        at += column.shape[along]
    return tuple(gathered)


def shifted(value, axis, steps):
    count = lax.axis_size(axis)
    first, last = (max(0, -steps), min(count, count - steps))
    return lax.ppermute(value, axis, [(source, source + steps) for source in range(first, last)])


def one_hot_rows(index_list, count):
    return (jnp.arange(count, dtype=jnp.int32)[:, None] == index_list[None, :]).astype(jnp.float32)


def pick_dot(selector, table):
    return jnp.dot(selector, table, precision=EXACT, preferred_element_type=jnp.float32)


def corner_forces(corner, elem_stiff):
    corner_force = [jnp.zeros_like(corner[:, 0]) for corner_index in range(4)]
    for head_node, tail_node, weight in SPRINGS:
        pull_term = weight * elem_stiff * (corner[:, tail_node] - corner[:, head_node])
        corner_force[head_node] = corner_force[head_node] + pull_term
        corner_force[tail_node] = corner_force[tail_node] - pull_term
    return jnp.stack(corner_force, 1)


def pair_forces(near_pos, far_pos, near_mask, far_mask, live_pair):
    offset = near_pos[:, :, :, None] - far_pos[:, :, None, :]
    weights = jnp.exp(-jnp.sum(offset * offset, 1))
    weights = weights * (near_mask[:, :, None] * far_mask[:, None, :]) * live_pair[:, None, None]
    pushed = jnp.sum(weights[:, None] * offset, 3)
    recoil = -jnp.sum(weights[:, None] * offset, 2)
    return (pushed, recoil)


def contact_sums(own_blocks, own_mask, recv_blocks, recv_mask, pair_first, pair_second, pair_live):
    pair_count = pair_first.shape[0]
    group_width = math.gcd(pair_count, 32)
    seg_width = own_blocks.shape[2]
    own_count = own_blocks.shape[0]
    recv_count = recv_blocks.shape[0]
    own_table = jnp.concatenate([own_blocks.reshape(own_count, 3 * seg_width), own_mask], 1)
    recv_table = jnp.concatenate([recv_blocks.reshape(recv_count, 3 * seg_width), recv_mask], 1)

    def one_group(group_index):
        group_start = group_index * group_width
        first_ids = lax.dynamic_slice_in_dim(pair_first, group_start, group_width)
        second_ids = lax.dynamic_slice_in_dim(pair_second, group_start, group_width)
        live_part = lax.dynamic_slice_in_dim(pair_live, group_start, group_width)
        near_rows = pick_dot(one_hot_rows(first_ids, own_count).T, own_table)
        far_rows = pick_dot(one_hot_rows(second_ids, recv_count).T, recv_table)
        near_pos = near_rows[:, : 3 * seg_width].reshape(group_width, 3, seg_width)
        far_pos = far_rows[:, : 3 * seg_width].reshape(group_width, 3, seg_width)
        return pair_forces(
            near_pos,
            far_pos,
            near_rows[:, 3 * seg_width :],
            far_rows[:, 3 * seg_width :],
            live_part,
        )

    pushed, recoil = lax.map(one_group, jnp.arange(pair_count // group_width, dtype=jnp.int32))
    pushed = pushed.reshape(pair_count, 3 * seg_width)
    recoil = recoil.reshape(pair_count, 3 * seg_width)
    own_force = pick_dot(one_hot_rows(pair_first, own_count), pushed).reshape(
        own_count, 3, seg_width
    )
    far_force = pick_dot(one_hot_rows(pair_second, recv_count), recoil).reshape(
        recv_count, 3, seg_width
    )
    return (own_force, far_force)


def shards(
    ref_pos,
    displacement,
    velocity,
    node_mass,
    elem_nodes,
    elem_part,
    elem_scale,
    part_stiff,
    shared,
    seg_node,
    seg_mask,
    send_blk,
    pair_a,
    pair_slot,
    pair_mask,
):
    groups = lax.axis_size("grp")
    within = lax.axis_size("dev")
    devices = groups * within
    part_count = part_stiff.shape[0]
    local_part = elem_part - lax.axis_index(("grp", "dev")) * part_count
    chooser = local_part[None, :] == jnp.arange(part_count, dtype=jnp.int32)[:, None]
    elem_stiff = jnp.sum(jnp.where(chooser, part_stiff[:, None], 0.0), 0) * elem_scale
    elem_count = elem_nodes.shape[1]
    block_count = seg_node.shape[0]
    seg_width = seg_node.shape[1]
    node_rows = jnp.concatenate([displacement, node_mass[None, :], ref_pos], 0)
    all_index = jnp.concatenate([elem_nodes.reshape(-1), seg_node.reshape(-1)], 0)
    picked = node_rows[:, all_index]
    corner = picked[0:3, : 4 * elem_count].reshape(3, 4, elem_count)
    elem_mass = jnp.min(picked[3, : 4 * elem_count].reshape(4, elem_count), 0)
    stacked = corner_forces(corner, elem_stiff)
    step_limit = jnp.min(COURANT * jnp.sqrt(elem_mass / elem_stiff))
    seg_rows = picked[:, 4 * elem_count :]
    position = (seg_rows[0:3] + seg_rows[4:7]).reshape(3, block_count, seg_width)
    blocks = jnp.moveaxis(position, 1, 0)
    seg_weight = seg_mask.astype(jnp.float32)
    chosen = send_blk[0]
    outgoing = blocks[chosen]
    out_mask = seg_weight[chosen]
    cap_count = chosen.shape[1]
    stamp = jnp.full((devices, 1), step_limit, jnp.float32)
    arrived, arrived_mask, stamps = in_one_piece(
        (outgoing, out_mask, stamp), ("grp", "dev"), 0, 0, 1
    )
    time_step = jnp.min(stamps)
    own_force, far_force = contact_sums(
        blocks,
        seg_weight,
        arrived.reshape(devices * cap_count, 3, seg_width),
        arrived_mask.reshape(devices * cap_count, seg_width),
        pair_a,
        pair_slot,
        pair_mask.astype(jnp.float32),
    )
    far_grid = far_force.reshape(devices, cap_count, 3, seg_width)
    returned = lax.all_to_all(far_grid, ("grp", "dev"), split_axis=0, concat_axis=0, tiled=True)
    back_force = pick_dot(
        one_hot_rows(chosen.reshape(-1), block_count),
        returned.reshape(devices * cap_count, 3 * seg_width),
    )
    seg_force = own_force + back_force.reshape(block_count, 3, seg_width)
    flat_force = jnp.moveaxis(seg_force, 1, 0).reshape(3, -1)
    all_force = jnp.concatenate([stacked.reshape(3, -1), flat_force], 1)
    totals = jnp.zeros_like(displacement).at[:, all_index].add(all_force)
    share_count = shared.shape[1]
    share_flat = shared.reshape(-1)
    share_rows = totals[:, share_flat]
    upper_rows = share_rows[:, :share_count]
    lower_rows = share_rows[:, share_count:]
    from_lower = shifted(lower_rows, "dev", 1)
    from_upper = shifted(upper_rows, "dev", -1)
    assembled = totals.at[:, share_flat].add(jnp.concatenate([from_lower, from_upper], 1))
    accelerate = assembled / node_mass[None, :]
    new_velocity = velocity + time_step * accelerate
    new_displace = displacement + time_step * new_velocity
    return (new_displace, new_velocity)


def solution(mesh):
    return jax.shard_map(
        shards,
        mesh=mesh,
        in_specs=(
            P(None, ("grp", "dev")),
            P(None, ("grp", "dev")),
            P(None, ("grp", "dev")),
            P(("grp", "dev")),
            P(None, ("grp", "dev")),
            P(("grp", "dev")),
            P(("grp", "dev")),
            P(("grp", "dev")),
            P(None, ("grp", "dev")),
            P(("grp", "dev"), None),
            P(("grp", "dev"), None),
            P(("grp", "dev"), None, None),
            P(("grp", "dev")),
            P(("grp", "dev")),
            P(("grp", "dev")),
        ),
        out_specs=(P(None, ("grp", "dev")), P(None, ("grp", "dev"))),
        check_vma=False,
    )
```

profile of v0, /device:TPU:96, one launch (start us, length us, event | category | flops | bytes accessed | tf_op | source)
XLA Modules:
  0.0 703.9 jit_solution(9541939636037551483)
XLA Ops:
  5.4 137.2 %gather_fusion = f32[40960,7]{1,0:T(8,128)} fusion(f32[7,8192]{0,1:T(8,128)} %copy.148, s32[40960]{0:T(1024)S(1)} %broadcast_clamp_fusion), kind=kCustom, calls=%fused_computation | custom fusion | bytes 2457600 | tf_op jit(solution)/shard_map/gather | solution.py:127
  142.6 6.6 slice_add_fusion
  149.2 11.2 %slice_reduce_fusion = f32[32768]{0:T(1024)S(1)} fusion(f32[7,40960]{0,1:T(8,128)} %bitcast.101), kind=kLoop, calls=%fused_computation.20 | loop fusion | bytes 262144 | tf_op jit(solution)/shard_map/slice | solution.py:129
  173.0 9.9 %all-to-all-start = ((f32[128,1,2561]{2,1,0:T(1,128)}), f32[128,1,2561]{2,1,0:T(1,128)S(1)}, u32[]{:S(2)}, u32[]{:S(2)}) async-start(f32[128,1,2561]{2,1,0:T(1,128)} %copy.151), calls=%async_computation | async-start | bytes 2752512 | tf_op jit(solution)/shard_map/all_to_all | solution.py:17
  182.9 6.5 slice.91
  189.4 5.9 fusion.22
  203.8 2.9 copy.173
  218.0 158.9 %while.12 = (s32[]{:T(128)}, f32[16,32,3,128]{3,2,1,0:T(4,128)}, f32[16,32,3,128]{3,2,1,0:T(4,128)}, s32[16]{0:T(128)S(1)}, s32[512]{0:T(512)S(1)}, /*index=5*/f...) while((s32[]{:T(128)}, f32[16,32,3,128]{3,2,1,0:T(4,128)}, ...), condition=%wide.region_8.9_spmd, body=%wide.region_4.8_spmd.sunk | while | flops 151005184 | bytes 10978639 | solution.py:86
  223.3 4.0 fusion.40
  233.2 4.0 fusion.40
  243.1 4.0 fusion.40
  253.1 4.0 fusion.40
  263.0 4.0 fusion.40
  272.9 4.0 fusion.40
  282.8 4.0 fusion.40
  292.8 4.0 fusion.40
  302.7 4.0 fusion.40
  312.6 4.0 fusion.40
  322.5 4.0 fusion.40
  332.5 4.0 fusion.40
  342.4 4.0 fusion.40
  352.3 4.0 fusion.40
  362.3 4.0 fusion.40
  372.2 4.0 fusion.40
  381.5 9.8 %all-to-all-start.1 = ((f32[128,5,3,128]{3,2,1,0:T(4,128)}), f32[128,5,3,128]{3,2,1,0:T(4,128)S(1)}, u32[]{:S(2)}, u32[]{:S(2)}) async-start(f32[128,5,3,128]{3,2,1,0:T(4,128)} %copy.162), calls=%async_computation.1 | async-start | bytes 2621440 | tf_op jit(solution)/shard_map/all_to_all | solution.py:155
  397.5 13.6 %all-to-all-done.1 = f32[128,5,3,128]{3,2,1,0:T(4,128)S(1)} async-done(((f32[128,5,3,128]{3,2,1,0:T(4,128)}), f32[128,5,3,128]{3,2,1,0:T(4,128)S(1)}, u32[]{:S(2)}, u32[]{:S(2)}) %all-to-all-start.1) | async-done | bytes 983072 | tf_op jit(solution)/shard_map/all_to_all | solution.py:155
  414.6 10.0 %copy.164 = f32[40960,3]{1,0:T(8,128)} copy(f32[40960,3]{0,1:T(4,128)S(1)} %maximum_bitcast_fusion.1) | data formatting | bytes 983040 | tf_op jit(solution)/shard_map/concatenate | solution.py:162
  424.6 219.6 %scatter_custom_fusion = f32[3,8192]{0,1:T(8,128)} fusion(s32[40960]{0:T(1024)} %bitcast.122, f32[40960,3]{1,0:T(8,128)} %copy.164, f32[]{:T(128)} %constant.15.clone.1), kind=kCustom, calls=%fused_computation.22 | custom fusion | flops 122880 | bytes 98816 | tf_op jit(solution)/shard_map/scatter-add | solution.py:163
  644.2 16.3 %gather_fusion.3 = f32[4096,3]{1,0:T(8,128)} fusion(f32[3,8192]{0,1:T(8,128)} %scatter_custom_fusion, s32[4096]{0:T(1024)S(1)} %broadcast_clamp_fusion.1), kind=kCustom, calls=%fused_computation.3 | custom fusion | bytes 114688 | tf_op jit(solution)/shard_map/gather | solution.py:166
  667.0 6.0 collective-permute-start
  675.2 24.2 %scatter_fusion = f32[3,8192]{0,1:T(8,128)} fusion(f32[3,8192]{0,1:T(8,128)} %scatter_custom_fusion, s32[4096]{0:T(1024)S(1)} %bitcast.127, f32[4096,3]{1,0:T(8,128)S(1)} %copy.167), kind=kCustom, calls=%fused_computation.5 | custom fusion | flops 12288 | bytes 163840 | tf_op jit(solution)/shard_map/scatter-add | solution.py:171
  699.5 2.9 copy.168
  (345 shorter events, 144.6 us)
Async XLA Ops:
  1.7 2.7 copy-start.4
  1.7 2.8 copy-start.6
  4.7 0.7 copy-start.1
  149.2 11.3 %copy-start.7 = (s32[64,128]{1,0:T(8,128)S(1)}, s32[64,128]{1,0:T(8,128)}, u32[]{:S(2)}) copy-start(s32[64,128]{1,0:T(8,128)} %param.27) | copy-start | bytes 98308
  149.2 11.3 %copy-start.11 = (s32[1,128,5]{1,0,2:T(1,128)S(1)}, s32[1,128,5]{1,0,2:T(1,128)}, u32[]{:S(2)}) copy-start(s32[1,128,5]{1,0,2:T(1,128)} %param.28) | copy-start | bytes 7684
  165.4 3.5 copy-start.8
  165.4 3.5 copy-start.15
  168.2 0.9 copy-start.9
  173.0 36.2 %all-to-all-start = ((f32[128,1,2561]{2,1,0:T(1,128)}), f32[128,1,2561]{2,1,0:T(1,128)S(1)}, u32[]{:S(2)}, u32[]{:S(2)}) async-start(f32[128,1,2561]{2,1,0:T(1,128)} %copy.151), calls=%async_computation | async-start | bytes 2752512 | tf_op jit(solution)/shard_map/all_to_all | solution.py:17
  203.8 3.6 copy-start.13
  206.7 2.4 copy-start.10
  214.2 3.8 copy-start.12
  214.2 3.8 copy-start.14
  381.5 29.6 %all-to-all-start.1 = ((f32[128,5,3,128]{3,2,1,0:T(4,128)}), f32[128,5,3,128]{3,2,1,0:T(4,128)S(1)}, u32[]{:S(2)}, u32[]{:S(2)}) async-start(f32[128,5,3,128]{3,2,1,0:T(4,128)} %copy.162), calls=%async_computation.1 | async-start | bytes 2621440 | tf_op jit(solution)/shard_map/all_to_all | solution.py:155
  412.1 2.3 copy-start
  664.7 9.0 %collective-permute-start.1 = (f32[3,2048]{1,0:T(4,128)S(1)}, f32[3,2048]{1,0:T(4,128)S(1)}, u32[]{:S(2)}, u32[]{:S(2)}) collective-permute-start(f32[3,2048]{1,0:T(4,128)S(1)} %copy.166), channel_id=1, source_target_pairs={{1,0},{2,1},{3,2},{4,3},{5,4},{6,5},{7,6},{8,7},{9,8},{10,9},{11,1... | collective-permute-start | bytes 73736 | tf_op jit(solution)/shard_map/ppermute | solution.py:31
  667.0 7.6 %collective-permute-start = (f32[3,2048]{1,0:T(4,128)S(1)}, f32[3,2048]{1,0:T(4,128)S(1)}, u32[]{:S(2)}, u32[]{:S(2)}) collective-permute-start(f32[3,2048]{1,0:T(4,128)S(1)} %copy.165), channel_id=1, source_target_pairs={{0,1},{1,2},{2,3},{3,4},{4,5},{5,6},{6,7},{7,8},{8,9},{9,10},{10,1... | collective-permute-start | bytes 73736 | tf_op jit(solution)/shard_map/ppermute | solution.py:31
  699.5 2.9 copy-start.2
  699.5 2.9 copy-start.3
  699.5 2.9 copy-start.5
where the time goes:
time: 709 us; the launch traced here: 704 us
  other arithmetic  377 us (53%)
  local copies, waits for them, and re-layouts  255 us (36%)
  starting transfers between devices  27.6 us (4%)
  matrix products  16.9 us (2%)
  waiting for transfers between devices  14.5 us (2%)
  loops' own time  11.7 us (2%)
    scatter-add x1, other arithmetic, shards(): totals = jnp.zeros_like(displacement).at[:, all_index].add(all_force)  220 us
    gather x1, local copies, waits for them, and re-layouts, shards(): picked = node_rows[:, all_index]  137 us
    reduce_sum x16, other arithmetic, pair_forces(): recoil = -jnp.sum(weights[:, None] * offset, 2)  63.9 us
    reduce_sum x16, other arithmetic, pair_forces(): weights = jnp.exp(-jnp.sum(offset * offset, 1))  33 us
    scatter-add x1, other arithmetic, shards(): totals.at[:, share_flat].add(jnp.concatenate([from_lower, from_upper], 1))  24.2 us
    unnamed x45, local copies, waits for them, and re-layouts  18.1 us
    dot_general x35, matrix products, pick_dot(): jnp.dot(selector, table, precision=EXACT, preferred_element_type=jnp.floa...  16.9 us
    gather x1, local copies, waits for them, and re-layouts, shards(): share_rows = totals[:, share_flat]  16.3 us
  transfers between devices with their start and end apart: 4, of which 2 were waited for; matrix products, arithmetic and copies ran while one was open for 5% of the time, Pallas kernels for 0%

commit v1 on v0

v1 whole, which is shorter than its diff:
```python
import math
from functools import partial

import jax
import jax.numpy as jnp
from jax import lax
from jax.experimental import pallas as pl
from jax.experimental.pallas import tpu as pltpu
from jax.sharding import PartitionSpec as P

SPRINGS = ((0, 1, 1.0), (1, 2, 1.0), (2, 3, 1.0), (3, 0, 1.0), (0, 2, 0.5), (1, 3, 0.5))
COURANT = 0.5
LOW = 256
PIECES = 3
SCALE = math.sqrt(math.log2(math.e))
PARK = 1.0e3
f32 = jnp.float32
bf16 = jnp.bfloat16


def pieces_of(x, count=PIECES):
    out = []
    for _ in range(count):
        head = x.astype(bf16)
        out.append(head)
        x = x - head.astype(f32)
    return out


def low_hot(idx):
    low = idx & (LOW - 1)
    rows = lax.broadcasted_iota(jnp.int32, (LOW, idx.shape[1]), 0)
    return jnp.where(rows == low, 1.0, 0.0).astype(bf16)


def high_mask(idx, high):
    rows = lax.broadcasted_iota(jnp.int32, (high, idx.shape[1]), 0)
    return rows == (idx >> 8)


def fill_table(tab, at, ref, row, high):
    for h in range(high):
        tab[at + h : at + h + 1, :] = ref[row : row + 1, h * LOW : (h + 1) * LOW]


def split_table(cut, tab):
    rows = tab.shape[0]
    for p, piece in enumerate(pieces_of(tab[...])):
        cut[p * rows : (p + 1) * rows, :] = piece


def pick(cut, hot, mask, comps, high):
    found = jnp.dot(cut[...], hot, preferred_element_type=f32)
    rows = comps * high
    found = (found[:rows] + found[rows : 2 * rows]) + found[2 * rows :]
    return [
        jnp.sum(jnp.where(mask, found[c * high : (c + 1) * high], 0.0), 0, keepdims=True)
        for c in range(comps)
    ]


def spread(force, mask, high):
    rows = [[], [], []]
    for value in force:
        wide = jnp.broadcast_to(value, mask.shape)
        for p, piece in enumerate(pieces_of(jnp.where(mask, wide, 0.0))):
            rows[p].append(piece)
    return jnp.concatenate(rows[0] + rows[1] + rows[2], 0)


def add_hot(left, hot):
    return lax.dot_general(left, hot, (((1,), (1,)), ((), ())), preferred_element_type=f32)


def send_body(send_ref, disp_ref, ref_ref, seg_ref, mask_ref, own_ref, out_ref, tab, cut):
    high = disp_ref.shape[1] // LOW
    blocks = seg_ref.shape[0]
    for c in range(3):
        fill_table(tab, c * high, disp_ref, c, high)
    for c in range(3):
        for h in range(high):
            at = c * high + h
            tab[at : at + 1, :] += ref_ref[c : c + 1, h * LOW : (h + 1) * LOW]
    split_table(cut, tab)
    group = 8

    def some(g, carry):
        base = pl.multiple_of(g * group, group)
        seg = seg_ref[pl.ds(base, group), :]
        idx = jnp.concatenate([seg[k : k + 1] for k in range(group)], 1)
        xyz = pick(cut, low_hot(idx), high_mask(idx, high), 3, high)
        weight = mask_ref[pl.ds(base, group), :].astype(f32)
        for k in range(group):
            for c in range(3):
                own_ref[base + k, c : c + 1, :] = xyz[c][:, k * 128 : (k + 1) * 128]
            own_ref[base + k, 3:4, :] = weight[k : k + 1]
        return carry

    lax.fori_loop(0, blocks // group, some, 0)
    peers, cap = out_ref.shape[0], out_ref.shape[1]

    def send(d, carry):
        for c in range(cap):
            out_ref[d, c] = own_ref[send_ref[d * cap + c]]
        return carry

    lax.fori_loop(0, peers, send, 0, unroll=4)


def element_body(
    first_ref, stiff_ref, disp_ref, mass_ref, nodes_ref, part_ref, scale_ref, tot_ref, lim_ref, tab, cut, acc
):
    high = disp_ref.shape[1] // LOW
    width = 256
    parts = stiff_ref.shape[0]
    for c in range(3):
        fill_table(tab, c * high, disp_ref, c, high)
    fill_table(tab, 3 * high, mass_ref, 0, high)
    split_table(cut, tab)
    acc[...] = jnp.zeros_like(acc)

    def some(g, limit):
        at = pl.ds(pl.multiple_of(g * width, width), width)
        part = part_ref[:, at] - first_ref[0]
        stiff = jnp.zeros(part.shape, f32)
        for k in range(parts):
            stiff = jnp.where(part == k, stiff_ref[k], stiff)
        stiff = stiff * scale_ref[:, at]
        nodes = nodes_ref[:, at]
        idx = jnp.concatenate([nodes[k : k + 1] for k in range(4)], 1)
        hot = low_hot(idx)
        mask = high_mask(idx, high)
        found = pick(cut, hot, mask, 4, high)
        corner = [[found[c][:, k * width : (k + 1) * width] for c in range(4)] for k in range(4)]
        mass = jnp.minimum(
            jnp.minimum(corner[0][3], corner[1][3]), jnp.minimum(corner[2][3], corner[3][3])
        )
        force = [[jnp.zeros((1, width), f32)] * 3 for _ in range(4)]
        for head, tail, weight in SPRINGS:
            pull = weight * stiff
            for c in range(3):
                term = pull * (corner[tail][c] - corner[head][c])
                force[head][c] = force[head][c] + term
                force[tail][c] = force[tail][c] - term
        joined = [jnp.concatenate([force[k][c] for k in range(4)], 1) for c in range(3)]
        acc[...] += add_hot(spread(joined, mask, high), hot)
        return jnp.minimum(limit, COURANT * jnp.sqrt(mass / stiff))

    limit = lax.fori_loop(
        0, nodes_ref.shape[1] // width, some, jnp.full((1, width), jnp.inf, f32)
    )
    rows = 3 * high
    tot_ref[...] = (acc[2 * rows :] + acc[rows : 2 * rows]) + acc[:rows]
    lim_ref[...] = jnp.broadcast_to(jnp.min(limit, 1, keepdims=True), lim_ref.shape)


def contact_body(
    near_ref, far_ref, own_ref, recv_ref, live_ref, lim_ref, own_out, far_out, wide, total, remote
):
    blocks = own_ref.shape[0]
    slots = recv_ref.shape[0]
    seg = own_ref.shape[2]
    cap = 5

    def park(block):
        weight = block[3:4]
        out = [jnp.where(weight > 0.5, block[0:1] * SCALE, PARK)]
        return out + [block[c : c + 1] * SCALE for c in range(1, 3)]

    def widen(b, carry):
        rows = park(own_ref[b])
        for c in range(3):
            wide[b, c] = jnp.broadcast_to(rows[c], (seg, seg)).T
            total[b, c] = jnp.zeros((seg, seg), f32)
        return carry

    lax.fori_loop(0, blocks, widen, 0)

    def ready(s, carry):
        block = recv_ref[s]
        remote[s, 0:1] = jnp.where(block[3:4] > 0.5, block[0:1] * SCALE, -PARK)
        for c in range(1, 3):
            remote[s, c : c + 1] = block[c : c + 1] * SCALE
        return carry

    lax.fori_loop(0, slots, ready, 0, unroll=4)
    far_out[...] = jnp.zeros_like(far_out)
    far_out[:, 15:16, :] = jnp.broadcast_to(lim_ref[...][None], (far_out.shape[0], 1, seg))
    live = jnp.sum(live_ref[...])

    def pair(p, carry):
        b = near_ref[p]
        s = far_ref[p]
        there = [jnp.broadcast_to(remote[s, c : c + 1, :], (8, seg)) for c in range(3)]
        recoil = [None] * 3
        for v in range(seg // 8):
            at = pl.ds(v * 8, 8)
            gap = [wide[b, c, at, :] - there[c] for c in range(3)]
            far = gap[0] * gap[0] + gap[1] * gap[1] + gap[2] * gap[2]
            weight = jnp.exp2(-far)
            for c in range(3):
                push = weight * gap[c]
                total[b, c, at, :] += push
                recoil[c] = push if recoil[c] is None else recoil[c] + push
        d = (s * 52429) >> 18
        row = (s - d * cap) * 3
        for c in range(3):
            far_out[d, pl.ds(row + c, 1), :] -= jnp.sum(recoil[c], 0, keepdims=True) * (1.0 / SCALE)
        return carry

    lax.fori_loop(0, live, pair, 0)

    def close(b, carry):
        for c in range(3):
            own_out[b, c : c + 1, :] = jnp.sum(total[b, c].T, 0, keepdims=True) * (1.0 / SCALE)
        return carry

    lax.fori_loop(0, blocks, close, 0)


def seg_body(
    send_ref, back_ref, own_ref, seg_ref, int_ref, share_ref, tot_ref, low_ref, up_ref, lim_ref, sums, cut, acc
):
    blocks = own_ref.shape[0]
    peers = back_ref.shape[0]
    cap = 5
    high = int_ref.shape[0] // 3
    sums[...] = jnp.zeros_like(sums)

    def take(d, carry):
        for c in range(cap):
            b = send_ref[d * cap + c]
            sums[c, b, 0:3, :] += back_ref[d, 3 * c : 3 * c + 3, :]
        return carry

    lax.fori_loop(0, peers, take, 0)
    acc[...] = jnp.zeros_like(acc)
    group = 8

    def some(g, carry):
        base = pl.multiple_of(g * group, group)
        seg = seg_ref[pl.ds(base, group), :]
        idx = jnp.concatenate([seg[k : k + 1] for k in range(group)], 1)
        blocks_in = []
        for k in range(group):
            b = base + k
            part = sums[0, b, 0:3] + sums[1, b, 0:3] + sums[2, b, 0:3] + sums[3, b, 0:3] + sums[4, b, 0:3]
            blocks_in.append(part + own_ref[b])
        force = jnp.concatenate(blocks_in, 1)
        left = spread([force[c : c + 1] for c in range(3)], high_mask(idx, high), high)
        acc[...] += add_hot(left, low_hot(idx))
        return carry

    lax.fori_loop(0, blocks // group, some, 0)
    rows = 3 * high
    tot_ref[...] = ((acc[2 * rows :] + acc[rows : 2 * rows]) + acc[:rows]) + int_ref[...]
    split_table(cut, tot_ref)
    count = share_ref.shape[1]
    for row, out in ((0, low_ref), (1, up_ref)):
        for at in range(0, count, 1024):
            idx = share_ref[row : row + 1, at : at + 1024]
            picked = pick(cut, low_hot(idx), high_mask(idx, high), 3, high)
            for c in range(3):
                out[c : c + 1, at : at + 1024] = picked[c]
    lim = jnp.min(back_ref[:, 15, :], 0, keepdims=True)
    lim_ref[...] = lim


def last_body(
    lim_ref, tot_ref, share_ref, low_ref, up_ref, vel_ref, disp_ref, mass_ref, new_disp, new_vel, acc
):
    high = tot_ref.shape[0] // 3
    count = share_ref.shape[1]
    total = jnp.zeros(acc.shape, f32)
    for row, src in ((0, low_ref), (1, up_ref)):
        for at in range(0, count, 1024):
            idx = share_ref[row : row + 1, at : at + 1024]
            force = [src[c : c + 1, at : at + 1024] for c in range(3)]
            total = total + add_hot(spread(force, high_mask(idx, high), high), low_hot(idx))
    rows = 3 * high
    acc[0:rows] = ((total[2 * rows :] + total[rows : 2 * rows]) + total[:rows]) + tot_ref[...]
    step = jnp.min(lim_ref[...], 1, keepdims=True)
    for h in range(high):
        at = slice(h * LOW, (h + 1) * LOW)
        mass = mass_ref[0:1, at]
        for c in range(3):
            vel = vel_ref[c : c + 1, at] + step * (acc[c * high + h : c * high + h + 1, :] / mass)
            new_vel[c : c + 1, at] = vel
            new_disp[c : c + 1, at] = disp_ref[c : c + 1, at] + step * vel


def vmem(count):
    return [pl.BlockSpec(memory_space=pltpu.VMEM)] * count


def smem(count):
    return [pl.BlockSpec(memory_space=pltpu.SMEM)] * count


def struct(*shape):
    return jax.ShapeDtypeStruct(shape, f32)


def send_call(send, disp, ref_pos, seg_node, seg_mask, peers):
    high = disp.shape[1] // LOW
    blocks, seg = seg_node.shape
    return pl.pallas_call(
        send_body,
        out_shape=(struct(blocks, 4, seg), struct(peers, send.shape[0] // peers, 4, seg)),
        in_specs=smem(1) + vmem(4),
        out_specs=tuple(vmem(2)),
        scratch_shapes=[
            pltpu.VMEM((3 * high, LOW), f32),
            pltpu.VMEM((PIECES * 3 * high, LOW), bf16),
        ],
    )(send, disp, ref_pos, seg_node, seg_mask)


def element_call(first, stiff, disp, mass, nodes, part, scale):
    high = disp.shape[1] // LOW
    return pl.pallas_call(
        element_body,
        out_shape=(struct(3 * high, LOW), struct(1, 128)),
        in_specs=smem(2) + vmem(5),
        out_specs=tuple(vmem(2)),
        scratch_shapes=[
            pltpu.VMEM((4 * high, LOW), f32),
            pltpu.VMEM((PIECES * 4 * high, LOW), bf16),
            pltpu.VMEM((PIECES * 3 * high, LOW), f32),
        ],
    )(first, stiff, disp, mass, nodes, part, scale)


def contact_call(pair_a, pair_slot, own, recv, live, lim, peers):
    blocks, _, seg = own.shape
    slots = recv.shape[0]
    return pl.pallas_call(
        contact_body,
        out_shape=(struct(blocks, 3, seg), struct(peers, 16, seg)),
        in_specs=smem(2) + vmem(4),
        out_specs=tuple(vmem(2)),
        scratch_shapes=[
            pltpu.VMEM((blocks, 3, seg, seg), f32),
            pltpu.VMEM((blocks, 3, seg, seg), f32),
            pltpu.VMEM((slots, 4, seg), f32),
        ],
        compiler_params=pltpu.CompilerParams(vmem_limit_bytes=56 << 20),
    )(pair_a, pair_slot, own, recv, live, lim)


def seg_call(send, back, own, seg_node, inner, shared):
    high = inner.shape[0] // 3
    count = shared.shape[1]
    return pl.pallas_call(
        seg_body,
        out_shape=(struct(3 * high, LOW), struct(3, count), struct(3, count), struct(1, 128)),
        in_specs=smem(1) + vmem(5),
        out_specs=tuple(vmem(4)),
        scratch_shapes=[
            pltpu.VMEM((5, own.shape[0], 4, 128), f32),
            pltpu.VMEM((PIECES * 3 * high, LOW), bf16),
            pltpu.VMEM((PIECES * 3 * high, LOW), f32),
        ],
    )(send, back, own, seg_node, inner, shared)


def last_call(lim, total, shared, lower, upper, vel, disp, mass):
    high = total.shape[0] // 3
    return pl.pallas_call(
        last_body,
        out_shape=(struct(*disp.shape), struct(*disp.shape)),
        in_specs=vmem(8),
        out_specs=tuple(vmem(2)),
        scratch_shapes=[pltpu.VMEM((PIECES * 3 * high, LOW), f32)],
    )(lim, total, shared, lower, upper, vel, disp, mass)


def shifted(value, axis, steps):
    count = lax.axis_size(axis)
    first, last = (max(0, -steps), min(count, count - steps))
    return lax.ppermute(value, axis, [(source, source + steps) for source in range(first, last)])


def shards(
    ref_pos,
    displacement,
    velocity,
    node_mass,
    elem_nodes,
    elem_part,
    elem_scale,
    part_stiff,
    shared,
    seg_node,
    seg_mask,
    send_blk,
    pair_a,
    pair_slot,
    pair_mask,
):
    peers = lax.axis_size("grp") * lax.axis_size("dev")
    send = send_blk.reshape(-1)
    mass = node_mass.reshape(1, -1)
    own, outgoing = send_call(send, displacement, ref_pos, seg_node, seg_mask, peers)
    arrived = lax.all_to_all(outgoing, ("grp", "dev"), split_axis=0, concat_axis=0, tiled=True)
    first = (lax.axis_index(("grp", "dev")) * part_stiff.shape[0]).reshape(1)
    inner, limit = element_call(
        first,
        part_stiff,
        displacement,
        mass,
        elem_nodes,
        elem_part.reshape(1, -1),
        elem_scale.reshape(1, -1),
    )
    own_force, far_force = contact_call(
        pair_a,
        pair_slot,
        own,
        arrived.reshape(-1, 4, own.shape[2]),
        pair_mask.reshape(-1, 128),
        limit,
        peers,
    )
    back = lax.all_to_all(far_force, ("grp", "dev"), split_axis=0, concat_axis=0, tiled=True)
    total, low_rows, up_rows, limits = seg_call(send, back, own_force, seg_node, inner, shared)
    from_lower = shifted(up_rows, "dev", 1)
    from_upper = shifted(low_rows, "dev", -1)
    return last_call(limits, total, shared, from_lower, from_upper, velocity, displacement, mass)


def solution(mesh):
    both = ("grp", "dev")
    return jax.shard_map(
        shards,
        mesh=mesh,
        in_specs=(
            P(None, both),
            P(None, both),
            P(None, both),
            P(both),
            P(None, both),
            P(both),
            P(both),
            P(both),
            P(None, both),
            P(both, None),
            P(both, None),
            P(both, None, None),
            P(both),
            P(both),
            P(both),
        ),
        out_specs=(P(None, both), P(None, both)),
        check_vma=False,
    )
```

time: 709 us -> 154 us (0.22)
  other arithmetic: 377 us -> 0 us
  local copies, waits for them, and re-layouts: 255 us -> 3.29 us
  Pallas kernels: 0 us -> 83.6 us
  blocking collectives: 0 us -> 43.7 us
  matrix products: 16.9 us -> 0 us
  loops' own time: 11.7 us -> 0 us
  starting transfers between devices: 27.6 us -> 16.2 us
  waiting for transfers between devices: 14.5 us -> 6.18 us
    scatter-add x2 -> x0, other arithmetic: 244 us -> none  [the longest x1 220 us: shards(): totals = jnp.zeros_like(displacement).at[:, all_index].add(all_force)]
    gather x4 -> x0, local copies, waits for them, and re-layouts: 158 us -> none  [the longest x1 137 us: shards(): picked = node_rows[:, all_index]]
    reduce_sum x33 -> x0, other arithmetic: 97 us -> none  [the longest x16 63.9 us: pair_forces(): recoil = -jnp.sum(weights[:, None] * offset, 2)]
    pallas_call x0 -> x5, Pallas kernels: none -> 83.6 us  [the longest x1 34.5 us: contact_call(): pl.pallas_call(contact_body, out_shape=(struct(blocks, 3, seg), struct(pe...]
    all_to_all x0 -> x1, blocking collectives: none -> 43.7 us  [shards(): lax.all_to_all(far_force, ('grp', 'dev'), split_axis=0, concat_axis=0, ti...]
    slice x74 -> x0, local copies, waits for them, and re-layouts: 30.7 us -> none  [the longest x1 11.2 us: shards(): elem_mass = jnp.min(picked[3, :4 * elem_count].reshape(4, elem_count), 0)]
    dot_general x35 -> x0, matrix products: 16.9 us -> none  [pick_dot(): jnp.dot(selector, table, precision=EXACT, preferred_element_type=jnp.floa...]
    unnamed x45 -> x7, local copies, waits for them, and re-layouts: 18.1 us -> 2.5 us
  transfers between devices with their start and end apart: 4 -> 3, of which waited for: 2 -> 1; matrix products, arithmetic and copies ran while one was open for 5% -> 0% of each run, Pallas kernels for 0% -> 20%
where the time goes in v1:
time: 154 us
  Pallas kernels  83.6 us (54%)
  blocking collectives  43.7 us (28%)
  starting transfers between devices  16.2 us (11%)
  waiting for transfers between devices  6.18 us (4%)
  local copies, waits for them, and re-layouts  3.29 us (2%)
    all_to_all x1, blocking collectives, shards(): lax.all_to_all(far_force, ('grp', 'dev'), split_axis=0, concat_axis=0, ti...  43.7 us
    pallas_call x1, Pallas kernels, contact_call(): pl.pallas_call(contact_body, out_shape=(struct(blocks, 3, seg), struct(pe...  34.5 us
    pallas_call x1, Pallas kernels, element_call(): pl.pallas_call(element_body, out_shape=(struct(3 * high, LOW), struct(1,...  30.2 us
    pallas_call x1, Pallas kernels, seg_call(): pl.pallas_call(seg_body, out_shape=(struct(3 * high, LOW), struct(3, coun...  10.2 us
    all_to_all x1, starting transfers between devices, shards(): lax.all_to_all(outgoing, ('grp', 'dev'), split_axis=0, concat_axis=0, til...  9.85 us
    ppermute x2, starting transfers between devices, shifted(): lax.ppermute(value, axis, [(source, source + steps) for source in range(f...  6.39 us
    ppermute x2, waiting for transfers between devices, shifted(): lax.ppermute(value, axis, [(source, source + steps) for source in range(f...  6.18 us
    pallas_call x1, Pallas kernels, send_call(): pl.pallas_call(send_body, out_shape=(struct(blocks, 4, seg), struct(peers...  5.78 us
  transfers between devices with their start and end apart: 3, of which 1 were waited for; matrix products, arithmetic and copies ran while one was open for 0% of the time, Pallas kernels for 20%

profile of v1, /device:TPU:96, one launch (start us, length us, event | category | flops | bytes accessed | tf_op | source)
XLA Modules:
  0.0 153.7 jit_solution(778529368735335976)
XLA Ops:
  0.6 0.8 copy.17
  1.4 0.8 reshape.25.send_ref
  2.2 5.8 %shard_map.158 = (f32[64,4,128]{2,1,0:T(4,128)}, f32[128,5,4,128]{3,2,1,0:T(4,128)}) custom-call(s32[640]{0:T(1024)} %reshape.25.send_ref, f32[3,8192]{1,0:T(4,128)} %disp_ref.5, f32[3,8192]{1,0:T(4,128)} %ref_ref.1, s32[64,128]{1,0:T(8,128)} %seg_ref.3, s32[64,128]{1,0:T(8,128)} %mask_ref.1), custom_call_target="tpu_custom_call" | custom-call | tf_op jit(solution)/shard_map/pallas_call | solution.py:307
  8.0 9.9 %all-to-all-start = ((f32[128,5,4,128]{3,2,1,0:T(4,128)}), f32[128,5,4,128]{3,2,1,0:T(4,128)S(1)}, u32[]{:S(2)}, u32[]{:S(2)}) async-start(f32[128,5,4,128]{3,2,1,0:T(4,128)} %get-tuple-element.13), calls=%async_computation | async-start | bytes 2621440 | tf_op jit(solution)/shard_map/all_to_all | solution.py:405
  17.9 30.2 %shard_map.159 = (f32[96,256]{1,0:T(8,128)}, f32[1,128]{1,0:T(1,128)}) custom-call(s32[1]{0:T(128)} %bitcast.2.first_ref, f32[4]{0:T(128)} %stiff_ref.1, f32[3,8192]{1,0:T(4,128)} %disp_ref.5, f32[1,8192]{1,0:T(1,128)} %bitcast.7, s32[4,8192]{1,0:T(4,128)} %nodes_ref.1, s32[1,8192]{1,0:T(1,128)} %bitcast.9, f32[1,8192]{1,0:T(1,128)} %bitcast.10), custom_call_target="tpu_custom_call" | custom-call | tf_op jit(solution)/shard_map/pallas_call | solution.py:321
  48.0 0.0 all-to-all-done
  48.0 0.0 copy-start
  48.0 1.1 copy-done
  49.1 34.5 %shard_map.160 = (f32[64,3,128]{2,1,0:T(4,128)}, f32[128,16,128]{2,1,0:T(8,128)}) custom-call(s32[512]{0:T(512)} %near_ref.1, s32[512]{0:T(512)} %far_ref.1, f32[64,4,128]{2,1,0:T(4,128)} %get-tuple-element.12.own_ref, f32[640,4,128]{2,1,0:T(4,128)} %bitcast.6, s32[4,128]{1,0:T(4,128)} %bitcast.11, f32[1,128]{1,0:T(1,128)} %get-tuple-element.14.lim_ref), custom_call_target="tpu_custom_call" | custom-call | tf_op jit(solution)/shard_map/pallas_call | solution.py:337
  83.6 43.7 %all_to_all.10.back_ref = f32[128,16,128]{2,1,0:T(8,128)} all-to-all(f32[128,16,128]{2,1,0:T(8,128)} %get-tuple-element.15), channel_id=1, replica_groups=mesh['grp'=8,'dev'=16] {'grp','dev'}, dimensions={0} | all-to-all | bytes 2097152 | tf_op jit(solution)/shard_map/all_to_all | solution.py:425
  127.3 10.2 %shard_map.161 = (f32[96,256]{1,0:T(8,128)}, f32[3,2048]{1,0:T(4,128)}, f32[3,2048]{1,0:T(4,128)}, f32[1,128]{1,0:T(1,128)}) custom-call(s32[640]{0:T(1024)} %reshape.25.send_ref, f32[128,16,128]{2,1,0:T(8,128)} %all_to_all.10.back_ref, f32[64,3,128]{2,1,0:T(4,128)} %get-tuple-element.16.own_ref, s32[64,128]{1,0:T(8,128)} %seg_ref.3, ...), custom_call_target="tpu_custom_call" | custom-call | tf_op jit(solution)/shard_map/pallas_call | solution.py:354
  137.5 4.5 %collective-permute-start = (f32[3,2048]{1,0:T(4,128)}, f32[3,2048]{1,0:T(4,128)S(1)}, u32[]{:S(2)}, u32[]{:S(2)}) collective-permute-start(f32[3,2048]{1,0:T(4,128)} %get-tuple-element.20), channel_id=1, source_target_pairs={{0,1},{1,2},{2,3},{3,4},{4,5},{5,6},{6,7},{7,8},{8,9},{9,10},{10,1... | collective-permute-start | bytes 73736 | tf_op jit(solution)/shard_map/ppermute | solution.py:381
  142.0 1.9 %collective-permute-start.1 = (f32[3,2048]{1,0:T(4,128)}, f32[3,2048]{1,0:T(4,128)S(1)}, u32[]{:S(2)}, u32[]{:S(2)}) collective-permute-start(f32[3,2048]{1,0:T(4,128)} %get-tuple-element.21), channel_id=1, source_target_pairs={{1,0},{2,1},{3,2},{4,3},{5,4},{6,5},{7,6},{8,7},{9,8},{10,9},{11,1... | collective-permute-start | bytes 73736 | tf_op jit(solution)/shard_map/ppermute | solution.py:381
  143.9 0.0 collective-permute-done.low_ref
  143.9 0.0 copy-start.1
  143.9 6.2 %collective-permute-done.1.up_ref = f32[3,2048]{1,0:T(4,128)S(1)} collective-permute-done((f32[3,2048]{1,0:T(4,128)}, f32[3,2048]{1,0:T(4,128)S(1)}, u32[]{:S(2)}, u32[]{:S(2)}) %collective-permute-start.1) | collective-permute-done | bytes 24608 | tf_op jit(solution)/shard_map/ppermute | solution.py:381
  150.1 0.0 copy-start.2
  150.1 0.0 copy-done.1
  150.1 0.6 copy-done.2
  150.7 3.0 %shard_map.162 = (f32[3,8192]{1,0:T(4,128)}, f32[3,8192]{1,0:T(4,128)}) custom-call(f32[1,128]{1,0:T(1,128)} %get-tuple-element.18.lim_ref, f32[96,256]{1,0:T(8,128)} %get-tuple-element.19.tot_ref, s32[2,2048]{1,0:T(2,128)} %share_ref.3, f32[3,2048]{1,0:T(4,128)} %copy-done.1, f32[3,2048]{1,0:T(4,128)} %copy-done.2, f32[3,8192]{1,0:T(4,128)} %vel_ref.1, ...), custom_call_target="tpu_custom_call" | custom-call | tf_op jit(solution)/shard_map/pallas_call | solution.py:369
Async XLA Ops:
  8.0 40.0 %all-to-all-start = ((f32[128,5,4,128]{3,2,1,0:T(4,128)}), f32[128,5,4,128]{3,2,1,0:T(4,128)S(1)}, u32[]{:S(2)}, u32[]{:S(2)}) async-start(f32[128,5,4,128]{3,2,1,0:T(4,128)} %get-tuple-element.13), calls=%async_computation | async-start | bytes 2621440 | tf_op jit(solution)/shard_map/all_to_all | solution.py:405
  48.0 1.1 copy-start
  137.5 6.4 %collective-permute-start = (f32[3,2048]{1,0:T(4,128)}, f32[3,2048]{1,0:T(4,128)S(1)}, u32[]{:S(2)}, u32[]{:S(2)}) collective-permute-start(f32[3,2048]{1,0:T(4,128)} %get-tuple-element.20), channel_id=1, source_target_pairs={{0,1},{1,2},{2,3},{3,4},{4,5},{5,6},{6,7},{7,8},{8,9},{9,10},{10,1... | collective-permute-start | bytes 73736 | tf_op jit(solution)/shard_map/ppermute | solution.py:381
  142.0 8.1 %collective-permute-start.1 = (f32[3,2048]{1,0:T(4,128)}, f32[3,2048]{1,0:T(4,128)S(1)}, u32[]{:S(2)}, u32[]{:S(2)}) collective-permute-start(f32[3,2048]{1,0:T(4,128)} %get-tuple-element.21), channel_id=1, source_target_pairs={{1,0},{2,1},{3,2},{4,3},{5,4},{6,5},{7,6},{8,7},{9,8},{10,9},{11,1... | collective-permute-start | bytes 73736 | tf_op jit(solution)/shard_map/ppermute | solution.py:381
  143.9 6.2 %copy-start.1 = (f32[3,2048]{1,0:T(4,128)}, f32[3,2048]{1,0:T(4,128)S(1)}, u32[]{:S(2)}) copy-start(f32[3,2048]{1,0:T(4,128)S(1)} %collective-permute-done.low_ref) | copy-start | bytes 73732
  150.1 0.6 copy-start.2

commit v2 on v1

--- a/solution.py
+++ b/solution.py
@@ -12,6 +12,7 @@
 COURANT = 0.5
 LOW = 256
 PIECES = 3
+WIDTH = 256
 SCALE = math.sqrt(math.log2(math.e))
 PARK = 1.0e3
 f32 = jnp.float32
@@ -28,9 +29,12 @@
 
 
 def low_hot(idx):
-    low = idx & (LOW - 1)
-    rows = lax.broadcasted_iota(jnp.int32, (LOW, idx.shape[1]), 0)
-    return jnp.where(rows == low, 1.0, 0.0).astype(bf16)
+    low = jnp.broadcast_to((idx & (LOW - 1)).astype(f32), (16, idx.shape[1])).astype(bf16)
+    line = lax.broadcasted_iota(jnp.int32, low.shape, 0).astype(f32).astype(bf16)
+    one, zero = jnp.ones(low.shape, bf16), jnp.zeros(low.shape, bf16)
+    return jnp.concatenate(
+        [jnp.where(low == line + float(16 * k), one, zero) for k in range(LOW // 16)], 0
+    )
 
 
 def high_mask(idx, high):
@@ -59,13 +63,15 @@
     ]
 
 
-def spread(force, mask, high):
-    rows = [[], [], []]
-    for value in force:
-        wide = jnp.broadcast_to(value, mask.shape)
-        for p, piece in enumerate(pieces_of(jnp.where(mask, wide, 0.0))):
-            rows[p].append(piece)
-    return jnp.concatenate(rows[0] + rows[1] + rows[2], 0)
+def cut_rows(force):
+    return jnp.concatenate([piece.astype(f32) for piece in pieces_of(force)], 0)
+
+
+def spread(ref, idx, high):
+    mask = high_mask(idx, high)
+    return jnp.concatenate(
+        [jnp.where(mask, ref[r : r + 1, :], 0.0).astype(bf16) for r in range(3 * PIECES)], 0
+    )
 
 
 def add_hot(left, hot):
@@ -96,7 +102,7 @@
             own_ref[base + k, 3:4, :] = weight[k : k + 1]
         return carry
 
-    lax.fori_loop(0, blocks // group, some, 0)
+    lax.fori_loop(0, blocks // group, some, 0, unroll=4)
     peers, cap = out_ref.shape[0], out_ref.shape[1]
 
     def send(d, carry):
@@ -107,17 +113,16 @@
     lax.fori_loop(0, peers, send, 0, unroll=4)
 
 
-def element_body(
-    first_ref, stiff_ref, disp_ref, mass_ref, nodes_ref, part_ref, scale_ref, tot_ref, lim_ref, tab, cut, acc
+def force_body(
+    first_ref, stiff_ref, disp_ref, mass_ref, nodes_ref, part_ref, scale_ref, force_ref, lim_ref, tab, cut
 ):
     high = disp_ref.shape[1] // LOW
-    width = 256
+    width = WIDTH
     parts = stiff_ref.shape[0]
     for c in range(3):
         fill_table(tab, c * high, disp_ref, c, high)
     fill_table(tab, 3 * high, mass_ref, 0, high)
     split_table(cut, tab)
-    acc[...] = jnp.zeros_like(acc)
 
     def some(g, limit):
         at = pl.ds(pl.multiple_of(g * width, width), width)
@@ -128,9 +133,7 @@
         stiff = stiff * scale_ref[:, at]
         nodes = nodes_ref[:, at]
         idx = jnp.concatenate([nodes[k : k + 1] for k in range(4)], 1)
-        hot = low_hot(idx)
-        mask = high_mask(idx, high)
-        found = pick(cut, hot, mask, 4, high)
+        found = pick(cut, low_hot(idx), high_mask(idx, high), 4, high)
         corner = [[found[c][:, k * width : (k + 1) * width] for c in range(4)] for k in range(4)]
         mass = jnp.minimum(
             jnp.minimum(corner[0][3], corner[1][3]), jnp.minimum(corner[2][3], corner[3][3])
@@ -143,52 +146,88 @@
                 force[head][c] = force[head][c] + term
                 force[tail][c] = force[tail][c] - term
         joined = [jnp.concatenate([force[k][c] for k in range(4)], 1) for c in range(3)]
-        acc[...] += add_hot(spread(joined, mask, high), hot)
+        force_ref[g, 0:9] = cut_rows(jnp.concatenate(joined, 0))
         return jnp.minimum(limit, COURANT * jnp.sqrt(mass / stiff))
 
     limit = lax.fori_loop(
-        0, nodes_ref.shape[1] // width, some, jnp.full((1, width), jnp.inf, f32)
+        0, nodes_ref.shape[1] // width, some, jnp.full((1, width), jnp.inf, f32), unroll=4
     )
+    lim_ref[...] = jnp.broadcast_to(jnp.min(limit, 1, keepdims=True), lim_ref.shape)
+
+
+def scatter_body(nodes_ref, force_ref, seg_ref, own_ref, tot_ref, acc, cut):
+    high = tot_ref.shape[0] // 3
+    acc[...] = jnp.zeros_like(acc)
+
+    def some(g, carry):
+        at = pl.ds(pl.multiple_of(g * WIDTH, WIDTH), WIDTH)
+        nodes = nodes_ref[:, at]
+        idx = jnp.concatenate([nodes[k : k + 1] for k in range(4)], 1)
+        acc[...] += add_hot(spread(force_ref.at[g], idx, high), low_hot(idx))
+        return carry
+
+    lax.fori_loop(0, force_ref.shape[0], some, 0, unroll=4)
+    group = 8
+
+    def more(g, carry):
+        base = pl.multiple_of(g * group, group)
+        seg = seg_ref[pl.ds(base, group), :]
+        idx = jnp.concatenate([seg[k : k + 1] for k in range(group)], 1)
+        cut[0:9] = cut_rows(jnp.concatenate([own_ref[base + k] for k in range(group)], 1))
+        acc[...] += add_hot(spread(cut, idx, high), low_hot(idx))
+        return carry
+
+    lax.fori_loop(0, seg_ref.shape[0] // group, more, 0, unroll=4)
     rows = 3 * high
     tot_ref[...] = (acc[2 * rows :] + acc[rows : 2 * rows]) + acc[:rows]
-    lim_ref[...] = jnp.broadcast_to(jnp.min(limit, 1, keepdims=True), lim_ref.shape)
 
 
 def contact_body(
-    near_ref, far_ref, own_ref, recv_ref, live_ref, lim_ref, own_out, far_out, wide, total, remote
+    near_ref, far_ref, own_ref, recv_ref, live_ref, lim_ref, own_out, far_out, wide, total_a, total_b, remote, rows, chosen
 ):
     blocks = own_ref.shape[0]
     slots = recv_ref.shape[0]
     seg = own_ref.shape[2]
     cap = 5
-
-    def park(block):
-        weight = block[3:4]
-        out = [jnp.where(weight > 0.5, block[0:1] * SCALE, PARK)]
-        return out + [block[c : c + 1] * SCALE for c in range(1, 3)]
-
-    def widen(b, carry):
-        rows = park(own_ref[b])
-        for c in range(3):
-            wide[b, c] = jnp.broadcast_to(rows[c], (seg, seg)).T
-            total[b, c] = jnp.zeros((seg, seg), f32)
-        return carry
-
-    lax.fori_loop(0, blocks, widen, 0)
-
+    group = 8
+    line = lax.broadcasted_iota(jnp.int32, (seg, 3 * seg), 0)
+    part = lax.broadcasted_iota(jnp.int32, (seg, 3 * seg), 1) >> 7
+    for k in range(group):
+        at = line - 16 * k
+        hit = (at == part) | (at == part + 3) | (at == part + 6)
+        chosen[k] = jnp.where(hit, 1.0, 0.0).astype(bf16)
+    rows[...] = jnp.zeros_like(rows)
+
+    def scaled(block, parked):
+        x = jnp.where(block[3:4] > 0.5, block[0:1] * SCALE, parked)
+        return jnp.concatenate([x, block[1:3] * SCALE], 0)
+
+    def widen(g, carry):
+        for k in range(group):
+            xyz = scaled(own_ref[g * group + k], PARK)
+            for p, piece in enumerate(pieces_of(xyz)):
+                rows[16 * k + 3 * p : 16 * k + 3 * p + 3, :] = piece.astype(f32)
+        columns = rows[...].T.astype(bf16)
+        for k in range(group):
+            out = jnp.dot(columns, chosen[k], preferred_element_type=f32)
+            for c in range(3):
+                wide[g * group + k, c] = out[:, c * seg : (c + 1) * seg]
+                total_a[g * group + k, c] = jnp.zeros((seg, seg), f32)
+                total_b[g * group + k, c] = jnp.zeros((seg, seg), f32)
+        return carry
+
+    lax.fori_loop(0, blocks // group, widen, 0)
     def ready(s, carry):
         block = recv_ref[s]
-        remote[s, 0:1] = jnp.where(block[3:4] > 0.5, block[0:1] * SCALE, -PARK)
-        for c in range(1, 3):
-            remote[s, c : c + 1] = block[c : c + 1] * SCALE
-        return carry
-
-    lax.fori_loop(0, slots, ready, 0, unroll=4)
+        remote[s, 0:3] = scaled(block, -PARK)
+        return carry
+
+    lax.fori_loop(0, slots, ready, 0, unroll=8)
     far_out[...] = jnp.zeros_like(far_out)
     far_out[:, 15:16, :] = jnp.broadcast_to(lim_ref[...][None], (far_out.shape[0], 1, seg))
     live = jnp.sum(live_ref[...])
 
-    def pair(p, carry):
+    def pair(p, total):
         b = near_ref[p]
         s = far_ref[p]
         there = [jnp.broadcast_to(remote[s, c : c + 1, :], (8, seg)) for c in range(3)]
@@ -206,22 +245,31 @@
         row = (s - d * cap) * 3
         for c in range(3):
             far_out[d, pl.ds(row + c, 1), :] -= jnp.sum(recoil[c], 0, keepdims=True) * (1.0 / SCALE)
-        return carry
-
-    lax.fori_loop(0, live, pair, 0)
+
+    def both(q, carry):
+        pair(2 * q, total_a)
+        pair(2 * q + 1, total_b)
+        return carry
+
+    lax.fori_loop(0, live >> 1, both, 0)
+
+    @pl.when((live & 1) == 1)
+    def _():
+        pair(live - 1, total_a)
 
     def close(b, carry):
         for c in range(3):
-            own_out[b, c : c + 1, :] = jnp.sum(total[b, c].T, 0, keepdims=True) * (1.0 / SCALE)
+            total = total_a[b, c] + total_b[b, c]
+            own_out[b, c : c + 1, :] = jnp.sum(total.T, 0, keepdims=True) * (1.0 / SCALE)
         return carry
 
     lax.fori_loop(0, blocks, close, 0)
 
 
 def seg_body(
-    send_ref, back_ref, own_ref, seg_ref, int_ref, share_ref, tot_ref, low_ref, up_ref, lim_ref, sums, cut, acc
+    send_ref, back_ref, seg_ref, int_ref, share_ref, tot_ref, low_ref, up_ref, lim_ref, sums, cut, acc, rows
 ):
-    blocks = own_ref.shape[0]
+    blocks = seg_ref.shape[0]
     peers = back_ref.shape[0]
     cap = 5
     high = int_ref.shape[0] // 3
@@ -245,15 +293,14 @@
         for k in range(group):
             b = base + k
             part = sums[0, b, 0:3] + sums[1, b, 0:3] + sums[2, b, 0:3] + sums[3, b, 0:3] + sums[4, b, 0:3]
-            blocks_in.append(part + own_ref[b])
-        force = jnp.concatenate(blocks_in, 1)
-        left = spread([force[c : c + 1] for c in range(3)], high_mask(idx, high), high)
-        acc[...] += add_hot(left, low_hot(idx))
-        return carry
-
-    lax.fori_loop(0, blocks // group, some, 0)
-    rows = 3 * high
-    tot_ref[...] = ((acc[2 * rows :] + acc[rows : 2 * rows]) + acc[:rows]) + int_ref[...]
+            blocks_in.append(part)
+        rows[0:9] = cut_rows(jnp.concatenate(blocks_in, 1))
+        acc[...] += add_hot(spread(rows, idx, high), low_hot(idx))
+        return carry
+
+    lax.fori_loop(0, blocks // group, some, 0, unroll=4)
+    size = 3 * high
+    tot_ref[...] = ((acc[2 * size :] + acc[size : 2 * size]) + acc[:size]) + int_ref[...]
     split_table(cut, tot_ref)
     count = share_ref.shape[1]
     for row, out in ((0, low_ref), (1, up_ref)):
@@ -267,7 +314,7 @@
 
 
 def last_body(
-    lim_ref, tot_ref, share_ref, low_ref, up_ref, vel_ref, disp_ref, mass_ref, new_disp, new_vel, acc
+    lim_ref, tot_ref, share_ref, low_ref, up_ref, vel_ref, disp_ref, mass_ref, new_disp, new_vel, acc, cut
 ):
     high = tot_ref.shape[0] // 3
     count = share_ref.shape[1]
@@ -275,8 +322,8 @@
     for row, src in ((0, low_ref), (1, up_ref)):
         for at in range(0, count, 1024):
             idx = share_ref[row : row + 1, at : at + 1024]
-            force = [src[c : c + 1, at : at + 1024] for c in range(3)]
-            total = total + add_hot(spread(force, high_mask(idx, high), high), low_hot(idx))
+            cut[0:9] = cut_rows(src[:, at : at + 1024])
+            total = total + add_hot(spread(cut, idx, high), low_hot(idx))
     rows = 3 * high
     acc[0:rows] = ((total[2 * rows :] + total[rows : 2 * rows]) + total[:rows]) + tot_ref[...]
     step = jnp.min(lim_ref[...], 1, keepdims=True)
@@ -316,19 +363,32 @@
     )(send, disp, ref_pos, seg_node, seg_mask)
 
 
-def element_call(first, stiff, disp, mass, nodes, part, scale):
+def force_call(first, stiff, disp, mass, nodes, part, scale):
     high = disp.shape[1] // LOW
     return pl.pallas_call(
-        element_body,
-        out_shape=(struct(3 * high, LOW), struct(1, 128)),
+        force_body,
+        out_shape=(struct(nodes.shape[1] // WIDTH, 16, 4 * WIDTH), struct(1, 128)),
         in_specs=smem(2) + vmem(5),
         out_specs=tuple(vmem(2)),
         scratch_shapes=[
             pltpu.VMEM((4 * high, LOW), f32),
             pltpu.VMEM((PIECES * 4 * high, LOW), bf16),
-            pltpu.VMEM((PIECES * 3 * high, LOW), f32),
         ],
     )(first, stiff, disp, mass, nodes, part, scale)
+
+
+def scatter_call(nodes, force, seg_node, own):
+    high = nodes.shape[1] // LOW
+    return pl.pallas_call(
+        scatter_body,
+        out_shape=struct(3 * high, LOW),
+        in_specs=vmem(4),
+        out_specs=vmem(1)[0],
+        scratch_shapes=[
+            pltpu.VMEM((PIECES * 3 * high, LOW), f32),
+            pltpu.VMEM((16, 1024), f32),
+        ],
+    )(nodes, force, seg_node, own)
 
 
 def contact_call(pair_a, pair_slot, own, recv, live, lim, peers):
@@ -342,26 +402,30 @@
         scratch_shapes=[
             pltpu.VMEM((blocks, 3, seg, seg), f32),
             pltpu.VMEM((blocks, 3, seg, seg), f32),
+            pltpu.VMEM((blocks, 3, seg, seg), f32),
             pltpu.VMEM((slots, 4, seg), f32),
+            pltpu.VMEM((seg, seg), f32),
+            pltpu.VMEM((8, seg, 3 * seg), bf16),
         ],
         compiler_params=pltpu.CompilerParams(vmem_limit_bytes=56 << 20),
     )(pair_a, pair_slot, own, recv, live, lim)
 
 
-def seg_call(send, back, own, seg_node, inner, shared):
+def seg_call(send, back, seg_node, inner, shared):
     high = inner.shape[0] // 3
     count = shared.shape[1]
     return pl.pallas_call(
         seg_body,
         out_shape=(struct(3 * high, LOW), struct(3, count), struct(3, count), struct(1, 128)),
-        in_specs=smem(1) + vmem(5),
+        in_specs=smem(1) + vmem(4),
         out_specs=tuple(vmem(4)),
         scratch_shapes=[
-            pltpu.VMEM((5, own.shape[0], 4, 128), f32),
+            pltpu.VMEM((5, seg_node.shape[0], 4, 128), f32),
             pltpu.VMEM((PIECES * 3 * high, LOW), bf16),
             pltpu.VMEM((PIECES * 3 * high, LOW), f32),
+            pltpu.VMEM((16, 1024), f32),
         ],
-    )(send, back, own, seg_node, inner, shared)
+    )(send, back, seg_node, inner, shared)
 
 
 def last_call(lim, total, shared, lower, upper, vel, disp, mass):
@@ -371,7 +435,10 @@
         out_shape=(struct(*disp.shape), struct(*disp.shape)),
         in_specs=vmem(8),
         out_specs=tuple(vmem(2)),
-        scratch_shapes=[pltpu.VMEM((PIECES * 3 * high, LOW), f32)],
+        scratch_shapes=[
+            pltpu.VMEM((PIECES * 3 * high, LOW), f32),
+            pltpu.VMEM((16, 1024), f32),
+        ],
     )(lim, total, shared, lower, upper, vel, disp, mass)
 
 
@@ -404,7 +471,7 @@
     own, outgoing = send_call(send, displacement, ref_pos, seg_node, seg_mask, peers)
     arrived = lax.all_to_all(outgoing, ("grp", "dev"), split_axis=0, concat_axis=0, tiled=True)
     first = (lax.axis_index(("grp", "dev")) * part_stiff.shape[0]).reshape(1)
-    inner, limit = element_call(
+    force, limit = force_call(
         first,
         part_stiff,
         displacement,
@@ -423,7 +490,8 @@
         peers,
     )
     back = lax.all_to_all(far_force, ("grp", "dev"), split_axis=0, concat_axis=0, tiled=True)
-    total, low_rows, up_rows, limits = seg_call(send, back, own_force, seg_node, inner, shared)
+    inner = scatter_call(elem_nodes, force, seg_node, own_force)
+    total, low_rows, up_rows, limits = seg_call(send, back, seg_node, inner, shared)
     from_lower = shifted(up_rows, "dev", 1)
     from_upper = shifted(low_rows, "dev", -1)
     return last_call(limits, total, shared, from_lower, from_upper, velocity, displacement, mass)

time: 154 us -> 130 us (0.84)
  blocking collectives: 43.7 us -> 0 us
  starting transfers between devices: 16.2 us -> 38.6 us
  Pallas kernels: 83.6 us -> 64.5 us
  waiting for transfers between devices: 6.18 us -> 21.6 us
    all_to_all x1 -> x0, blocking collectives: 43.7 us -> none  [shards(): lax.all_to_all(far_force, ('grp', 'dev'), split_axis=0, concat_axis=0, ti...]
    all_to_all x0 -> x1, starting transfers between devices: none -> 22.3 us  [shards(): lax.all_to_all(far_force, ('grp', 'dev'), split_axis=0, concat_axis=0, ti...]
    all_to_all x1, waiting for transfers between devices: 0.01 us -> 8.9 us  [shards(): lax.all_to_all(outgoing, ('grp', 'dev'), split_axis=0, concat_axis=0, til...]
    pallas_call x1 -> x2, Pallas kernels: 30.2 us -> 21.3 us  [the longest x1 10.9 us: force_call(): pl.pallas_call(force_body, out_shape=(struct(nodes.shape[1] // WIDTH, 16,...]
    pallas_call x1, Pallas kernels: 34.5 us -> 27.7 us  [contact_call(): pl.pallas_call(contact_body, out_shape=(struct(blocks, 3, seg), struct(pe...]
    all_to_all x0 -> x1, waiting for transfers between devices: none -> 6.5 us  [shards(): lax.all_to_all(far_force, ('grp', 'dev'), split_axis=0, concat_axis=0, ti...]
    pallas_call x1, Pallas kernels: 10.2 us -> 7.99 us  [seg_call(): pl.pallas_call(seg_body, out_shape=(struct(3 * high, LOW), struct(3, coun...]
    unnamed x7 -> x9, local copies, waits for them, and re-layouts: 2.5 us -> 3.42 us
  transfers between devices with their start and end apart: 3 -> 4, of which waited for: 1 -> 3; matrix products, arithmetic and copies ran while one was open for 0% -> 0% of each run, Pallas kernels for 20% -> 16%
where the time goes in v2:
time: 130 us
  Pallas kernels  64.5 us (50%)
  starting transfers between devices  38.6 us (30%)
  waiting for transfers between devices  21.6 us (17%)
  local copies, waits for them, and re-layouts  4.22 us (3%)
    pallas_call x1, Pallas kernels, contact_call(): pl.pallas_call(contact_body, out_shape=(struct(blocks, 3, seg), struct(pe...  27.7 us
    all_to_all x1, starting transfers between devices, shards(): lax.all_to_all(far_force, ('grp', 'dev'), split_axis=0, concat_axis=0, ti...  22.3 us
    pallas_call x1, Pallas kernels, force_call(): pl.pallas_call(force_body, out_shape=(struct(nodes.shape[1] // WIDTH, 16,...  10.9 us
    pallas_call x1, Pallas kernels, scatter_call(): pl.pallas_call(scatter_body, out_shape=struct(3 * high, LOW), in_specs=vm...  10.4 us
    all_to_all x1, starting transfers between devices, shards(): lax.all_to_all(outgoing, ('grp', 'dev'), split_axis=0, concat_axis=0, til...  9.85 us
    all_to_all x1, waiting for transfers between devices, shards(): lax.all_to_all(outgoing, ('grp', 'dev'), split_axis=0, concat_axis=0, til...  8.9 us
    pallas_call x1, Pallas kernels, seg_call(): pl.pallas_call(seg_body, out_shape=(struct(3 * high, LOW), struct(3, coun...  7.99 us
    all_to_all x1, waiting for transfers between devices, shards(): lax.all_to_all(far_force, ('grp', 'dev'), split_axis=0, concat_axis=0, ti...  6.5 us
  transfers between devices with their start and end apart: 4, of which 3 were waited for; matrix products, arithmetic and copies ran while one was open for 0% of the time, Pallas kernels for 16%

profile of v2, /device:TPU:96, one launch (start us, length us, event | category | flops | bytes accessed | tf_op | source)
XLA Modules:
  0.0 129.6 jit_solution(12054030439710355921)
XLA Ops:
  0.6 0.8 copy.17
  1.4 0.8 reshape.25.send_ref
  2.2 4.7 %shard_map.158 = (f32[64,4,128]{2,1,0:T(4,128)}, f32[128,5,4,128]{3,2,1,0:T(4,128)}) custom-call(s32[640]{0:T(1024)} %reshape.25.send_ref, f32[3,8192]{1,0:T(4,128)} %disp_ref.5, f32[3,8192]{1,0:T(4,128)} %ref_ref.1, s32[64,128]{1,0:T(8,128)} %seg_ref.5, s32[64,128]{1,0:T(8,128)} %mask_ref.1), custom_call_target="tpu_custom_call" | custom-call | tf_op jit(solution)/shard_map/pallas_call | solution.py:354
  6.9 9.9 %all-to-all-start = ((f32[128,5,4,128]{3,2,1,0:T(4,128)}), f32[128,5,4,128]{3,2,1,0:T(4,128)S(1)}, u32[]{:S(2)}, u32[]{:S(2)}) async-start(f32[128,5,4,128]{3,2,1,0:T(4,128)} %get-tuple-element.13), calls=%async_computation | async-start | bytes 2621440 | tf_op jit(solution)/shard_map/all_to_all | solution.py:472
  16.8 10.9 %shard_map.159 = (f32[32,16,1024]{2,1,0:T(8,128)}, f32[1,128]{1,0:T(1,128)}) custom-call(s32[1]{0:T(128)} %bitcast.2.first_ref, f32[4]{0:T(128)} %stiff_ref.1, f32[3,8192]{1,0:T(4,128)} %disp_ref.5, f32[1,8192]{1,0:T(1,128)} %bitcast.7, s32[4,8192]{1,0:T(4,128)} %nodes_ref.3, s32[1,8192]{1,0:T(1,128)} %bitcast.9, f32[1,8192]{1,0:T(1,128)} %bitcast.10), custom_call_target="tpu_custom_call" | custom-call | tf_op jit(solution)/shard_map/pallas_call | solution.py:368
  27.7 8.9 %all-to-all-done = f32[128,5,4,128]{3,2,1,0:T(4,128)S(1)} async-done(((f32[128,5,4,128]{3,2,1,0:T(4,128)}), f32[128,5,4,128]{3,2,1,0:T(4,128)S(1)}, u32[]{:S(2)}, u32[]{:S(2)}) %all-to-all-start) | async-done | bytes 1310752 | tf_op jit(solution)/shard_map/all_to_all | solution.py:472
  36.6 0.0 copy-start
  36.6 1.1 copy-done
  37.6 27.7 %shard_map.160 = (f32[64,3,128]{2,1,0:T(4,128)}, f32[128,16,128]{2,1,0:T(8,128)}) custom-call(s32[512]{0:T(512)} %near_ref.1, s32[512]{0:T(512)} %far_ref.1, f32[64,4,128]{2,1,0:T(4,128)} %get-tuple-element.12.own_ref, f32[640,4,128]{2,1,0:T(4,128)} %bitcast.6, s32[4,128]{1,0:T(4,128)} %bitcast.11, f32[1,128]{1,0:T(1,128)} %get-tuple-element.14.lim_ref), custom_call_target="tpu_custom_call" | custom-call | tf_op jit(solution)/shard_map/pallas_call | solution.py:397
  65.3 22.3 %all-to-all-start.1 = ((f32[128,16,128]{2,1,0:T(8,128)}), f32[128,16,128]{2,1,0:T(8,128)S(1)}, u32[]{:S(2)}, u32[]{:S(2)}) async-start(f32[128,16,128]{2,1,0:T(8,128)} %get-tuple-element.15), calls=%async_computation.1 | async-start | bytes 2097152 | tf_op jit(solution)/shard_map/all_to_all | solution.py:492
  87.6 10.4 %shard_map.161.int_ref = f32[96,256]{1,0:T(8,128)} custom-call(s32[4,8192]{1,0:T(4,128)} %nodes_ref.3, f32[32,16,1024]{2,1,0:T(8,128)} %get-tuple-element.16.force_ref, s32[64,128]{1,0:T(8,128)} %seg_ref.5, f32[64,3,128]{2,1,0:T(4,128)} %get-tuple-element.17.own_ref), custom_call_target="tpu_custom_call" | custom-call | tf_op jit(solution)/shard_map/pallas_call | solution.py:382
  98.1 6.5 %all-to-all-done.1.back_ref = f32[128,16,128]{2,1,0:T(8,128)S(1)} async-done(((f32[128,16,128]{2,1,0:T(8,128)}), f32[128,16,128]{2,1,0:T(8,128)S(1)}, u32[]{:S(2)}, u32[]{:S(2)}) %all-to-all-start.1) | async-done | bytes 1048608 | tf_op jit(solution)/shard_map/all_to_all | solution.py:492
  104.6 0.0 copy-start.1
  104.6 1.0 copy-done.1
  105.5 8.0 %shard_map.162 = (f32[96,256]{1,0:T(8,128)}, f32[3,2048]{1,0:T(4,128)}, f32[3,2048]{1,0:T(4,128)}, f32[1,128]{1,0:T(1,128)}) custom-call(s32[640]{0:T(1024)} %reshape.25.send_ref, f32[128,16,128]{2,1,0:T(8,128)} %copy-done.1, s32[64,128]{1,0:T(8,128)} %seg_ref.5, f32[96,256]{1,0:T(8,128)} %shard_map.161.int_ref, s32[2,2048]{1,0:T(2,128)} %share_ref.3), custom_call_target="tpu_custom_call" | custom-call | tf_op jit(solution)/shard_map/pallas_call | solution.py:417
  113.5 4.5 %collective-permute-start = (f32[3,2048]{1,0:T(4,128)}, f32[3,2048]{1,0:T(4,128)S(1)}, u32[]{:S(2)}, u32[]{:S(2)}) collective-permute-start(f32[3,2048]{1,0:T(4,128)} %get-tuple-element.20), channel_id=1, source_target_pairs={{0,1},{1,2},{2,3},{3,4},{4,5},{5,6},{6,7},{7,8},{8,9},{9,10},{10,1... | collective-permute-start | bytes 73736 | tf_op jit(solution)/shard_map/ppermute | solution.py:448
  118.0 1.9 %collective-permute-start.1 = (f32[3,2048]{1,0:T(4,128)}, f32[3,2048]{1,0:T(4,128)S(1)}, u32[]{:S(2)}, u32[]{:S(2)}) collective-permute-start(f32[3,2048]{1,0:T(4,128)} %get-tuple-element.21), channel_id=1, source_target_pairs={{1,0},{2,1},{3,2},{4,3},{5,4},{6,5},{7,6},{8,7},{9,8},{10,9},{11,1... | collective-permute-start | bytes 73736 | tf_op jit(solution)/shard_map/ppermute | solution.py:448
  119.9 0.0 collective-permute-done.low_ref
  119.9 0.0 copy-start.2
  120.0 6.2 %collective-permute-done.1.up_ref = f32[3,2048]{1,0:T(4,128)S(1)} collective-permute-done((f32[3,2048]{1,0:T(4,128)}, f32[3,2048]{1,0:T(4,128)S(1)}, u32[]{:S(2)}, u32[]{:S(2)}) %collective-permute-start.1) | collective-permute-done | bytes 24608 | tf_op jit(solution)/shard_map/ppermute | solution.py:448
  126.1 0.0 copy-start.3
  126.1 0.0 copy-done.2
  126.1 0.6 copy-done.3
  126.7 2.8 %shard_map.163 = (f32[3,8192]{1,0:T(4,128)}, f32[3,8192]{1,0:T(4,128)}) custom-call(f32[1,128]{1,0:T(1,128)} %get-tuple-element.18.lim_ref, f32[96,256]{1,0:T(8,128)} %get-tuple-element.19.tot_ref, s32[2,2048]{1,0:T(2,128)} %share_ref.3, f32[3,2048]{1,0:T(4,128)} %copy-done.2, f32[3,2048]{1,0:T(4,128)} %copy-done.3, f32[3,8192]{1,0:T(4,128)} %vel_ref.1, ...), custom_call_target="tpu_custom_call" | custom-call | tf_op jit(solution)/shard_map/pallas_call | solution.py:433
Async XLA Ops:
  6.9 29.7 %all-to-all-start = ((f32[128,5,4,128]{3,2,1,0:T(4,128)}), f32[128,5,4,128]{3,2,1,0:T(4,128)S(1)}, u32[]{:S(2)}, u32[]{:S(2)}) async-start(f32[128,5,4,128]{3,2,1,0:T(4,128)} %get-tuple-element.13), calls=%async_computation | async-start | bytes 2621440 | tf_op jit(solution)/shard_map/all_to_all | solution.py:472
  36.6 1.1 copy-start
  65.3 39.2 %all-to-all-start.1 = ((f32[128,16,128]{2,1,0:T(8,128)}), f32[128,16,128]{2,1,0:T(8,128)S(1)}, u32[]{:S(2)}, u32[]{:S(2)}) async-start(f32[128,16,128]{2,1,0:T(8,128)} %get-tuple-element.15), calls=%async_computation.1 | async-start | bytes 2097152 | tf_op jit(solution)/shard_map/all_to_all | solution.py:492
  104.6 1.0 copy-start.1
  113.5 6.4 %collective-permute-start = (f32[3,2048]{1,0:T(4,128)}, f32[3,2048]{1,0:T(4,128)S(1)}, u32[]{:S(2)}, u32[]{:S(2)}) collective-permute-start(f32[3,2048]{1,0:T(4,128)} %get-tuple-element.20), channel_id=1, source_target_pairs={{0,1},{1,2},{2,3},{3,4},{4,5},{5,6},{6,7},{7,8},{8,9},{9,10},{10,1... | collective-permute-start | bytes 73736 | tf_op jit(solution)/shard_map/ppermute | solution.py:448
  118.0 8.1 %collective-permute-start.1 = (f32[3,2048]{1,0:T(4,128)}, f32[3,2048]{1,0:T(4,128)S(1)}, u32[]{:S(2)}, u32[]{:S(2)}) collective-permute-start(f32[3,2048]{1,0:T(4,128)} %get-tuple-element.21), channel_id=1, source_target_pairs={{1,0},{2,1},{3,2},{4,3},{5,4},{6,5},{7,6},{8,7},{9,8},{10,9},{11,1... | collective-permute-start | bytes 73736 | tf_op jit(solution)/shard_map/ppermute | solution.py:448
  119.9 6.2 %copy-start.2 = (f32[3,2048]{1,0:T(4,128)}, f32[3,2048]{1,0:T(4,128)S(1)}, u32[]{:S(2)}) copy-start(f32[3,2048]{1,0:T(4,128)S(1)} %collective-permute-done.low_ref) | copy-start | bytes 73732
  126.1 0.6 copy-start.3

commit v3 on v2

--- a/solution.py
+++ b/solution.py
@@ -183,7 +183,7 @@
 
 
 def contact_body(
-    near_ref, far_ref, own_ref, recv_ref, live_ref, lim_ref, own_out, far_out, wide, total_a, total_b, remote, rows, chosen
+    near_ref, far_ref, own_ref, recv_ref, live_ref, lim_ref, own_out, far_out, wide, total_a, total_b, remote, rows, chosen, recoils
 ):
     blocks = own_ref.shape[0]
     slots = recv_ref.shape[0]
@@ -216,15 +216,14 @@
                 total_b[g * group + k, c] = jnp.zeros((seg, seg), f32)
         return carry
 
-    lax.fori_loop(0, blocks // group, widen, 0)
+    lax.fori_loop(0, blocks // group, widen, 0, unroll=4)
     def ready(s, carry):
         block = recv_ref[s]
         remote[s, 0:3] = scaled(block, -PARK)
         return carry
 
     lax.fori_loop(0, slots, ready, 0, unroll=8)
-    far_out[...] = jnp.zeros_like(far_out)
-    far_out[:, 15:16, :] = jnp.broadcast_to(lim_ref[...][None], (far_out.shape[0], 1, seg))
+    recoils[...] = jnp.zeros_like(recoils)
     live = jnp.sum(live_ref[...])
 
     def pair(p, total):
@@ -241,10 +240,8 @@
                 push = weight * gap[c]
                 total[b, c, at, :] += push
                 recoil[c] = push if recoil[c] is None else recoil[c] + push
-        d = (s * 52429) >> 18
-        row = (s - d * cap) * 3
         for c in range(3):
-            far_out[d, pl.ds(row + c, 1), :] -= jnp.sum(recoil[c], 0, keepdims=True) * (1.0 / SCALE)
+            recoils[c, pl.ds(pl.multiple_of(s * 8, 8), 8), :] += recoil[c]
 
     def both(q, carry):
         pair(2 * q, total_a)
@@ -263,7 +260,22 @@
             own_out[b, c : c + 1, :] = jnp.sum(total.T, 0, keepdims=True) * (1.0 / SCALE)
         return carry
 
-    lax.fori_loop(0, blocks, close, 0)
+    lax.fori_loop(0, blocks, close, 0, unroll=8)
+    peers = slots // cap
+    stamp = jnp.broadcast_to(lim_ref[...], (8, seg))
+
+    def finish(g, carry):
+        for k in range(cap):
+            for c in range(3):
+                at = g * (64 * cap) + k * 8
+                rows = [recoils[c, pl.ds(at + r, 8, stride=8 * cap), :] for r in range(8)]
+                while len(rows) > 1:
+                    rows = [x + y for x, y in zip(rows[::2], rows[1::2])]
+                far_out[pl.ds(g * 128 + 3 * k + c, 8, stride=16), :] = rows[0] * (-1.0 / SCALE)
+        far_out[pl.ds(g * 128 + 15, 8, stride=16), :] = stamp
+        return carry
+
+    lax.fori_loop(0, peers // 8, finish, 0, unroll=4)
 
 
 def seg_body(
@@ -396,7 +408,7 @@
     slots = recv.shape[0]
     return pl.pallas_call(
         contact_body,
-        out_shape=(struct(blocks, 3, seg), struct(peers, 16, seg)),
+        out_shape=(struct(blocks, 3, seg), struct(peers * 16, seg)),
         in_specs=smem(2) + vmem(4),
         out_specs=tuple(vmem(2)),
         scratch_shapes=[
@@ -406,6 +418,7 @@
             pltpu.VMEM((slots, 4, seg), f32),
             pltpu.VMEM((seg, seg), f32),
             pltpu.VMEM((8, seg, 3 * seg), bf16),
+            pltpu.VMEM((3, slots * 8, seg), f32),
         ],
         compiler_params=pltpu.CompilerParams(vmem_limit_bytes=56 << 20),
     )(pair_a, pair_slot, own, recv, live, lim)
@@ -489,7 +502,9 @@
         limit,
         peers,
     )
-    back = lax.all_to_all(far_force, ("grp", "dev"), split_axis=0, concat_axis=0, tiled=True)
+    back = lax.all_to_all(
+        far_force.reshape(peers, 16, -1), ("grp", "dev"), split_axis=0, concat_axis=0, tiled=True
+    )
     inner = scatter_call(elem_nodes, force, seg_node, own_force)
     total, low_rows, up_rows, limits = seg_call(send, back, seg_node, inner, shared)
     from_lower = shifted(up_rows, "dev", 1)

time: 130 us -> 124 us (0.954)
  starting transfers between devices: 38.6 us -> 30 us
  Pallas kernels: 64.5 us -> 66.8 us
    all_to_all x1, starting transfers between devices: 22.3 us -> 13.8 us  [shards(): lax.all_to_all(far_force.reshape(peers, 16, -1), ('grp', 'dev'), split_ax...]
    pallas_call x1, Pallas kernels: 27.7 us -> 29.9 us  [contact_call(): pl.pallas_call(contact_body, out_shape=(struct(blocks, 3, seg), struct(pe...]
  transfers between devices with their start and end apart: 4 -> 4, of which waited for: 3 -> 3; matrix products, arithmetic and copies ran while one was open for 0% -> 0% of each run, Pallas kernels for 16% -> 17%
where the time goes in v3:
time: 124 us; the launch traced here: 123 us
  Pallas kernels  66.8 us (54%)
  starting transfers between devices  30 us (24%)
  waiting for transfers between devices  21.6 us (17%)
  local copies, waits for them, and re-layouts  4.22 us (3%)
    pallas_call x1, Pallas kernels, contact_call(): pl.pallas_call(contact_body, out_shape=(struct(blocks, 3, seg), struct(pe...  29.9 us
    all_to_all x1, starting transfers between devices, shards(): lax.all_to_all(far_force.reshape(peers, 16, -1), ('grp', 'dev'), split_ax...  13.8 us
    pallas_call x1, Pallas kernels, force_call(): pl.pallas_call(force_body, out_shape=(struct(nodes.shape[1] // WIDTH, 16,...  10.9 us
    pallas_call x1, Pallas kernels, scatter_call(): pl.pallas_call(scatter_body, out_shape=struct(3 * high, LOW), in_specs=vm...  10.4 us
    all_to_all x1, starting transfers between devices, shards(): lax.all_to_all(outgoing, ('grp', 'dev'), split_axis=0, concat_axis=0, til...  9.85 us
    all_to_all x1, waiting for transfers between devices, shards(): lax.all_to_all(outgoing, ('grp', 'dev'), split_axis=0, concat_axis=0, til...  8.9 us
    pallas_call x1, Pallas kernels, seg_call(): pl.pallas_call(seg_body, out_shape=(struct(3 * high, LOW), struct(3, coun...  7.99 us
    all_to_all x1, waiting for transfers between devices, shards(): lax.all_to_all(far_force.reshape(peers, 16, -1), ('grp', 'dev'), split_ax...  6.5 us
  transfers between devices with their start and end apart: 4, of which 3 were waited for; matrix products, arithmetic and copies ran while one was open for 0% of the time, Pallas kernels for 17%

profile of v3, /device:TPU:96, one launch (start us, length us, event | category | flops | bytes accessed | tf_op | source)
XLA Modules:
  0.0 123.3 jit_solution(15279936895732747546)
XLA Ops:
  0.6 0.8 copy.17
  1.4 0.8 reshape.28.send_ref
  2.2 4.7 %shard_map.158 = (f32[64,4,128]{2,1,0:T(4,128)}, f32[128,5,4,128]{3,2,1,0:T(4,128)}) custom-call(s32[640]{0:T(1024)} %reshape.28.send_ref, f32[3,8192]{1,0:T(4,128)} %disp_ref.5, f32[3,8192]{1,0:T(4,128)} %ref_ref.1, s32[64,128]{1,0:T(8,128)} %seg_ref.5, s32[64,128]{1,0:T(8,128)} %mask_ref.1), custom_call_target="tpu_custom_call" | custom-call | tf_op jit(solution)/shard_map/pallas_call | solution.py:366
  6.9 9.9 %all-to-all-start = ((f32[128,5,4,128]{3,2,1,0:T(4,128)}), f32[128,5,4,128]{3,2,1,0:T(4,128)S(1)}, u32[]{:S(2)}, u32[]{:S(2)}) async-start(f32[128,5,4,128]{3,2,1,0:T(4,128)} %get-tuple-element.13), calls=%async_computation | async-start | bytes 2621440 | tf_op jit(solution)/shard_map/all_to_all | solution.py:485
  16.8 10.9 %shard_map.159 = (f32[32,16,1024]{2,1,0:T(8,128)}, f32[1,128]{1,0:T(1,128)}) custom-call(s32[1]{0:T(128)} %bitcast.2.first_ref, f32[4]{0:T(128)} %stiff_ref.1, f32[3,8192]{1,0:T(4,128)} %disp_ref.5, f32[1,8192]{1,0:T(1,128)} %bitcast.9, s32[4,8192]{1,0:T(4,128)} %nodes_ref.3, s32[1,8192]{1,0:T(1,128)} %bitcast.11, f32[1,8192]{1,0:T(1,128)} %bitcast.12), custom_call_target="tpu_custom_call" | custom-call | tf_op jit(solution)/shard_map/pallas_call | solution.py:380
  27.7 8.9 %all-to-all-done = f32[128,5,4,128]{3,2,1,0:T(4,128)S(1)} async-done(((f32[128,5,4,128]{3,2,1,0:T(4,128)}), f32[128,5,4,128]{3,2,1,0:T(4,128)S(1)}, u32[]{:S(2)}, u32[]{:S(2)}) %all-to-all-start) | async-done | bytes 1310752 | tf_op jit(solution)/shard_map/all_to_all | solution.py:485
  36.6 0.0 copy-start
  36.6 1.1 copy-done
  37.6 29.9 %shard_map.160 = (f32[64,3,128]{2,1,0:T(4,128)}, f32[2048,128]{1,0:T(8,128)}) custom-call(s32[512]{0:T(512)} %near_ref.1, s32[512]{0:T(512)} %far_ref.1, f32[64,4,128]{2,1,0:T(4,128)} %get-tuple-element.12.own_ref, f32[640,4,128]{2,1,0:T(4,128)} %bitcast.7, s32[4,128]{1,0:T(4,128)} %bitcast.13, f32[1,128]{1,0:T(1,128)} %get-tuple-element.14.lim_ref), custom_call_target="tpu_custom_call" | custom-call | tf_op jit(solution)/shard_map/pallas_call | solution.py:409
  67.5 13.8 %all-to-all-start.1 = ((f32[128,16,128]{2,1,0:T(8,128)}), f32[128,16,128]{2,1,0:T(8,128)S(1)}, u32[]{:S(2)}, u32[]{:S(2)}) async-start(f32[128,16,128]{2,1,0:T(8,128)} %bitcast.8), calls=%async_computation.1 | async-start | bytes 2097152 | tf_op jit(solution)/shard_map/all_to_all | solution.py:505
  81.3 10.4 %shard_map.161.int_ref = f32[96,256]{1,0:T(8,128)} custom-call(s32[4,8192]{1,0:T(4,128)} %nodes_ref.3, f32[32,16,1024]{2,1,0:T(8,128)} %get-tuple-element.16.force_ref, s32[64,128]{1,0:T(8,128)} %seg_ref.5, f32[64,3,128]{2,1,0:T(4,128)} %get-tuple-element.17.own_ref), custom_call_target="tpu_custom_call" | custom-call | tf_op jit(solution)/shard_map/pallas_call | solution.py:394
  91.8 6.5 %all-to-all-done.1.back_ref = f32[128,16,128]{2,1,0:T(8,128)S(1)} async-done(((f32[128,16,128]{2,1,0:T(8,128)}), f32[128,16,128]{2,1,0:T(8,128)S(1)}, u32[]{:S(2)}, u32[]{:S(2)}) %all-to-all-start.1) | async-done | bytes 1048608 | tf_op jit(solution)/shard_map/all_to_all | solution.py:505
  98.3 0.0 copy-start.1
  98.3 1.0 copy-done.1
  99.2 8.0 %shard_map.162 = (f32[96,256]{1,0:T(8,128)}, f32[3,2048]{1,0:T(4,128)}, f32[3,2048]{1,0:T(4,128)}, f32[1,128]{1,0:T(1,128)}) custom-call(s32[640]{0:T(1024)} %reshape.28.send_ref, f32[128,16,128]{2,1,0:T(8,128)} %copy-done.1, s32[64,128]{1,0:T(8,128)} %seg_ref.5, f32[96,256]{1,0:T(8,128)} %shard_map.161.int_ref, s32[2,2048]{1,0:T(2,128)} %share_ref.3), custom_call_target="tpu_custom_call" | custom-call | tf_op jit(solution)/shard_map/pallas_call | solution.py:430
  107.2 4.5 %collective-permute-start = (f32[3,2048]{1,0:T(4,128)}, f32[3,2048]{1,0:T(4,128)S(1)}, u32[]{:S(2)}, u32[]{:S(2)}) collective-permute-start(f32[3,2048]{1,0:T(4,128)} %get-tuple-element.20), channel_id=1, source_target_pairs={{0,1},{1,2},{2,3},{3,4},{4,5},{5,6},{6,7},{7,8},{8,9},{9,10},{10,1... | collective-permute-start | bytes 73736 | tf_op jit(solution)/shard_map/ppermute | solution.py:461
  111.7 1.9 %collective-permute-start.1 = (f32[3,2048]{1,0:T(4,128)}, f32[3,2048]{1,0:T(4,128)S(1)}, u32[]{:S(2)}, u32[]{:S(2)}) collective-permute-start(f32[3,2048]{1,0:T(4,128)} %get-tuple-element.21), channel_id=1, source_target_pairs={{1,0},{2,1},{3,2},{4,3},{5,4},{6,5},{7,6},{8,7},{9,8},{10,9},{11,1... | collective-permute-start | bytes 73736 | tf_op jit(solution)/shard_map/ppermute | solution.py:461
  113.6 0.0 collective-permute-done.low_ref
  113.6 0.0 copy-start.2
  113.7 6.2 %collective-permute-done.1.up_ref = f32[3,2048]{1,0:T(4,128)S(1)} collective-permute-done((f32[3,2048]{1,0:T(4,128)}, f32[3,2048]{1,0:T(4,128)S(1)}, u32[]{:S(2)}, u32[]{:S(2)}) %collective-permute-start.1) | collective-permute-done | bytes 24608 | tf_op jit(solution)/shard_map/ppermute | solution.py:461
  119.8 0.0 copy-start.3
  119.8 0.0 copy-done.2
  119.8 0.6 copy-done.3
  120.4 2.8 %shard_map.163 = (f32[3,8192]{1,0:T(4,128)}, f32[3,8192]{1,0:T(4,128)}) custom-call(f32[1,128]{1,0:T(1,128)} %get-tuple-element.18.lim_ref, f32[96,256]{1,0:T(8,128)} %get-tuple-element.19.tot_ref, s32[2,2048]{1,0:T(2,128)} %share_ref.3, f32[3,2048]{1,0:T(4,128)} %copy-done.2, f32[3,2048]{1,0:T(4,128)} %copy-done.3, f32[3,8192]{1,0:T(4,128)} %vel_ref.1, ...), custom_call_target="tpu_custom_call" | custom-call | tf_op jit(solution)/shard_map/pallas_call | solution.py:446
Async XLA Ops:
  6.9 29.7 %all-to-all-start = ((f32[128,5,4,128]{3,2,1,0:T(4,128)}), f32[128,5,4,128]{3,2,1,0:T(4,128)S(1)}, u32[]{:S(2)}, u32[]{:S(2)}) async-start(f32[128,5,4,128]{3,2,1,0:T(4,128)} %get-tuple-element.13), calls=%async_computation | async-start | bytes 2621440 | tf_op jit(solution)/shard_map/all_to_all | solution.py:485
  36.6 1.1 copy-start
  67.5 30.7 %all-to-all-start.1 = ((f32[128,16,128]{2,1,0:T(8,128)}), f32[128,16,128]{2,1,0:T(8,128)S(1)}, u32[]{:S(2)}, u32[]{:S(2)}) async-start(f32[128,16,128]{2,1,0:T(8,128)} %bitcast.8), calls=%async_computation.1 | async-start | bytes 2097152 | tf_op jit(solution)/shard_map/all_to_all | solution.py:505
  98.3 1.0 copy-start.1
  107.2 6.4 %collective-permute-start = (f32[3,2048]{1,0:T(4,128)}, f32[3,2048]{1,0:T(4,128)S(1)}, u32[]{:S(2)}, u32[]{:S(2)}) collective-permute-start(f32[3,2048]{1,0:T(4,128)} %get-tuple-element.20), channel_id=1, source_target_pairs={{0,1},{1,2},{2,3},{3,4},{4,5},{5,6},{6,7},{7,8},{8,9},{9,10},{10,1... | collective-permute-start | bytes 73736 | tf_op jit(solution)/shard_map/ppermute | solution.py:461
  111.7 8.1 %collective-permute-start.1 = (f32[3,2048]{1,0:T(4,128)}, f32[3,2048]{1,0:T(4,128)S(1)}, u32[]{:S(2)}, u32[]{:S(2)}) collective-permute-start(f32[3,2048]{1,0:T(4,128)} %get-tuple-element.21), channel_id=1, source_target_pairs={{1,0},{2,1},{3,2},{4,3},{5,4},{6,5},{7,6},{8,7},{9,8},{10,9},{11,1... | collective-permute-start | bytes 73736 | tf_op jit(solution)/shard_map/ppermute | solution.py:461
  113.6 6.2 %copy-start.2 = (f32[3,2048]{1,0:T(4,128)}, f32[3,2048]{1,0:T(4,128)S(1)}, u32[]{:S(2)}) copy-start(f32[3,2048]{1,0:T(4,128)S(1)} %collective-permute-done.low_ref) | copy-start | bytes 73732
  119.8 0.6 copy-start.3

commit v4 on v3

--- a/solution.py
+++ b/solution.py
@@ -107,7 +107,7 @@
 
     def send(d, carry):
         for c in range(cap):
-            out_ref[d, c] = own_ref[send_ref[d * cap + c]]
+            out_ref[d, c] = own_ref[send_ref[c * peers + d]]
         return carry
 
     lax.fori_loop(0, peers, send, 0, unroll=4)
@@ -243,16 +243,20 @@
         for c in range(3):
             recoils[c, pl.ds(pl.multiple_of(s * 8, 8), 8), :] += recoil[c]
 
-    def both(q, carry):
-        pair(2 * q, total_a)
-        pair(2 * q + 1, total_b)
-        return carry
-
-    lax.fori_loop(0, live >> 1, both, 0)
-
-    @pl.when((live & 1) == 1)
-    def _():
-        pair(live - 1, total_a)
+    def four(q, carry):
+        pair(4 * q, total_a)
+        pair(4 * q + 1, total_b)
+        pair(4 * q + 2, total_a)
+        pair(4 * q + 3, total_b)
+        return carry
+
+    def one(p, carry):
+        pair(p, total_a)
+        return carry
+
+    whole = live >> 2
+    lax.fori_loop(0, whole, four, 0)
+    lax.fori_loop(4 * whole, live, one, 0)
 
     def close(b, carry):
         for c in range(3):
@@ -282,18 +286,17 @@
     send_ref, back_ref, seg_ref, int_ref, share_ref, tot_ref, low_ref, up_ref, lim_ref, sums, cut, acc, rows
 ):
     blocks = seg_ref.shape[0]
-    peers = back_ref.shape[0]
+    peers = back_ref.shape[0] // 16
     cap = 5
     high = int_ref.shape[0] // 3
+    line = lax.broadcasted_iota(jnp.int32, (blocks, peers), 0)
     sums[...] = jnp.zeros_like(sums)
-
-    def take(d, carry):
-        for c in range(cap):
-            b = send_ref[d * cap + c]
-            sums[c, b, 0:3, :] += back_ref[d, 3 * c : 3 * c + 3, :]
-        return carry
-
-    lax.fori_loop(0, peers, take, 0)
+    for c in range(cap):
+        hot = jnp.where(line == send_ref[c : c + 1, :], 1.0, 0.0).astype(bf16)
+        for k in range(3):
+            force = back_ref[pl.ds(3 * c + k, peers, stride=16), :]
+            found = jnp.dot(hot, jnp.concatenate(pieces_of(force), 1), preferred_element_type=f32)
+            sums[k] += (found[:, 256:] + found[:, 128:256]) + found[:, :128]
     acc[...] = jnp.zeros_like(acc)
     group = 8
 
@@ -301,12 +304,9 @@
         base = pl.multiple_of(g * group, group)
         seg = seg_ref[pl.ds(base, group), :]
         idx = jnp.concatenate([seg[k : k + 1] for k in range(group)], 1)
-        blocks_in = []
-        for k in range(group):
-            b = base + k
-            part = sums[0, b, 0:3] + sums[1, b, 0:3] + sums[2, b, 0:3] + sums[3, b, 0:3] + sums[4, b, 0:3]
-            blocks_in.append(part)
-        rows[0:9] = cut_rows(jnp.concatenate(blocks_in, 1))
+        force = [sums[c, pl.ds(base, group), :] for c in range(3)]
+        force = [jnp.concatenate([f[k : k + 1] for k in range(group)], 1) for f in force]
+        rows[0:9] = cut_rows(jnp.concatenate(force, 0))
         acc[...] += add_hot(spread(rows, idx, high), low_hot(idx))
         return carry
 
@@ -321,7 +321,7 @@
             picked = pick(cut, low_hot(idx), high_mask(idx, high), 3, high)
             for c in range(3):
                 out[c : c + 1, at : at + 1024] = picked[c]
-    lim = jnp.min(back_ref[:, 15, :], 0, keepdims=True)
+    lim = jnp.min(back_ref[pl.ds(15, peers, stride=16), :], 0, keepdims=True)
     lim_ref[...] = lim
 
 
@@ -372,6 +372,7 @@
             pltpu.VMEM((3 * high, LOW), f32),
             pltpu.VMEM((PIECES * 3 * high, LOW), bf16),
         ],
+        compiler_params=pltpu.CompilerParams(vmem_limit_bytes=24 << 20),
     )(send, disp, ref_pos, seg_node, seg_mask)
 
 
@@ -386,6 +387,7 @@
             pltpu.VMEM((4 * high, LOW), f32),
             pltpu.VMEM((PIECES * 4 * high, LOW), bf16),
         ],
+        compiler_params=pltpu.CompilerParams(vmem_limit_bytes=24 << 20),
     )(first, stiff, disp, mass, nodes, part, scale)
 
 
@@ -400,6 +402,7 @@
             pltpu.VMEM((PIECES * 3 * high, LOW), f32),
             pltpu.VMEM((16, 1024), f32),
         ],
+        compiler_params=pltpu.CompilerParams(vmem_limit_bytes=24 << 20),
     )(nodes, force, seg_node, own)
 
 
@@ -420,7 +423,7 @@
             pltpu.VMEM((8, seg, 3 * seg), bf16),
             pltpu.VMEM((3, slots * 8, seg), f32),
         ],
-        compiler_params=pltpu.CompilerParams(vmem_limit_bytes=56 << 20),
+        compiler_params=pltpu.CompilerParams(vmem_limit_bytes=52 << 20),
     )(pair_a, pair_slot, own, recv, live, lim)
 
 
@@ -430,15 +433,16 @@
     return pl.pallas_call(
         seg_body,
         out_shape=(struct(3 * high, LOW), struct(3, count), struct(3, count), struct(1, 128)),
-        in_specs=smem(1) + vmem(4),
+        in_specs=vmem(5),
         out_specs=tuple(vmem(4)),
         scratch_shapes=[
-            pltpu.VMEM((5, seg_node.shape[0], 4, 128), f32),
+            pltpu.VMEM((3, seg_node.shape[0], 128), f32),
             pltpu.VMEM((PIECES * 3 * high, LOW), bf16),
             pltpu.VMEM((PIECES * 3 * high, LOW), f32),
             pltpu.VMEM((16, 1024), f32),
         ],
-    )(send, back, seg_node, inner, shared)
+        compiler_params=pltpu.CompilerParams(vmem_limit_bytes=24 << 20),
+    )(send, back.reshape(-1, 128), seg_node, inner, shared)
 
 
 def last_call(lim, total, shared, lower, upper, vel, disp, mass):
@@ -452,6 +456,7 @@
             pltpu.VMEM((PIECES * 3 * high, LOW), f32),
             pltpu.VMEM((16, 1024), f32),
         ],
+        compiler_params=pltpu.CompilerParams(vmem_limit_bytes=24 << 20),
     )(lim, total, shared, lower, upper, vel, disp, mass)
 
 
@@ -479,9 +484,9 @@
     pair_mask,
 ):
     peers = lax.axis_size("grp") * lax.axis_size("dev")
-    send = send_blk.reshape(-1)
     mass = node_mass.reshape(1, -1)
-    own, outgoing = send_call(send, displacement, ref_pos, seg_node, seg_mask, peers)
+    send = send_blk[0].T
+    own, outgoing = send_call(send.reshape(-1), displacement, ref_pos, seg_node, seg_mask, peers)
     arrived = lax.all_to_all(outgoing, ("grp", "dev"), split_axis=0, concat_axis=0, tiled=True)
     first = (lax.axis_index(("grp", "dev")) * part_stiff.shape[0]).reshape(1)
     force, limit = force_call(

time: 124 us -> 119 us (0.960)
  Pallas kernels: 66.8 us -> 51.6 us
  local copies, waits for them, and re-layouts: 4.22 us -> 8.95 us
  waiting for transfers between devices: 21.6 us -> 24.1 us
  starting transfers between devices: 30 us -> 32.3 us
    unnamed x9 -> x45, local copies, waits for them, and re-layouts: 3.42 us -> 8.95 us
    pallas_call x1, Pallas kernels: 29.9 us -> 25.1 us  [contact_call(): pl.pallas_call(contact_body, out_shape=(struct(blocks, 3, seg), struct(pe...]
    pallas_call x1, Pallas kernels: 7.99 us -> 3.19 us  [seg_call(): pl.pallas_call(seg_body, out_shape=(struct(3 * high, LOW), struct(3, coun...]
    pallas_call x1, Pallas kernels: 10.4 us -> 8.18 us  [scatter_call(): pl.pallas_call(scatter_body, out_shape=struct(3 * high, LOW), in_specs=vm...]
    all_to_all x1, starting transfers between devices: 13.8 us -> 15.7 us  [shards(): lax.all_to_all(far_force.reshape(peers, 16, -1), ('grp', 'dev'), split_ax...]
    pallas_call x1, Pallas kernels: 10.9 us -> 9.21 us  [force_call(): pl.pallas_call(force_body, out_shape=(struct(nodes.shape[1] // WIDTH, 16,...]
    all_to_all x1, waiting for transfers between devices: 8.9 us -> 10.3 us  [shards(): lax.all_to_all(outgoing, ('grp', 'dev'), split_axis=0, concat_axis=0, til...]
    all_to_all x1, waiting for transfers between devices: 6.5 us -> 7.82 us  [shards(): lax.all_to_all(far_force.reshape(peers, 16, -1), ('grp', 'dev'), split_ax...]
  transfers between devices with their start and end apart: 4 -> 4, of which waited for: 3 -> 3; matrix products, arithmetic and copies ran while one was open for 0% -> 0% of each run, Pallas kernels for 17% -> 15%
where the time goes in v4:
time: 119 us; the launch traced here: 118 us
  Pallas kernels  51.6 us (43%)
  starting transfers between devices  32.3 us (27%)
  waiting for transfers between devices  24.1 us (20%)
  local copies, waits for them, and re-layouts  8.95 us (8%)
    pallas_call x1, Pallas kernels, contact_call(): pl.pallas_call(contact_body, out_shape=(struct(blocks, 3, seg), struct(pe...  25.1 us
    all_to_all x1, starting transfers between devices, shards(): lax.all_to_all(far_force.reshape(peers, 16, -1), ('grp', 'dev'), split_ax...  15.7 us
    all_to_all x1, starting transfers between devices, shards(): lax.all_to_all(outgoing, ('grp', 'dev'), split_axis=0, concat_axis=0, til...  10.3 us
    all_to_all x1, waiting for transfers between devices, shards(): lax.all_to_all(outgoing, ('grp', 'dev'), split_axis=0, concat_axis=0, til...  10.3 us
    pallas_call x1, Pallas kernels, force_call(): pl.pallas_call(force_body, out_shape=(struct(nodes.shape[1] // WIDTH, 16,...  9.21 us
    unnamed x45, local copies, waits for them, and re-layouts  8.95 us
    pallas_call x1, Pallas kernels, scatter_call(): pl.pallas_call(scatter_body, out_shape=struct(3 * high, LOW), in_specs=vm...  8.18 us
    all_to_all x1, waiting for transfers between devices, shards(): lax.all_to_all(far_force.reshape(peers, 16, -1), ('grp', 'dev'), split_ax...  7.82 us
  transfers between devices with their start and end apart: 4, of which 3 were waited for; matrix products, arithmetic and copies ran while one was open for 0% of the time, Pallas kernels for 15%

profile of v4, /device:TPU:96, one launch (start us, length us, event | category | flops | bytes accessed | tf_op | source)
XLA Modules:
  0.0 117.8 jit_solution(17913029008480630738)
XLA Ops:
  0.6 0.7 copy.20
  1.3 0.9 copy-done
  2.2 0.8 copy-done.4
  3.0 0.9 copy-done.9
  3.9 0.8 copy-done.15
  4.6 4.2 %shard_map.158 = (f32[64,4,128]{2,1,0:T(4,128)S(1)}, f32[128,5,4,128]{3,2,1,0:T(4,128)}) custom-call(s32[640]{0:T(1024)S(1)} %bitcast.21, f32[3,8192]{1,0:T(4,128)S(1)} %copy-done, f32[3,8192]{1,0:T(4,128)S(1)} %copy-done.9, s32[64,128]{1,0:T(8,128)S(1)} %copy-done.4, s32[64,128]{1,0:T(8,128)S(1)} %copy-done.15), custom_call_target="tpu_custom_call" | custom-call | tf_op jit(solution)/shard_map/pallas_call | solution.py:366
  8.9 0.0 copy-start.16
  8.9 0.0 copy-start.17
  8.9 0.0 copy-start.21
  8.9 0.0 copy-start.18
  8.9 0.0 copy-start.19
  8.9 0.0 copy-start.20
  8.9 10.3 %all-to-all-start = ((f32[128,5,4,128]{3,2,1,0:T(4,128)}), f32[128,5,4,128]{3,2,1,0:T(4,128)}, u32[]{:S(2)}, u32[]{:S(2)}) async-start(f32[128,5,4,128]{3,2,1,0:T(4,128)} %get-tuple-element.13), calls=%async_computation | async-start | bytes 2621440 | tf_op jit(solution)/shard_map/all_to_all | solution.py:490
  19.3 9.2 %shard_map.159 = (f32[32,16,1024]{2,1,0:T(8,128)S(1)}, f32[1,128]{1,0:T(1,128)S(1)}) custom-call(s32[1]{0:T(128)} %bitcast.4.first_ref, f32[4]{0:T(128)S(1)} %copy-done.21, f32[3,8192]{1,0:T(4,128)S(1)} %copy-done.1, f32[1,8192]{1,0:T(1,128)S(1)} %bitcast.19, s32[4,8192]{1,0:T(4,128)S(1)} %copy-done.3, s32[1,8192]{1,0:T(1,128)S(1)} %bitcast.23, ...), custom_call_target="tpu_custom_call" | custom-call | tf_op jit(solution)/shard_map/pallas_call | solution.py:381
  28.5 10.3 %all-to-all-done = f32[128,5,4,128]{3,2,1,0:T(4,128)} async-done(((f32[128,5,4,128]{3,2,1,0:T(4,128)}), f32[128,5,4,128]{3,2,1,0:T(4,128)}, u32[]{:S(2)}, u32[]{:S(2)}) %all-to-all-start) | async-done | bytes 1310752 | tf_op jit(solution)/shard_map/all_to_all | solution.py:490
  38.7 25.1 %shard_map.160 = (f32[64,3,128]{2,1,0:T(4,128)S(1)}, f32[2048,128]{1,0:T(8,128)S(1)}) custom-call(s32[512]{0:T(512)S(1)} %copy-done.18, s32[512]{0:T(512)S(1)} %copy-done.19, f32[64,4,128]{2,1,0:T(4,128)S(1)} %get-tuple-element.12.own_ref, f32[640,4,128]{2,1,0:T(4,128)} %bitcast.2.recv_ref, s32[4,128]{1,0:T(4,128)S(1)} %bitcast.25, ...), custom_call_target="tpu_custom_call" | custom-call | tf_op jit(solution)/shard_map/pallas_call | solution.py:412
  63.8 1.0 copy-done.2
  64.8 0.7 copy-done.7
  65.5 15.7 %all-to-all-start.1 = ((f32[128,16,128]{2,1,0:T(8,128)}), f32[128,16,128]{2,1,0:T(8,128)S(1)}, u32[]{:S(2)}, u32[]{:S(2)}) async-start(f32[128,16,128]{2,1,0:T(8,128)} %bitcast.18), calls=%async_computation.1 | async-start | bytes 2097152 | tf_op jit(solution)/shard_map/all_to_all | solution.py:510
  81.1 0.0 copy-start.8
  81.2 0.9 copy-done.8
  82.0 8.2 %shard_map.161.int_ref = f32[96,256]{1,0:T(8,128)S(1)} custom-call(s32[4,8192]{1,0:T(4,128)S(1)} %copy-done.3, f32[32,16,1024]{2,1,0:T(8,128)S(1)} %get-tuple-element.16.force_ref, s32[64,128]{1,0:T(8,128)S(1)} %copy-done.5, f32[64,3,128]{2,1,0:T(4,128)S(1)} %copy-done.8), custom_call_target="tpu_custom_call" | custom-call | tf_op jit(solution)/shard_map/pallas_call | solution.py:396
  90.2 7.8 %all-to-all-done.1 = f32[128,16,128]{2,1,0:T(8,128)S(1)} async-done(((f32[128,16,128]{2,1,0:T(8,128)}), f32[128,16,128]{2,1,0:T(8,128)S(1)}, u32[]{:S(2)}, u32[]{:S(2)}) %all-to-all-start.1) | async-done | bytes 1048608 | tf_op jit(solution)/shard_map/all_to_all | solution.py:510
  98.1 0.7 copy-done.14
  98.7 3.2 %shard_map.162 = (f32[96,256]{1,0:T(8,128)S(1)}, f32[3,2048]{1,0:T(4,128)S(1)}, f32[3,2048]{1,0:T(4,128)S(1)}, f32[1,128]{1,0:T(1,128)S(1)}) custom-call(s32[5,128]{1,0:T(8,128)S(1)} %bitcast.22, f32[2048,128]{1,0:T(8,128)S(1)} %bitcast.17, s32[64,128]{1,0:T(8,128)S(1)} %copy-done.5, f32[96,256]{1,0:T(8,128)S(1)} %shard_map.161.int_ref, s32[2,2048]{1,0:T(2,128)S(1)} %copy-done.12), custom_call_target="tpu_custom_call" | custom-call | tf_op jit(solution)/shard_map/pallas_call | solution.py:433
  101.9 4.5 %collective-permute-start = (f32[3,2048]{1,0:T(4,128)S(1)}, f32[3,2048]{1,0:T(4,128)S(1)}, u32[]{:S(2)}, u32[]{:S(2)}) collective-permute-start(f32[3,2048]{1,0:T(4,128)S(1)} %get-tuple-element.20), channel_id=1, source_target_pairs={{0,1},{1,2},{2,3},{3,4},{4,5},{5,6},{6,7},{7,8},{8,9},{9,10},{10,1... | collective-permute-start | bytes 73736 | tf_op jit(solution)/shard_map/ppermute | solution.py:466
  106.4 1.9 %collective-permute-start.1 = (f32[3,2048]{1,0:T(4,128)S(1)}, f32[3,2048]{1,0:T(4,128)S(1)}, u32[]{:S(2)}, u32[]{:S(2)}) collective-permute-start(f32[3,2048]{1,0:T(4,128)S(1)} %get-tuple-element.21), channel_id=1, source_target_pairs={{1,0},{2,1},{3,2},{4,3},{5,4},{6,5},{7,6},{8,7},{9,8},{10,9},{11,1... | collective-permute-start | bytes 73736 | tf_op jit(solution)/shard_map/ppermute | solution.py:466
  108.4 0.0 collective-permute-done.low_ref
  108.4 6.0 %collective-permute-done.1.up_ref = f32[3,2048]{1,0:T(4,128)S(1)} collective-permute-done((f32[3,2048]{1,0:T(4,128)S(1)}, f32[3,2048]{1,0:T(4,128)S(1)}, u32[]{:S(2)}, u32[]{:S(2)}) %collective-permute-start.1) | collective-permute-done | bytes 24608 | tf_op jit(solution)/shard_map/ppermute | solution.py:466
  114.3 0.9 copy-done.6
  115.3 0.8 copy-done.11
  116.0 1.8 %shard_map.163 = (f32[3,8192]{1,0:T(4,128)}, f32[3,8192]{1,0:T(4,128)}) custom-call(f32[1,128]{1,0:T(1,128)S(1)} %get-tuple-element.18.lim_ref, f32[96,256]{1,0:T(8,128)S(1)} %get-tuple-element.19.tot_ref, s32[2,2048]{1,0:T(2,128)S(1)} %copy-done.12, f32[3,2048]{1,0:T(4,128)S(1)} %collective-permute-done.low_ref, ...), custom_call_target="tpu_custom_call" | custom-call | tf_op jit(solution)/shard_map/pallas_call | solution.py:450
  (27 shorter events, 0.0 us)
Async XLA Ops:
  1.3 7.5 %copy-start.13 = (s32[1,128,5]{1,2,0:T(8,128)}, s32[1,128,5]{1,2,0:T(8,128)S(1)}, u32[]{:S(2)}) copy-start(s32[1,128,5]{1,2,0:T(8,128)S(1)} %copy.20) | copy-start | bytes 7684
  1.3 0.9 copy-start
  2.2 0.8 copy-start.4
  3.0 0.9 copy-start.9
  3.9 0.8 copy-start.15
  8.8 10.4 %copy-start.1 = (f32[3,8192]{1,0:T(4,128)S(1)}, f32[3,8192]{1,0:T(4,128)}, u32[]{:S(2)}) copy-start(f32[3,8192]{1,0:T(4,128)} %disp_ref.5) | copy-start | bytes 294916
  8.8 10.4 %copy-start.3 = (s32[4,8192]{1,0:T(4,128)S(1)}, s32[4,8192]{1,0:T(4,128)}, u32[]{:S(2)}) copy-start(s32[4,8192]{1,0:T(4,128)} %nodes_ref.3) | copy-start | bytes 393220
  8.8 10.4 %copy-start.10 = (f32[8192]{0:T(1024)S(1)}, f32[8192]{0:T(1024)}, u32[]{:S(2)}) copy-start(f32[8192]{0:T(1024)} %param.18) | copy-start | bytes 98308
  8.9 10.4 %copy-start.16 = (s32[8192]{0:T(1024)S(1)}, s32[8192]{0:T(1024)}, u32[]{:S(2)}) copy-start(s32[8192]{0:T(1024)} %param.20) | copy-start | bytes 98308
  8.9 10.4 %copy-start.17 = (f32[8192]{0:T(1024)S(1)}, f32[8192]{0:T(1024)}, u32[]{:S(2)}) copy-start(f32[8192]{0:T(1024)} %param.21) | copy-start | bytes 98308
  8.9 10.4 %copy-start.21 = (f32[4]{0:T(128)S(1)}, f32[4]{0:T(128)}, u32[]{:S(2)}) copy-start(f32[4]{0:T(128)} %stiff_ref.1) | copy-start | bytes 52
  8.9 29.8 %copy-start.18 = (s32[512]{0:T(512)S(1)}, s32[512]{0:T(512)}, u32[]{:S(2)}) copy-start(s32[512]{0:T(512)} %near_ref.1) | copy-start | bytes 6148
  8.9 29.8 %copy-start.19 = (s32[512]{0:T(512)S(1)}, s32[512]{0:T(512)}, u32[]{:S(2)}) copy-start(s32[512]{0:T(512)} %far_ref.1) | copy-start | bytes 6148
  8.9 29.8 %copy-start.20 = (s32[512]{0:T(512)S(1)}, s32[512]{0:T(512)}, u32[]{:S(2)}) copy-start(s32[512]{0:T(512)} %param.29) | copy-start | bytes 6148
  8.9 29.8 %all-to-all-start = ((f32[128,5,4,128]{3,2,1,0:T(4,128)}), f32[128,5,4,128]{3,2,1,0:T(4,128)}, u32[]{:S(2)}, u32[]{:S(2)}) async-start(f32[128,5,4,128]{3,2,1,0:T(4,128)} %get-tuple-element.13), calls=%async_computation | async-start | bytes 2621440 | tf_op jit(solution)/shard_map/all_to_all | solution.py:490
  63.8 1.0 copy-start.2
  64.8 0.7 copy-start.7
  65.5 15.7 %copy-start.5 = (s32[64,128]{1,0:T(8,128)S(1)}, s32[64,128]{1,0:T(8,128)}, u32[]{:S(2)}) copy-start(s32[64,128]{1,0:T(8,128)} %seg_ref.5) | copy-start | bytes 98308
  65.5 32.6 %copy-start.12 = (s32[2,2048]{1,0:T(2,128)S(1)}, s32[2,2048]{1,0:T(2,128)}, u32[]{:S(2)}) copy-start(s32[2,2048]{1,0:T(2,128)} %share_ref.3) | copy-start | bytes 49156
  65.5 32.6 %all-to-all-start.1 = ((f32[128,16,128]{2,1,0:T(8,128)}), f32[128,16,128]{2,1,0:T(8,128)S(1)}, u32[]{:S(2)}, u32[]{:S(2)}) async-start(f32[128,16,128]{2,1,0:T(8,128)} %bitcast.18), calls=%async_computation.1 | async-start | bytes 2097152 | tf_op jit(solution)/shard_map/all_to_all | solution.py:510
  81.1 0.9 copy-start.8
  98.1 0.7 copy-start.14
  101.9 6.4 %collective-permute-start = (f32[3,2048]{1,0:T(4,128)S(1)}, f32[3,2048]{1,0:T(4,128)S(1)}, u32[]{:S(2)}, u32[]{:S(2)}) collective-permute-start(f32[3,2048]{1,0:T(4,128)S(1)} %get-tuple-element.20), channel_id=1, source_target_pairs={{0,1},{1,2},{2,3},{3,4},{4,5},{5,6},{6,7},{7,8},{8,9},{9,10},{10,1... | collective-permute-start | bytes 73736 | tf_op jit(solution)/shard_map/ppermute | solution.py:466
  106.4 7.9 %collective-permute-start.1 = (f32[3,2048]{1,0:T(4,128)S(1)}, f32[3,2048]{1,0:T(4,128)S(1)}, u32[]{:S(2)}, u32[]{:S(2)}) collective-permute-start(f32[3,2048]{1,0:T(4,128)S(1)} %get-tuple-element.21), channel_id=1, source_target_pairs={{1,0},{2,1},{3,2},{4,3},{5,4},{6,5},{7,6},{8,7},{9,8},{10,9},{11,1... | collective-permute-start | bytes 73736 | tf_op jit(solution)/shard_map/ppermute | solution.py:466
  114.3 0.9 copy-start.6
  115.3 0.8 copy-start.11

commit v5 on v4

--- a/solution.py
+++ b/solution.py
@@ -12,6 +12,8 @@
 COURANT = 0.5
 LOW = 256
 PIECES = 3
+FULL_VMEM = 64 << 20
+SMALL_VMEM = 16 << 20
 WIDTH = 256
 SCALE = math.sqrt(math.log2(math.e))
 PARK = 1.0e3
@@ -155,8 +157,15 @@
     lim_ref[...] = jnp.broadcast_to(jnp.min(limit, 1, keepdims=True), lim_ref.shape)
 
 
-def scatter_body(nodes_ref, force_ref, seg_ref, own_ref, tot_ref, acc, cut):
+def scatter_body(
+    nodes_ref, force_ref, seg_ref, own, vel_ref, disp_ref, mass_ref, tot_ref, vel_out, disp_out, inv_out, acc, cut
+):
     high = tot_ref.shape[0] // 3
+    for c in range(3):
+        fill_table(vel_out, c * high, vel_ref, c, high)
+        fill_table(disp_out, c * high, disp_ref, c, high)
+    fill_table(inv_out, 0, mass_ref, 0, high)
+    inv_out[...] = 1.0 / inv_out[...]
     acc[...] = jnp.zeros_like(acc)
 
     def some(g, carry):
@@ -173,7 +182,7 @@
         base = pl.multiple_of(g * group, group)
         seg = seg_ref[pl.ds(base, group), :]
         idx = jnp.concatenate([seg[k : k + 1] for k in range(group)], 1)
-        cut[0:9] = cut_rows(jnp.concatenate([own_ref[base + k] for k in range(group)], 1))
+        cut[0:9] = cut_rows(jnp.concatenate([own[base + k] for k in range(group)], 1))
         acc[...] += add_hot(spread(cut, idx, high), low_hot(idx))
         return carry
 
@@ -183,12 +192,15 @@
 
 
 def contact_body(
-    near_ref, far_ref, own_ref, recv_ref, live_ref, lim_ref, own_out, far_out, wide, total_a, total_b, remote, rows, chosen, recoils
+    near_ref, far_ref, own_ref, recv_ref, live_ref, lim_ref, own_out, far_out, wide, total_a, total_b, recoils, landed, near, far, rows, chosen, sems
 ):
-    blocks = own_ref.shape[0]
-    slots = recv_ref.shape[0]
-    seg = own_ref.shape[2]
+    blocks = total_a.shape[0]
+    slots = landed.shape[0]
+    seg = landed.shape[2]
     cap = 5
+    fetch = pltpu.make_async_copy(recv_ref, landed, sems.at[0])
+    fetch.start()
+
     group = 8
     line = lax.broadcasted_iota(jnp.int32, (seg, 3 * seg), 0)
     part = lax.broadcasted_iota(jnp.int32, (seg, 3 * seg), 1) >> 7
@@ -198,13 +210,11 @@
         chosen[k] = jnp.where(hit, 1.0, 0.0).astype(bf16)
     rows[...] = jnp.zeros_like(rows)
 
-    def scaled(block, parked):
-        x = jnp.where(block[3:4] > 0.5, block[0:1] * SCALE, parked)
-        return jnp.concatenate([x, block[1:3] * SCALE], 0)
-
     def widen(g, carry):
         for k in range(group):
-            xyz = scaled(own_ref[g * group + k], PARK)
+            block = own_ref[g * group + k]
+            x = jnp.where(block[3:4] > 0.5, block[0:1] * SCALE, PARK)
+            xyz = jnp.concatenate([x, block[1:3] * SCALE], 0)
             for p, piece in enumerate(pieces_of(xyz)):
                 rows[16 * k + 3 * p : 16 * k + 3 * p + 3, :] = piece.astype(f32)
         columns = rows[...].T.astype(bf16)
@@ -217,25 +227,22 @@
         return carry
 
     lax.fori_loop(0, blocks // group, widen, 0, unroll=4)
-    def ready(s, carry):
-        block = recv_ref[s]
-        remote[s, 0:3] = scaled(block, -PARK)
-        return carry
-
-    lax.fori_loop(0, slots, ready, 0, unroll=8)
     recoils[...] = jnp.zeros_like(recoils)
     live = jnp.sum(live_ref[...])
+    fetch.wait()
 
     def pair(p, total):
         b = near_ref[p]
         s = far_ref[p]
-        there = [jnp.broadcast_to(remote[s, c : c + 1, :], (8, seg)) for c in range(3)]
+        there = [jnp.broadcast_to(landed[s, c : c + 1, :], (8, seg)) for c in range(4)]
+        x = jnp.where(there[3] > 0.5, there[0] * SCALE, -PARK)
+        there = [x, there[1] * SCALE, there[2] * SCALE]
         recoil = [None] * 3
         for v in range(seg // 8):
             at = pl.ds(v * 8, 8)
             gap = [wide[b, c, at, :] - there[c] for c in range(3)]
-            far = gap[0] * gap[0] + gap[1] * gap[1] + gap[2] * gap[2]
-            weight = jnp.exp2(-far)
+            square = gap[0] * gap[0] + gap[1] * gap[1] + gap[2] * gap[2]
+            weight = jnp.exp2(-square)
             for c in range(3):
                 push = weight * gap[c]
                 total[b, c, at, :] += push
@@ -257,14 +264,6 @@
     whole = live >> 2
     lax.fori_loop(0, whole, four, 0)
     lax.fori_loop(4 * whole, live, one, 0)
-
-    def close(b, carry):
-        for c in range(3):
-            total = total_a[b, c] + total_b[b, c]
-            own_out[b, c : c + 1, :] = jnp.sum(total.T, 0, keepdims=True) * (1.0 / SCALE)
-        return carry
-
-    lax.fori_loop(0, blocks, close, 0, unroll=8)
     peers = slots // cap
     stamp = jnp.broadcast_to(lim_ref[...], (8, seg))
 
@@ -275,11 +274,25 @@
                 rows = [recoils[c, pl.ds(at + r, 8, stride=8 * cap), :] for r in range(8)]
                 while len(rows) > 1:
                     rows = [x + y for x, y in zip(rows[::2], rows[1::2])]
-                far_out[pl.ds(g * 128 + 3 * k + c, 8, stride=16), :] = rows[0] * (-1.0 / SCALE)
-        far_out[pl.ds(g * 128 + 15, 8, stride=16), :] = stamp
+                far[pl.ds(g * 128 + 3 * k + c, 8, stride=16), :] = rows[0] * (-1.0 / SCALE)
+        far[pl.ds(g * 128 + 15, 8, stride=16), :] = stamp
         return carry
 
     lax.fori_loop(0, peers // 8, finish, 0, unroll=4)
+    give_far = pltpu.make_async_copy(far, far_out, sems.at[1])
+    give_far.start()
+
+    def close(b, carry):
+        for c in range(3):
+            total = total_a[b, c] + total_b[b, c]
+            near[b, c : c + 1, :] = jnp.sum(total.T, 0, keepdims=True) * (1.0 / SCALE)
+        return carry
+
+    lax.fori_loop(0, blocks, close, 0, unroll=8)
+    give_near = pltpu.make_async_copy(near, own_out, sems.at[2])
+    give_near.start()
+    give_far.wait()
+    give_near.wait()
 
 
 def seg_body(
@@ -326,30 +339,35 @@
 
 
 def last_body(
-    lim_ref, tot_ref, share_ref, low_ref, up_ref, vel_ref, disp_ref, mass_ref, new_disp, new_vel, acc, cut
+    lim_ref, tot_ref, share_ref, low_ref, up_ref, vel_ref, disp_ref, inv_ref, new_disp, new_vel, cut
 ):
     high = tot_ref.shape[0] // 3
     count = share_ref.shape[1]
-    total = jnp.zeros(acc.shape, f32)
+    total = jnp.zeros((PIECES * 3 * high, LOW), f32)
     for row, src in ((0, low_ref), (1, up_ref)):
-        for at in range(0, count, 1024):
+        for k, at in enumerate(range(0, count, 1024)):
             idx = share_ref[row : row + 1, at : at + 1024]
-            cut[0:9] = cut_rows(src[:, at : at + 1024])
-            total = total + add_hot(spread(cut, idx, high), low_hot(idx))
-    rows = 3 * high
-    acc[0:rows] = ((total[2 * rows :] + total[rows : 2 * rows]) + total[:rows]) + tot_ref[...]
+            rows = cut.at[2 * row + k]
+            rows[0:9] = cut_rows(src[:, at : at + 1024])
+            total = total + add_hot(spread(rows, idx, high), low_hot(idx))
+    size = 3 * high
+    force = ((total[2 * size :] + total[size : 2 * size]) + total[:size]) + tot_ref[...]
     step = jnp.min(lim_ref[...], 1, keepdims=True)
-    for h in range(high):
-        at = slice(h * LOW, (h + 1) * LOW)
-        mass = mass_ref[0:1, at]
-        for c in range(3):
-            vel = vel_ref[c : c + 1, at] + step * (acc[c * high + h : c * high + h + 1, :] / mass)
-            new_vel[c : c + 1, at] = vel
-            new_disp[c : c + 1, at] = disp_ref[c : c + 1, at] + step * vel
+    for c in range(3):
+        at = slice(c * high, (c + 1) * high)
+        vel = vel_ref[at] + step * (force[at] * inv_ref[...])
+        disp = disp_ref[at] + step * vel
+        for h in range(high):
+            new_vel[c : c + 1, h * LOW : (h + 1) * LOW] = vel[h : h + 1]
+            new_disp[c : c + 1, h * LOW : (h + 1) * LOW] = disp[h : h + 1]
 
 
 def vmem(count):
     return [pl.BlockSpec(memory_space=pltpu.VMEM)] * count
+
+
+def hbm(count):
+    return [pl.BlockSpec(memory_space=pltpu.HBM)] * count
 
 
 def smem(count):
@@ -372,7 +390,6 @@
             pltpu.VMEM((3 * high, LOW), f32),
             pltpu.VMEM((PIECES * 3 * high, LOW), bf16),
         ],
-        compiler_params=pltpu.CompilerParams(vmem_limit_bytes=24 << 20),
     )(send, disp, ref_pos, seg_node, seg_mask)
 
 
@@ -387,23 +404,23 @@
             pltpu.VMEM((4 * high, LOW), f32),
             pltpu.VMEM((PIECES * 4 * high, LOW), bf16),
         ],
-        compiler_params=pltpu.CompilerParams(vmem_limit_bytes=24 << 20),
+        compiler_params=pltpu.CompilerParams(vmem_limit_bytes=FULL_VMEM),
     )(first, stiff, disp, mass, nodes, part, scale)
 
 
-def scatter_call(nodes, force, seg_node, own):
+def scatter_call(nodes, force, seg_node, own, vel, disp, mass):
     high = nodes.shape[1] // LOW
     return pl.pallas_call(
         scatter_body,
-        out_shape=struct(3 * high, LOW),
-        in_specs=vmem(4),
-        out_specs=vmem(1)[0],
+        out_shape=(struct(3 * high, LOW), struct(3 * high, LOW), struct(3 * high, LOW), struct(high, LOW)),
+        in_specs=vmem(7),
+        out_specs=tuple(vmem(4)),
         scratch_shapes=[
             pltpu.VMEM((PIECES * 3 * high, LOW), f32),
             pltpu.VMEM((16, 1024), f32),
         ],
-        compiler_params=pltpu.CompilerParams(vmem_limit_bytes=24 << 20),
-    )(nodes, force, seg_node, own)
+        compiler_params=pltpu.CompilerParams(vmem_limit_bytes=SMALL_VMEM),
+    )(nodes, force, seg_node, own, vel, disp, mass)
 
 
 def contact_call(pair_a, pair_slot, own, recv, live, lim, peers):
@@ -412,18 +429,21 @@
     return pl.pallas_call(
         contact_body,
         out_shape=(struct(blocks, 3, seg), struct(peers * 16, seg)),
-        in_specs=smem(2) + vmem(4),
-        out_specs=tuple(vmem(2)),
+        in_specs=smem(2) + vmem(1) + hbm(1) + vmem(2),
+        out_specs=tuple(hbm(2)),
         scratch_shapes=[
             pltpu.VMEM((blocks, 3, seg, seg), f32),
             pltpu.VMEM((blocks, 3, seg, seg), f32),
             pltpu.VMEM((blocks, 3, seg, seg), f32),
-            pltpu.VMEM((slots, 4, seg), f32),
+            pltpu.VMEM((3, slots * 8, seg), f32),
+            pltpu.VMEM(recv.shape, f32),
+            pltpu.VMEM((blocks, 3, seg), f32),
+            pltpu.VMEM((peers * 16, seg), f32),
             pltpu.VMEM((seg, seg), f32),
             pltpu.VMEM((8, seg, 3 * seg), bf16),
-            pltpu.VMEM((3, slots * 8, seg), f32),
+            pltpu.SemaphoreType.DMA((3,)),
         ],
-        compiler_params=pltpu.CompilerParams(vmem_limit_bytes=52 << 20),
+        compiler_params=pltpu.CompilerParams(vmem_limit_bytes=FULL_VMEM),
     )(pair_a, pair_slot, own, recv, live, lim)
 
 
@@ -441,23 +461,21 @@
             pltpu.VMEM((PIECES * 3 * high, LOW), f32),
             pltpu.VMEM((16, 1024), f32),
         ],
-        compiler_params=pltpu.CompilerParams(vmem_limit_bytes=24 << 20),
+        compiler_params=pltpu.CompilerParams(vmem_limit_bytes=SMALL_VMEM),
     )(send, back.reshape(-1, 128), seg_node, inner, shared)
 
 
-def last_call(lim, total, shared, lower, upper, vel, disp, mass):
-    high = total.shape[0] // 3
+def last_call(lim, total, shared, lower, upper, vel, disp, inv):
+    high = inv.shape[0]
+    nodes = struct(3, high * LOW)
     return pl.pallas_call(
         last_body,
-        out_shape=(struct(*disp.shape), struct(*disp.shape)),
+        out_shape=(nodes, nodes),
         in_specs=vmem(8),
         out_specs=tuple(vmem(2)),
-        scratch_shapes=[
-            pltpu.VMEM((PIECES * 3 * high, LOW), f32),
-            pltpu.VMEM((16, 1024), f32),
-        ],
-        compiler_params=pltpu.CompilerParams(vmem_limit_bytes=24 << 20),
-    )(lim, total, shared, lower, upper, vel, disp, mass)
+        scratch_shapes=[pltpu.VMEM((4, 16, 1024), f32)],
+        compiler_params=pltpu.CompilerParams(vmem_limit_bytes=SMALL_VMEM),
+    )(lim, total, shared, lower, upper, vel, disp, inv)
 
 
 def shifted(value, axis, steps):
@@ -510,11 +528,13 @@
     back = lax.all_to_all(
         far_force.reshape(peers, 16, -1), ("grp", "dev"), split_axis=0, concat_axis=0, tiled=True
     )
-    inner = scatter_call(elem_nodes, force, seg_node, own_force)
+    inner, vel, disp, inv = scatter_call(
+        elem_nodes, force, seg_node, own_force, velocity, displacement, mass
+    )
     total, low_rows, up_rows, limits = seg_call(send, back, seg_node, inner, shared)
     from_lower = shifted(up_rows, "dev", 1)
     from_upper = shifted(low_rows, "dev", -1)
-    return last_call(limits, total, shared, from_lower, from_upper, velocity, displacement, mass)
+    return last_call(limits, total, shared, from_lower, from_upper, vel, disp, inv)
 
 
 def solution(mesh):

time: 119 us -> 111 us (0.933)
  waiting for transfers between devices: 24.1 us -> 18 us
  Pallas kernels: 51.6 us -> 54.5 us
  local copies, waits for them, and re-layouts: 8.95 us -> 6.41 us
  starting transfers between devices: 32.3 us -> 31.1 us
    all_to_all x1, waiting for transfers between devices: 7.82 us -> 3.45 us  [shards(): lax.all_to_all(far_force.reshape(peers, 16, -1), ('grp', 'dev'), split_ax...]
    unnamed x45 -> x21, local copies, waits for them, and re-layouts: 8.95 us -> 6.41 us
    pallas_call x1, Pallas kernels: 9.21 us -> 10.9 us  [force_call(): pl.pallas_call(force_body, out_shape=(struct(nodes.shape[1] // WIDTH, 16,...]
    all_to_all x1, waiting for transfers between devices: 10.3 us -> 8.59 us  [shards(): lax.all_to_all(outgoing, ('grp', 'dev'), split_axis=0, concat_axis=0, til...]
  transfers between devices with their start and end apart: 4 -> 4, of which waited for: 3 -> 3; matrix products, arithmetic and copies ran while one was open for 0% -> 0% of each run, Pallas kernels for 15% -> 17%
where the time goes in v5:
time: 111 us
  Pallas kernels  54.5 us (49%)
  starting transfers between devices  31.1 us (28%)
  waiting for transfers between devices  18 us (16%)
  local copies, waits for them, and re-layouts  6.41 us (6%)
    pallas_call x1, Pallas kernels, contact_call(): pl.pallas_call(contact_body, out_shape=(struct(blocks, 3, seg), struct(pe...  25.8 us
    all_to_all x1, starting transfers between devices, shards(): lax.all_to_all(far_force.reshape(peers, 16, -1), ('grp', 'dev'), split_ax...  14.5 us
    pallas_call x1, Pallas kernels, force_call(): pl.pallas_call(force_body, out_shape=(struct(nodes.shape[1] // WIDTH, 16,...  10.9 us
    all_to_all x1, starting transfers between devices, shards(): lax.all_to_all(outgoing, ('grp', 'dev'), split_axis=0, concat_axis=0, til...  10.3 us
    all_to_all x1, waiting for transfers between devices, shards(): lax.all_to_all(outgoing, ('grp', 'dev'), split_axis=0, concat_axis=0, til...  8.59 us
    pallas_call x1, Pallas kernels, scatter_call(): pl.pallas_call(scatter_body, out_shape=(struct(3 * high, LOW), struct(3 *...  8.32 us
    unnamed x21, local copies, waits for them, and re-layouts  6.41 us
    ppermute x2, starting transfers between devices, shifted(): lax.ppermute(value, axis, [(source, source + steps) for source in range(f...  6.4 us
  transfers between devices with their start and end apart: 4, of which 3 were waited for; matrix products, arithmetic and copies ran while one was open for 0% of the time, Pallas kernels for 17%

profile of v5, /device:TPU:96, one launch (start us, length us, event | category | flops | bytes accessed | tf_op | source)
XLA Modules:
  0.0 110.7 jit_solution(11133771298785064280)
XLA Ops:
  0.6 1.3 %copy.20 = s32[1,128,5]{1,2,0:T(8,128)} copy(s32[1,128,5]{1,0,2:T(1,128)} %param.26) | data formatting | bytes 5120
  1.9 4.6 %shard_map.158 = (f32[64,4,128]{2,1,0:T(4,128)}, f32[128,5,4,128]{3,2,1,0:T(4,128)}) custom-call(s32[640]{0:T(1024)} %bitcast.20, f32[3,8192]{1,0:T(4,128)} %disp_ref.5, f32[3,8192]{1,0:T(4,128)} %ref_ref.1, s32[64,128]{1,0:T(8,128)} %seg_ref.5, s32[64,128]{1,0:T(8,128)} %mask_ref.1), custom_call_target="tpu_custom_call" | custom-call | tf_op jit(solution)/shard_map/pallas_call | solution.py:384
  6.5 10.3 %all-to-all-start = ((f32[128,5,4,128]{3,2,1,0:T(4,128)}), f32[128,5,4,128]{3,2,1,0:T(4,128)}, u32[]{:S(2)}, u32[]{:S(2)}) async-start(f32[128,5,4,128]{3,2,1,0:T(4,128)} %get-tuple-element.17), calls=%async_computation | async-start | bytes 2621440 | tf_op jit(solution)/shard_map/all_to_all | solution.py:508
  16.8 10.9 %shard_map.159 = (f32[32,16,1024]{2,1,0:T(8,128)}, f32[1,128]{1,0:T(1,128)}) custom-call(s32[1]{0:T(128)} %bitcast.4.first_ref, f32[4]{0:T(128)} %stiff_ref.1, f32[3,8192]{1,0:T(4,128)} %disp_ref.5, f32[1,8192]{1,0:T(1,128)} %bitcast.18, s32[4,8192]{1,0:T(4,128)} %nodes_ref.3, s32[1,8192]{1,0:T(1,128)} %bitcast.23, f32[1,8192]{1,0:T(1,128)} %bitcast.24), custom_call_target="tpu_custom_call" | custom-call | tf_op jit(solution)/shard_map/pallas_call | solution.py:398
  27.7 8.6 %all-to-all-done = f32[128,5,4,128]{3,2,1,0:T(4,128)} async-done(((f32[128,5,4,128]{3,2,1,0:T(4,128)}), f32[128,5,4,128]{3,2,1,0:T(4,128)}, u32[]{:S(2)}, u32[]{:S(2)}) %all-to-all-start) | async-done | bytes 1310752 | tf_op jit(solution)/shard_map/all_to_all | solution.py:508
  36.3 25.8 %shard_map.160 = (f32[64,3,128]{2,1,0:T(4,128)}, f32[2048,128]{1,0:T(8,128)}) custom-call(s32[512]{0:T(512)} %near_ref.1, s32[512]{0:T(512)} %far_ref.1, f32[64,4,128]{2,1,0:T(4,128)} %get-tuple-element.16.own_ref, f32[640,4,128]{2,1,0:T(4,128)} %bitcast.2.recv_ref, s32[4,128]{1,0:T(4,128)} %bitcast.25, f32[1,128]{1,0:T(1,128)} %get-tuple-element.18.lim_ref), custom_call_target="tpu_custom_call" | custom-call | tf_op jit(solution)/shard_map/pallas_call | solution.py:429
  62.1 0.0 copy-start
  62.1 14.5 %all-to-all-start.1 = ((f32[128,16,128]{2,1,0:T(8,128)}), f32[128,16,128]{2,1,0:T(8,128)S(1)}, u32[]{:S(2)}, u32[]{:S(2)}) async-start(f32[128,16,128]{2,1,0:T(8,128)} %bitcast.22), calls=%async_computation.1 | async-start | bytes 2097152 | tf_op jit(solution)/shard_map/all_to_all | solution.py:528
  76.6 0.0 copy-done
  76.6 0.0 copy-start.1
  76.6 0.9 copy-done.1
  77.5 0.0 copy-start.2
  77.5 0.9 copy-done.2
  78.4 0.0 copy-start.3
  78.4 0.8 copy-done.3
  79.2 0.0 copy-start.5
  79.2 0.8 copy-done.5
  80.0 0.0 copy-start.6
  80.0 0.9 copy-done.6
  80.9 0.0 copy-start.7
  80.9 0.9 copy-done.7
  81.8 8.3 %shard_map.161 = (f32[96,256]{1,0:T(8,128)S(1)}, f32[96,256]{1,0:T(8,128)S(1)}, f32[96,256]{1,0:T(8,128)S(1)}, f32[32,256]{1,0:T(8,128)S(1)}) custom-call(s32[4,8192]{1,0:T(4,128)S(1)} %copy-done.2, f32[32,16,1024]{2,1,0:T(8,128)S(1)} %copy-done, s32[64,128]{1,0:T(8,128)S(1)} %copy-done.3, f32[64,3,128]{2,1,0:T(4,128)S(1)} %copy-done.7, ...), custom_call_target="tpu_custom_call" | custom-call | tf_op jit(solution)/shard_map/pallas_call | solution.py:413
  90.1 3.4 %all-to-all-done.1 = f32[128,16,128]{2,1,0:T(8,128)S(1)} async-done(((f32[128,16,128]{2,1,0:T(8,128)}), f32[128,16,128]{2,1,0:T(8,128)S(1)}, u32[]{:S(2)}, u32[]{:S(2)}) %all-to-all-start.1) | async-done | bytes 1048608 | tf_op jit(solution)/shard_map/all_to_all | solution.py:528
  93.6 0.0 copy-done.4
  93.6 0.0 copy-done.8
  93.6 0.0 copy-done.9
  93.6 3.2 %shard_map.162 = (f32[96,256]{1,0:T(8,128)S(1)}, f32[3,2048]{1,0:T(4,128)S(1)}, f32[3,2048]{1,0:T(4,128)S(1)}, f32[1,128]{1,0:T(1,128)S(1)}) custom-call(s32[5,128]{1,0:T(8,128)S(1)} %bitcast.21, f32[2048,128]{1,0:T(8,128)S(1)} %bitcast.17, s32[64,128]{1,0:T(8,128)S(1)} %copy-done.4, f32[96,256]{1,0:T(8,128)S(1)} %get-tuple-element.22.int_ref, ...), custom_call_target="tpu_custom_call" | custom-call | tf_op jit(solution)/shard_map/pallas_call | solution.py:453
  96.8 4.5 %collective-permute-start = (f32[3,2048]{1,0:T(4,128)S(1)}, f32[3,2048]{1,0:T(4,128)S(1)}, u32[]{:S(2)}, u32[]{:S(2)}) collective-permute-start(f32[3,2048]{1,0:T(4,128)S(1)} %get-tuple-element.25), channel_id=1, source_target_pairs={{0,1},{1,2},{2,3},{3,4},{4,5},{5,6},{6,7},{7,8},{8,9},{9,10},{10,1... | collective-permute-start | bytes 73736 | tf_op jit(solution)/shard_map/ppermute | solution.py:484
  101.2 1.9 %collective-permute-start.1 = (f32[3,2048]{1,0:T(4,128)S(1)}, f32[3,2048]{1,0:T(4,128)S(1)}, u32[]{:S(2)}, u32[]{:S(2)}) collective-permute-start(f32[3,2048]{1,0:T(4,128)S(1)} %get-tuple-element.26), channel_id=1, source_target_pairs={{1,0},{2,1},{3,2},{4,3},{5,4},{6,5},{7,6},{8,7},{9,8},{10,9},{11,1... | collective-permute-start | bytes 73736 | tf_op jit(solution)/shard_map/ppermute | solution.py:484
  103.2 0.0 collective-permute-done.low_ref
  103.2 6.0 %collective-permute-done.1.up_ref = f32[3,2048]{1,0:T(4,128)S(1)} collective-permute-done((f32[3,2048]{1,0:T(4,128)S(1)}, f32[3,2048]{1,0:T(4,128)S(1)}, u32[]{:S(2)}, u32[]{:S(2)}) %collective-permute-start.1) | collective-permute-done | bytes 24608 | tf_op jit(solution)/shard_map/ppermute | solution.py:484
  109.2 1.6 %shard_map.163 = (f32[3,8192]{1,0:T(4,128)}, f32[3,8192]{1,0:T(4,128)}) custom-call(f32[1,128]{1,0:T(1,128)S(1)} %get-tuple-element.23.lim_ref, f32[96,256]{1,0:T(8,128)S(1)} %get-tuple-element.24.tot_ref, s32[2,2048]{1,0:T(2,128)S(1)} %copy-done.8, f32[3,2048]{1,0:T(4,128)S(1)} %collective-permute-done.low_ref, ...), custom_call_target="tpu_custom_call" | custom-call | tf_op jit(solution)/shard_map/pallas_call | solution.py:471
  (3 shorter events, 0.0 us)
Async XLA Ops:
  6.5 29.8 %all-to-all-start = ((f32[128,5,4,128]{3,2,1,0:T(4,128)}), f32[128,5,4,128]{3,2,1,0:T(4,128)}, u32[]{:S(2)}, u32[]{:S(2)}) async-start(f32[128,5,4,128]{3,2,1,0:T(4,128)} %get-tuple-element.17), calls=%async_computation | async-start | bytes 2621440 | tf_op jit(solution)/shard_map/all_to_all | solution.py:508
  62.1 14.5 %copy-start = (f32[32,16,1024]{2,1,0:T(8,128)S(1)}, f32[32,16,1024]{2,1,0:T(8,128)}, u32[]{:S(2)}) copy-start(f32[32,16,1024]{2,1,0:T(8,128)} %get-tuple-element.20.force_ref) | copy-start | bytes 6291460
  62.1 31.4 %all-to-all-start.1 = ((f32[128,16,128]{2,1,0:T(8,128)}), f32[128,16,128]{2,1,0:T(8,128)S(1)}, u32[]{:S(2)}, u32[]{:S(2)}) async-start(f32[128,16,128]{2,1,0:T(8,128)} %bitcast.22), calls=%async_computation.1 | async-start | bytes 2097152 | tf_op jit(solution)/shard_map/all_to_all | solution.py:528
  76.6 0.9 copy-start.1
  77.5 0.9 copy-start.2
  78.4 0.8 copy-start.3
  79.2 0.8 copy-start.5
  80.0 0.9 copy-start.6
  80.9 0.9 copy-start.7
  81.8 11.8 %copy-start.4 = (s32[64,128]{1,0:T(8,128)S(1)}, s32[64,128]{1,0:T(8,128)}, u32[]{:S(2)}) copy-start(s32[64,128]{1,0:T(8,128)} %seg_ref.5) | copy-start | bytes 98308
  81.8 11.8 %copy-start.8 = (s32[2,2048]{1,0:T(2,128)S(1)}, s32[2,2048]{1,0:T(2,128)}, u32[]{:S(2)}) copy-start(s32[2,2048]{1,0:T(2,128)} %share_ref.3) | copy-start | bytes 49156
  81.8 11.8 %copy-start.9 = (s32[1,128,5]{1,2,0:T(8,128)S(1)}, s32[1,128,5]{1,2,0:T(8,128)}, u32[]{:S(2)}) copy-start(s32[1,128,5]{1,2,0:T(8,128)} %copy.20) | copy-start | bytes 7684
  96.8 6.4 %collective-permute-start = (f32[3,2048]{1,0:T(4,128)S(1)}, f32[3,2048]{1,0:T(4,128)S(1)}, u32[]{:S(2)}, u32[]{:S(2)}) collective-permute-start(f32[3,2048]{1,0:T(4,128)S(1)} %get-tuple-element.25), channel_id=1, source_target_pairs={{0,1},{1,2},{2,3},{3,4},{4,5},{5,6},{6,7},{7,8},{8,9},{9,10},{10,1... | collective-permute-start | bytes 73736 | tf_op jit(solution)/shard_map/ppermute | solution.py:484
  101.2 7.9 %collective-permute-start.1 = (f32[3,2048]{1,0:T(4,128)S(1)}, f32[3,2048]{1,0:T(4,128)S(1)}, u32[]{:S(2)}, u32[]{:S(2)}) collective-permute-start(f32[3,2048]{1,0:T(4,128)S(1)} %get-tuple-element.26), channel_id=1, source_target_pairs={{1,0},{2,1},{3,2},{4,3},{5,4},{6,5},{7,6},{8,7},{9,8},{10,9},{11,1... | collective-permute-start | bytes 73736 | tf_op jit(solution)/shard_map/ppermute | solution.py:484

commit v6 on v5

--- a/solution.py
+++ b/solution.py
@@ -109,7 +109,7 @@
 
     def send(d, carry):
         for c in range(cap):
-            out_ref[d, c] = own_ref[send_ref[c * peers + d]]
+            out_ref[d, c] = own_ref[send_ref[c, 0, d]]
         return carry
 
     lax.fori_loop(0, peers, send, 0, unroll=4)
@@ -251,19 +251,23 @@
             recoils[c, pl.ds(pl.multiple_of(s * 8, 8), 8), :] += recoil[c]
 
     def four(q, carry):
-        pair(4 * q, total_a)
-        pair(4 * q + 1, total_b)
-        pair(4 * q + 2, total_a)
-        pair(4 * q + 3, total_b)
+        pair(8 * q, total_a)
+        pair(8 * q + 1, total_b)
+        pair(8 * q + 2, total_a)
+        pair(8 * q + 3, total_b)
+        pair(8 * q + 4, total_a)
+        pair(8 * q + 5, total_b)
+        pair(8 * q + 6, total_a)
+        pair(8 * q + 7, total_b)
         return carry
 
     def one(p, carry):
         pair(p, total_a)
         return carry
 
-    whole = live >> 2
+    whole = live >> 3
     lax.fori_loop(0, whole, four, 0)
-    lax.fori_loop(4 * whole, live, one, 0)
+    lax.fori_loop(8 * whole, live, one, 0)
     peers = slots // cap
     stamp = jnp.broadcast_to(lim_ref[...], (8, seg))
 
@@ -283,7 +287,15 @@
     give_far.start()
 
     def close(b, carry):
-        for c in range(3):
+        total = total_a[b, 0] + total_b[b, 0]
+        summed = lax.dot_general(
+            jnp.ones((16, 3 * seg), bf16),
+            jnp.concatenate(pieces_of(total), 1),
+            (((1,), (1,)), ((), ())),
+            preferred_element_type=f32,
+        )
+        near[b, 0:1, :] = summed[0:1] * (1.0 / SCALE)
+        for c in (1, 2):
             total = total_a[b, c] + total_b[b, c]
             near[b, c : c + 1, :] = jnp.sum(total.T, 0, keepdims=True) * (1.0 / SCALE)
         return carry
@@ -305,7 +317,7 @@
     line = lax.broadcasted_iota(jnp.int32, (blocks, peers), 0)
     sums[...] = jnp.zeros_like(sums)
     for c in range(cap):
-        hot = jnp.where(line == send_ref[c : c + 1, :], 1.0, 0.0).astype(bf16)
+        hot = jnp.where(line == send_ref[c], 1.0, 0.0).astype(bf16)
         for k in range(3):
             force = back_ref[pl.ds(3 * c + k, peers, stride=16), :]
             found = jnp.dot(hot, jnp.concatenate(pieces_of(force), 1), preferred_element_type=f32)
@@ -383,7 +395,7 @@
     blocks, seg = seg_node.shape
     return pl.pallas_call(
         send_body,
-        out_shape=(struct(blocks, 4, seg), struct(peers, send.shape[0] // peers, 4, seg)),
+        out_shape=(struct(blocks, 4, seg), struct(peers, send.shape[0], 4, seg)),
         in_specs=smem(1) + vmem(4),
         out_specs=tuple(vmem(2)),
         scratch_shapes=[
@@ -503,8 +515,8 @@
 ):
     peers = lax.axis_size("grp") * lax.axis_size("dev")
     mass = node_mass.reshape(1, -1)
-    send = send_blk[0].T
-    own, outgoing = send_call(send.reshape(-1), displacement, ref_pos, seg_node, seg_mask, peers)
+    send = send_blk.transpose(2, 0, 1)
+    own, outgoing = send_call(send, displacement, ref_pos, seg_node, seg_mask, peers)
     arrived = lax.all_to_all(outgoing, ("grp", "dev"), split_axis=0, concat_axis=0, tiled=True)
     first = (lax.axis_index(("grp", "dev")) * part_stiff.shape[0]).reshape(1)
     force, limit = force_call(

time: 111 us -> 108 us (0.973)
  starting transfers between devices: 31.1 us -> 22.9 us
  Pallas kernels: 54.5 us -> 61.3 us
  local copies, waits for them, and re-layouts: 6.41 us -> 5.14 us
    all_to_all x1, starting transfers between devices: 14.5 us -> 6.22 us  [shards(): lax.all_to_all(far_force.reshape(peers, 16, -1), ('grp', 'dev'), split_ax...]
    pallas_call x1, Pallas kernels: 25.8 us -> 32.4 us  [contact_call(): pl.pallas_call(contact_body, out_shape=(struct(blocks, 3, seg), struct(pe...]
    unnamed x21 -> x20, local copies, waits for them, and re-layouts: 6.41 us -> 5.14 us
  transfers between devices with their start and end apart: 4 -> 4, of which waited for: 3 -> 3; matrix products, arithmetic and copies ran while one was open for 0% -> 0% of each run, Pallas kernels for 17% -> 18%
where the time goes in v6:
time: 108 us
  Pallas kernels  61.3 us (57%)
  starting transfers between devices  22.9 us (21%)
  waiting for transfers between devices  18 us (17%)
  local copies, waits for them, and re-layouts  5.14 us (5%)
    pallas_call x1, Pallas kernels, contact_call(): pl.pallas_call(contact_body, out_shape=(struct(blocks, 3, seg), struct(pe...  32.4 us
    pallas_call x1, Pallas kernels, force_call(): pl.pallas_call(force_body, out_shape=(struct(nodes.shape[1] // WIDTH, 16,...  10.9 us
    all_to_all x1, starting transfers between devices, shards(): lax.all_to_all(outgoing, ('grp', 'dev'), split_axis=0, concat_axis=0, til...  10.3 us
    all_to_all x1, waiting for transfers between devices, shards(): lax.all_to_all(outgoing, ('grp', 'dev'), split_axis=0, concat_axis=0, til...  8.59 us
    pallas_call x1, Pallas kernels, scatter_call(): pl.pallas_call(scatter_body, out_shape=(struct(3 * high, LOW), struct(3 *...  8.31 us
    ppermute x2, starting transfers between devices, shifted(): lax.ppermute(value, axis, [(source, source + steps) for source in range(f...  6.4 us
    all_to_all x1, starting transfers between devices, shards(): lax.all_to_all(far_force.reshape(peers, 16, -1), ('grp', 'dev'), split_ax...  6.22 us
    ppermute x2, waiting for transfers between devices, shifted(): lax.ppermute(value, axis, [(source, source + steps) for source in range(f...  5.98 us
  transfers between devices with their start and end apart: 4, of which 3 were waited for; matrix products, arithmetic and copies ran while one was open for 0% of the time, Pallas kernels for 18%

profile of v6, /device:TPU:96, one launch (start us, length us, event | category | flops | bytes accessed | tf_op | source)
XLA Modules:
  0.0 108.0 jit_solution(7215557898188616509)
XLA Ops:
  0.6 4.9 %shard_map.158 = (f32[64,4,128]{2,1,0:T(4,128)}, f32[128,5,4,128]{3,2,1,0:T(4,128)}) custom-call(s32[5,1,128]{2,1,0:T(1,128)} %bitcast.12, f32[3,8192]{1,0:T(4,128)} %disp_ref.5, f32[3,8192]{1,0:T(4,128)} %ref_ref.1, s32[64,128]{1,0:T(8,128)} %seg_ref.5, s32[64,128]{1,0:T(8,128)} %mask_ref.1), custom_call_target="tpu_custom_call" | custom-call | tf_op jit(solution)/shard_map/pallas_call | solution.py:396
  5.5 10.3 %all-to-all-start = ((f32[128,5,4,128]{3,2,1,0:T(4,128)}), f32[128,5,4,128]{3,2,1,0:T(4,128)}, u32[]{:S(2)}, u32[]{:S(2)}) async-start(f32[128,5,4,128]{3,2,1,0:T(4,128)} %get-tuple-element.17), calls=%async_computation | async-start | bytes 2621440 | tf_op jit(solution)/shard_map/all_to_all | solution.py:520
  15.8 10.9 %shard_map.159 = (f32[32,16,1024]{2,1,0:T(8,128)}, f32[1,128]{1,0:T(1,128)}) custom-call(s32[1]{0:T(128)} %bitcast.3.first_ref, f32[4]{0:T(128)} %stiff_ref.1, f32[3,8192]{1,0:T(4,128)} %disp_ref.5, f32[1,8192]{1,0:T(1,128)} %bitcast.10, s32[4,8192]{1,0:T(4,128)} %nodes_ref.3, s32[1,8192]{1,0:T(1,128)} %bitcast.15, f32[1,8192]{1,0:T(1,128)} %bitcast.16), custom_call_target="tpu_custom_call" | custom-call | tf_op jit(solution)/shard_map/pallas_call | solution.py:410
  26.7 8.6 %all-to-all-done = f32[128,5,4,128]{3,2,1,0:T(4,128)} async-done(((f32[128,5,4,128]{3,2,1,0:T(4,128)}), f32[128,5,4,128]{3,2,1,0:T(4,128)}, u32[]{:S(2)}, u32[]{:S(2)}) %all-to-all-start) | async-done | bytes 1310752 | tf_op jit(solution)/shard_map/all_to_all | solution.py:520
  35.3 32.4 %shard_map.160 = (f32[64,3,128]{2,1,0:T(4,128)}, f32[2048,128]{1,0:T(8,128)}) custom-call(s32[512]{0:T(512)} %near_ref.1, s32[512]{0:T(512)} %far_ref.1, f32[64,4,128]{2,1,0:T(4,128)} %get-tuple-element.16.own_ref, f32[640,4,128]{2,1,0:T(4,128)} %bitcast.1.recv_ref, s32[4,128]{1,0:T(4,128)} %bitcast.17, f32[1,128]{1,0:T(1,128)} %get-tuple-element.18.lim_ref), custom_call_target="tpu_custom_call" | custom-call | tf_op jit(solution)/shard_map/pallas_call | solution.py:441
  67.7 0.0 copy-start
  67.7 6.2 %all-to-all-start.1 = ((f32[128,16,128]{2,1,0:T(8,128)}), f32[128,16,128]{2,1,0:T(8,128)S(1)}, u32[]{:S(2)}, u32[]{:S(2)}) async-start(f32[128,16,128]{2,1,0:T(8,128)} %bitcast.14), calls=%async_computation.1 | async-start | bytes 2097152 | tf_op jit(solution)/shard_map/all_to_all | solution.py:540
  73.9 0.0 copy-done
  73.9 0.0 copy-start.1
  73.9 0.9 copy-done.1
  74.8 0.0 copy-start.2
  74.8 0.9 copy-done.2
  75.7 0.0 copy-start.3
  75.7 0.8 copy-done.3
  76.5 0.0 copy-start.5
  76.5 0.8 copy-done.5
  77.2 0.9 copy-done.6
  78.1 0.0 copy-start.7
  78.1 0.9 copy-done.7
  79.1 0.0 copy-start.4
  79.1 0.0 copy-start.8
  79.1 8.3 %shard_map.161 = (f32[96,256]{1,0:T(8,128)S(1)}, f32[96,256]{1,0:T(8,128)S(1)}, f32[96,256]{1,0:T(8,128)S(1)}, f32[32,256]{1,0:T(8,128)S(1)}) custom-call(s32[4,8192]{1,0:T(4,128)S(1)} %copy-done.2, f32[32,16,1024]{2,1,0:T(8,128)S(1)} %copy-done, s32[64,128]{1,0:T(8,128)S(1)} %copy-done.3, f32[64,3,128]{2,1,0:T(4,128)S(1)} %copy-done.7, ...), custom_call_target="tpu_custom_call" | custom-call | tf_op jit(solution)/shard_map/pallas_call | solution.py:425
  87.4 3.5 %all-to-all-done.1 = f32[128,16,128]{2,1,0:T(8,128)S(1)} async-done(((f32[128,16,128]{2,1,0:T(8,128)}), f32[128,16,128]{2,1,0:T(8,128)S(1)}, u32[]{:S(2)}, u32[]{:S(2)}) %all-to-all-start.1) | async-done | bytes 1048608 | tf_op jit(solution)/shard_map/all_to_all | solution.py:540
  90.8 0.0 copy-done.4
  90.8 0.0 copy-done.8
  90.8 0.0 copy-done.9
  90.8 3.2 %shard_map.162 = (f32[96,256]{1,0:T(8,128)S(1)}, f32[3,2048]{1,0:T(4,128)S(1)}, f32[3,2048]{1,0:T(4,128)S(1)}, f32[1,128]{1,0:T(1,128)S(1)}) custom-call(s32[5,1,128]{2,1,0:T(1,128)S(1)} %bitcast.13, f32[2048,128]{1,0:T(8,128)S(1)} %bitcast.9, s32[64,128]{1,0:T(8,128)S(1)} %copy-done.4, f32[96,256]{1,0:T(8,128)S(1)} %get-tuple-element.22.int_ref, ...), custom_call_target="tpu_custom_call" | custom-call | tf_op jit(solution)/shard_map/pallas_call | solution.py:465
  94.0 4.5 %collective-permute-start = (f32[3,2048]{1,0:T(4,128)S(1)}, f32[3,2048]{1,0:T(4,128)S(1)}, u32[]{:S(2)}, u32[]{:S(2)}) collective-permute-start(f32[3,2048]{1,0:T(4,128)S(1)} %get-tuple-element.25), channel_id=1, source_target_pairs={{0,1},{1,2},{2,3},{3,4},{4,5},{5,6},{6,7},{7,8},{8,9},{9,10},{10,1... | collective-permute-start | bytes 73736 | tf_op jit(solution)/shard_map/ppermute | solution.py:496
  98.5 1.9 %collective-permute-start.1 = (f32[3,2048]{1,0:T(4,128)S(1)}, f32[3,2048]{1,0:T(4,128)S(1)}, u32[]{:S(2)}, u32[]{:S(2)}) collective-permute-start(f32[3,2048]{1,0:T(4,128)S(1)} %get-tuple-element.26), channel_id=1, source_target_pairs={{1,0},{2,1},{3,2},{4,3},{5,4},{6,5},{7,6},{8,7},{9,8},{10,9},{11,1... | collective-permute-start | bytes 73736 | tf_op jit(solution)/shard_map/ppermute | solution.py:496
  100.5 0.0 collective-permute-done.low_ref
  100.5 6.0 %collective-permute-done.1.up_ref = f32[3,2048]{1,0:T(4,128)S(1)} collective-permute-done((f32[3,2048]{1,0:T(4,128)S(1)}, f32[3,2048]{1,0:T(4,128)S(1)}, u32[]{:S(2)}, u32[]{:S(2)}) %collective-permute-start.1) | collective-permute-done | bytes 24608 | tf_op jit(solution)/shard_map/ppermute | solution.py:496
  106.4 1.6 %shard_map.163 = (f32[3,8192]{1,0:T(4,128)}, f32[3,8192]{1,0:T(4,128)}) custom-call(f32[1,128]{1,0:T(1,128)S(1)} %get-tuple-element.23.lim_ref, f32[96,256]{1,0:T(8,128)S(1)} %get-tuple-element.24.tot_ref, s32[2,2048]{1,0:T(2,128)S(1)} %copy-done.8, f32[3,2048]{1,0:T(4,128)S(1)} %collective-permute-done.low_ref, ...), custom_call_target="tpu_custom_call" | custom-call | tf_op jit(solution)/shard_map/pallas_call | solution.py:483
  (2 shorter events, 0.0 us)
Async XLA Ops:
  5.5 29.8 %all-to-all-start = ((f32[128,5,4,128]{3,2,1,0:T(4,128)}), f32[128,5,4,128]{3,2,1,0:T(4,128)}, u32[]{:S(2)}, u32[]{:S(2)}) async-start(f32[128,5,4,128]{3,2,1,0:T(4,128)} %get-tuple-element.17), calls=%async_computation | async-start | bytes 2621440 | tf_op jit(solution)/shard_map/all_to_all | solution.py:520
  67.7 6.2 %copy-start = (f32[32,16,1024]{2,1,0:T(8,128)S(1)}, f32[32,16,1024]{2,1,0:T(8,128)}, u32[]{:S(2)}) copy-start(f32[32,16,1024]{2,1,0:T(8,128)} %get-tuple-element.20.force_ref) | copy-start | bytes 6291460
  67.7 23.1 %all-to-all-start.1 = ((f32[128,16,128]{2,1,0:T(8,128)}), f32[128,16,128]{2,1,0:T(8,128)S(1)}, u32[]{:S(2)}, u32[]{:S(2)}) async-start(f32[128,16,128]{2,1,0:T(8,128)} %bitcast.14), calls=%async_computation.1 | async-start | bytes 2097152 | tf_op jit(solution)/shard_map/all_to_all | solution.py:540
  73.9 0.9 copy-start.1
  74.8 0.9 copy-start.2
  75.7 0.8 copy-start.3
  76.5 0.8 copy-start.5
  77.2 0.9 copy-start.6
  78.1 0.9 copy-start.7
  79.1 11.8 %copy-start.4 = (s32[64,128]{1,0:T(8,128)S(1)}, s32[64,128]{1,0:T(8,128)}, u32[]{:S(2)}) copy-start(s32[64,128]{1,0:T(8,128)} %seg_ref.5) | copy-start | bytes 98308
  79.1 11.8 %copy-start.8 = (s32[2,2048]{1,0:T(2,128)S(1)}, s32[2,2048]{1,0:T(2,128)}, u32[]{:S(2)}) copy-start(s32[2,2048]{1,0:T(2,128)} %share_ref.3) | copy-start | bytes 49156
  79.1 11.8 %copy-start.9 = (s32[1,128,5]{1,0,2:T(1,128)S(1)}, s32[1,128,5]{1,0,2:T(1,128)}, u32[]{:S(2)}) copy-start(s32[1,128,5]{1,0,2:T(1,128)} %param.26) | copy-start | bytes 7684
  94.0 6.4 %collective-permute-start = (f32[3,2048]{1,0:T(4,128)S(1)}, f32[3,2048]{1,0:T(4,128)S(1)}, u32[]{:S(2)}, u32[]{:S(2)}) collective-permute-start(f32[3,2048]{1,0:T(4,128)S(1)} %get-tuple-element.25), channel_id=1, source_target_pairs={{0,1},{1,2},{2,3},{3,4},{4,5},{5,6},{6,7},{7,8},{8,9},{9,10},{10,1... | collective-permute-start | bytes 73736 | tf_op jit(solution)/shard_map/ppermute | solution.py:496
  98.5 7.9 %collective-permute-start.1 = (f32[3,2048]{1,0:T(4,128)S(1)}, f32[3,2048]{1,0:T(4,128)S(1)}, u32[]{:S(2)}, u32[]{:S(2)}) collective-permute-start(f32[3,2048]{1,0:T(4,128)S(1)} %get-tuple-element.26), channel_id=1, source_target_pairs={{1,0},{2,1},{3,2},{4,3},{5,4},{6,5},{7,6},{8,7},{9,8},{10,9},{11,1... | collective-permute-start | bytes 73736 | tf_op jit(solution)/shard_map/ppermute | solution.py:496

commit v7 on v6

--- a/solution.py
+++ b/solution.py
@@ -202,12 +202,13 @@
     fetch.start()
 
     group = 8
-    line = lax.broadcasted_iota(jnp.int32, (seg, 3 * seg), 0)
-    part = lax.broadcasted_iota(jnp.int32, (seg, 3 * seg), 1) >> 7
+    line = lax.broadcasted_iota(jnp.int32, (16, 3 * seg), 0)
+    part = lax.broadcasted_iota(jnp.int32, (16, 3 * seg), 1) >> 7
+    hit = (line == part) | (line == part + 3) | (line == part + 6)
+    hit = jnp.where(hit, 1.0, 0.0).astype(bf16)
+    chosen[...] = jnp.zeros_like(chosen)
     for k in range(group):
-        at = line - 16 * k
-        hit = (at == part) | (at == part + 3) | (at == part + 6)
-        chosen[k] = jnp.where(hit, 1.0, 0.0).astype(bf16)
+        chosen[k, 16 * k : 16 * k + 16, :] = hit
     rows[...] = jnp.zeros_like(rows)
 
     def widen(g, carry):
@@ -300,7 +301,7 @@
             near[b, c : c + 1, :] = jnp.sum(total.T, 0, keepdims=True) * (1.0 / SCALE)
         return carry
 
-    lax.fori_loop(0, blocks, close, 0, unroll=8)
+    lax.fori_loop(0, blocks, close, 0, unroll=16)
     give_near = pltpu.make_async_copy(near, own_out, sems.at[2])
     give_near.start()
     give_far.wait()
@@ -315,13 +316,15 @@
     cap = 5
     high = int_ref.shape[0] // 3
     line = lax.broadcasted_iota(jnp.int32, (blocks, peers), 0)
-    sums[...] = jnp.zeros_like(sums)
-    for c in range(cap):
-        hot = jnp.where(line == send_ref[c], 1.0, 0.0).astype(bf16)
-        for k in range(3):
-            force = back_ref[pl.ds(3 * c + k, peers, stride=16), :]
-            found = jnp.dot(hot, jnp.concatenate(pieces_of(force), 1), preferred_element_type=f32)
-            sums[k] += (found[:, 256:] + found[:, 128:256]) + found[:, :128]
+    hot = jnp.concatenate(
+        [jnp.where(line == send_ref[c], 1.0, 0.0).astype(bf16) for c in range(cap)], 1
+    )
+    for k in range(3):
+        force = jnp.concatenate(
+            [back_ref[pl.ds(3 * c + k, peers, stride=16), :] for c in range(cap)], 0
+        )
+        found = jnp.dot(hot, jnp.concatenate(pieces_of(force), 1), preferred_element_type=f32)
+        sums[k] = (found[:, 256:] + found[:, 128:256]) + found[:, :128]
     acc[...] = jnp.zeros_like(acc)
     group = 8
 

time: 108 us -> 107 us (level)
  Pallas kernels: 61.3 us -> 50.8 us
  starting transfers between devices: 22.9 us -> 31.7 us
    pallas_call x1, Pallas kernels: 32.4 us -> 22.1 us  [contact_call(): pl.pallas_call(contact_body, out_shape=(struct(blocks, 3, seg), struct(pe...]
    all_to_all x1, starting transfers between devices: 6.22 us -> 15.1 us  [shards(): lax.all_to_all(far_force.reshape(peers, 16, -1), ('grp', 'dev'), split_ax...]
where the time goes in v7:
time: 107 us; the launch traced here: 106 us
  Pallas kernels  50.8 us (47%)
  starting transfers between devices  31.7 us (30%)
  waiting for transfers between devices  18 us (17%)
  local copies, waits for them, and re-layouts  5.14 us (5%)
    pallas_call x1, Pallas kernels, contact_call(): pl.pallas_call(contact_body, out_shape=(struct(blocks, 3, seg), struct(pe...  22.1 us
    all_to_all x1, starting transfers between devices, shards(): lax.all_to_all(far_force.reshape(peers, 16, -1), ('grp', 'dev'), split_ax...  15.1 us
    pallas_call x1, Pallas kernels, force_call(): pl.pallas_call(force_body, out_shape=(struct(nodes.shape[1] // WIDTH, 16,...  10.9 us
    all_to_all x1, starting transfers between devices, shards(): lax.all_to_all(outgoing, ('grp', 'dev'), split_axis=0, concat_axis=0, til...  10.3 us
    all_to_all x1, waiting for transfers between devices, shards(): lax.all_to_all(outgoing, ('grp', 'dev'), split_axis=0, concat_axis=0, til...  8.59 us
    pallas_call x1, Pallas kernels, scatter_call(): pl.pallas_call(scatter_body, out_shape=(struct(3 * high, LOW), struct(3 *...  8.31 us
    ppermute x2, starting transfers between devices, shifted(): lax.ppermute(value, axis, [(source, source + steps) for source in range(f...  6.4 us
    ppermute x2, waiting for transfers between devices, shifted(): lax.ppermute(value, axis, [(source, source + steps) for source in range(f...  5.98 us
  transfers between devices with their start and end apart: 4, of which 3 were waited for; matrix products, arithmetic and copies ran while one was open for 0% of the time, Pallas kernels for 18%

profile of v7, /device:TPU:96, one launch (start us, length us, event | category | flops | bytes accessed | tf_op | source)
XLA Modules:
  0.0 106.4 jit_solution(8547644477564883271)
XLA Ops:
  0.6 4.9 %shard_map.158 = (f32[64,4,128]{2,1,0:T(4,128)}, f32[128,5,4,128]{3,2,1,0:T(4,128)}) custom-call(s32[5,1,128]{2,1,0:T(1,128)} %bitcast.12, f32[3,8192]{1,0:T(4,128)} %disp_ref.5, f32[3,8192]{1,0:T(4,128)} %ref_ref.1, s32[64,128]{1,0:T(8,128)} %seg_ref.5, s32[64,128]{1,0:T(8,128)} %mask_ref.1), custom_call_target="tpu_custom_call" | custom-call | tf_op jit(solution)/shard_map/pallas_call | solution.py:399
  5.5 10.3 %all-to-all-start = ((f32[128,5,4,128]{3,2,1,0:T(4,128)}), f32[128,5,4,128]{3,2,1,0:T(4,128)}, u32[]{:S(2)}, u32[]{:S(2)}) async-start(f32[128,5,4,128]{3,2,1,0:T(4,128)} %get-tuple-element.17), calls=%async_computation | async-start | bytes 2621440 | tf_op jit(solution)/shard_map/all_to_all | solution.py:523
  15.8 10.9 %shard_map.159 = (f32[32,16,1024]{2,1,0:T(8,128)}, f32[1,128]{1,0:T(1,128)}) custom-call(s32[1]{0:T(128)} %bitcast.3.first_ref, f32[4]{0:T(128)} %stiff_ref.1, f32[3,8192]{1,0:T(4,128)} %disp_ref.5, f32[1,8192]{1,0:T(1,128)} %bitcast.10, s32[4,8192]{1,0:T(4,128)} %nodes_ref.3, s32[1,8192]{1,0:T(1,128)} %bitcast.15, f32[1,8192]{1,0:T(1,128)} %bitcast.16), custom_call_target="tpu_custom_call" | custom-call | tf_op jit(solution)/shard_map/pallas_call | solution.py:413
  26.7 8.6 %all-to-all-done = f32[128,5,4,128]{3,2,1,0:T(4,128)} async-done(((f32[128,5,4,128]{3,2,1,0:T(4,128)}), f32[128,5,4,128]{3,2,1,0:T(4,128)}, u32[]{:S(2)}, u32[]{:S(2)}) %all-to-all-start) | async-done | bytes 1310752 | tf_op jit(solution)/shard_map/all_to_all | solution.py:523
  35.3 22.1 %shard_map.160 = (f32[64,3,128]{2,1,0:T(4,128)}, f32[2048,128]{1,0:T(8,128)}) custom-call(s32[512]{0:T(512)} %near_ref.1, s32[512]{0:T(512)} %far_ref.1, f32[64,4,128]{2,1,0:T(4,128)} %get-tuple-element.16.own_ref, f32[640,4,128]{2,1,0:T(4,128)} %bitcast.1.recv_ref, s32[4,128]{1,0:T(4,128)} %bitcast.17, f32[1,128]{1,0:T(1,128)} %get-tuple-element.18.lim_ref), custom_call_target="tpu_custom_call" | custom-call | tf_op jit(solution)/shard_map/pallas_call | solution.py:444
  57.4 0.0 copy-start
  57.4 15.1 %all-to-all-start.1 = ((f32[128,16,128]{2,1,0:T(8,128)}), f32[128,16,128]{2,1,0:T(8,128)S(1)}, u32[]{:S(2)}, u32[]{:S(2)}) async-start(f32[128,16,128]{2,1,0:T(8,128)} %bitcast.14), calls=%async_computation.1 | async-start | bytes 2097152 | tf_op jit(solution)/shard_map/all_to_all | solution.py:543
  72.5 0.0 copy-done
  72.5 0.0 copy-start.1
  72.5 0.9 copy-done.1
  73.4 0.0 copy-start.2
  73.4 0.9 copy-done.2
  74.3 0.0 copy-start.3
  74.3 0.8 copy-done.3
  75.1 0.0 copy-start.5
  75.1 0.8 copy-done.5
  75.8 0.9 copy-done.6
  76.7 0.0 copy-start.7
  76.7 0.9 copy-done.7
  77.6 0.0 copy-start.4
  77.6 0.0 copy-start.8
  77.6 8.3 %shard_map.161 = (f32[96,256]{1,0:T(8,128)S(1)}, f32[96,256]{1,0:T(8,128)S(1)}, f32[96,256]{1,0:T(8,128)S(1)}, f32[32,256]{1,0:T(8,128)S(1)}) custom-call(s32[4,8192]{1,0:T(4,128)S(1)} %copy-done.2, f32[32,16,1024]{2,1,0:T(8,128)S(1)} %copy-done, s32[64,128]{1,0:T(8,128)S(1)} %copy-done.3, f32[64,3,128]{2,1,0:T(4,128)S(1)} %copy-done.7, ...), custom_call_target="tpu_custom_call" | custom-call | tf_op jit(solution)/shard_map/pallas_call | solution.py:428
  86.0 3.5 %all-to-all-done.1 = f32[128,16,128]{2,1,0:T(8,128)S(1)} async-done(((f32[128,16,128]{2,1,0:T(8,128)}), f32[128,16,128]{2,1,0:T(8,128)S(1)}, u32[]{:S(2)}, u32[]{:S(2)}) %all-to-all-start.1) | async-done | bytes 1048608 | tf_op jit(solution)/shard_map/all_to_all | solution.py:543
  89.4 0.0 copy-done.4
  89.4 0.0 copy-done.8
  89.4 0.0 copy-done.9
  89.4 3.0 %shard_map.162 = (f32[96,256]{1,0:T(8,128)S(1)}, f32[3,2048]{1,0:T(4,128)S(1)}, f32[3,2048]{1,0:T(4,128)S(1)}, f32[1,128]{1,0:T(1,128)S(1)}) custom-call(s32[5,1,128]{2,1,0:T(1,128)S(1)} %bitcast.13, f32[2048,128]{1,0:T(8,128)S(1)} %bitcast.9, s32[64,128]{1,0:T(8,128)S(1)} %copy-done.4, f32[96,256]{1,0:T(8,128)S(1)} %get-tuple-element.22.int_ref, ...), custom_call_target="tpu_custom_call" | custom-call | tf_op jit(solution)/shard_map/pallas_call | solution.py:468
  92.5 4.5 %collective-permute-start = (f32[3,2048]{1,0:T(4,128)S(1)}, f32[3,2048]{1,0:T(4,128)S(1)}, u32[]{:S(2)}, u32[]{:S(2)}) collective-permute-start(f32[3,2048]{1,0:T(4,128)S(1)} %get-tuple-element.25), channel_id=1, source_target_pairs={{0,1},{1,2},{2,3},{3,4},{4,5},{5,6},{6,7},{7,8},{8,9},{9,10},{10,1... | collective-permute-start | bytes 73736 | tf_op jit(solution)/shard_map/ppermute | solution.py:499
  96.9 1.9 %collective-permute-start.1 = (f32[3,2048]{1,0:T(4,128)S(1)}, f32[3,2048]{1,0:T(4,128)S(1)}, u32[]{:S(2)}, u32[]{:S(2)}) collective-permute-start(f32[3,2048]{1,0:T(4,128)S(1)} %get-tuple-element.26), channel_id=1, source_target_pairs={{1,0},{2,1},{3,2},{4,3},{5,4},{6,5},{7,6},{8,7},{9,8},{10,9},{11,1... | collective-permute-start | bytes 73736 | tf_op jit(solution)/shard_map/ppermute | solution.py:499
  98.9 0.0 collective-permute-done.low_ref
  98.9 6.0 %collective-permute-done.1.up_ref = f32[3,2048]{1,0:T(4,128)S(1)} collective-permute-done((f32[3,2048]{1,0:T(4,128)S(1)}, f32[3,2048]{1,0:T(4,128)S(1)}, u32[]{:S(2)}, u32[]{:S(2)}) %collective-permute-start.1) | collective-permute-done | bytes 24608 | tf_op jit(solution)/shard_map/ppermute | solution.py:499
  104.9 1.6 %shard_map.163 = (f32[3,8192]{1,0:T(4,128)}, f32[3,8192]{1,0:T(4,128)}) custom-call(f32[1,128]{1,0:T(1,128)S(1)} %get-tuple-element.23.lim_ref, f32[96,256]{1,0:T(8,128)S(1)} %get-tuple-element.24.tot_ref, s32[2,2048]{1,0:T(2,128)S(1)} %copy-done.8, f32[3,2048]{1,0:T(4,128)S(1)} %collective-permute-done.low_ref, ...), custom_call_target="tpu_custom_call" | custom-call | tf_op jit(solution)/shard_map/pallas_call | solution.py:486
  (2 shorter events, 0.0 us)
Async XLA Ops:
  5.5 29.8 %all-to-all-start = ((f32[128,5,4,128]{3,2,1,0:T(4,128)}), f32[128,5,4,128]{3,2,1,0:T(4,128)}, u32[]{:S(2)}, u32[]{:S(2)}) async-start(f32[128,5,4,128]{3,2,1,0:T(4,128)} %get-tuple-element.17), calls=%async_computation | async-start | bytes 2621440 | tf_op jit(solution)/shard_map/all_to_all | solution.py:523
  57.4 15.1 %copy-start = (f32[32,16,1024]{2,1,0:T(8,128)S(1)}, f32[32,16,1024]{2,1,0:T(8,128)}, u32[]{:S(2)}) copy-start(f32[32,16,1024]{2,1,0:T(8,128)} %get-tuple-element.20.force_ref) | copy-start | bytes 6291460
  57.4 32.0 %all-to-all-start.1 = ((f32[128,16,128]{2,1,0:T(8,128)}), f32[128,16,128]{2,1,0:T(8,128)S(1)}, u32[]{:S(2)}, u32[]{:S(2)}) async-start(f32[128,16,128]{2,1,0:T(8,128)} %bitcast.14), calls=%async_computation.1 | async-start | bytes 2097152 | tf_op jit(solution)/shard_map/all_to_all | solution.py:543
  72.5 0.9 copy-start.1
  73.4 0.9 copy-start.2
  74.3 0.8 copy-start.3
  75.1 0.8 copy-start.5
  75.8 0.9 copy-start.6
  76.7 0.9 copy-start.7
  77.6 11.8 %copy-start.4 = (s32[64,128]{1,0:T(8,128)S(1)}, s32[64,128]{1,0:T(8,128)}, u32[]{:S(2)}) copy-start(s32[64,128]{1,0:T(8,128)} %seg_ref.5) | copy-start | bytes 98308
  77.6 11.8 %copy-start.8 = (s32[2,2048]{1,0:T(2,128)S(1)}, s32[2,2048]{1,0:T(2,128)}, u32[]{:S(2)}) copy-start(s32[2,2048]{1,0:T(2,128)} %share_ref.3) | copy-start | bytes 49156
  77.6 11.8 %copy-start.9 = (s32[1,128,5]{1,0,2:T(1,128)S(1)}, s32[1,128,5]{1,0,2:T(1,128)}, u32[]{:S(2)}) copy-start(s32[1,128,5]{1,0,2:T(1,128)} %param.26) | copy-start | bytes 7684
  92.5 6.4 %collective-permute-start = (f32[3,2048]{1,0:T(4,128)S(1)}, f32[3,2048]{1,0:T(4,128)S(1)}, u32[]{:S(2)}, u32[]{:S(2)}) collective-permute-start(f32[3,2048]{1,0:T(4,128)S(1)} %get-tuple-element.25), channel_id=1, source_target_pairs={{0,1},{1,2},{2,3},{3,4},{4,5},{5,6},{6,7},{7,8},{8,9},{9,10},{10,1... | collective-permute-start | bytes 73736 | tf_op jit(solution)/shard_map/ppermute | solution.py:499
  96.9 7.9 %collective-permute-start.1 = (f32[3,2048]{1,0:T(4,128)S(1)}, f32[3,2048]{1,0:T(4,128)S(1)}, u32[]{:S(2)}, u32[]{:S(2)}) collective-permute-start(f32[3,2048]{1,0:T(4,128)S(1)} %get-tuple-element.26), channel_id=1, source_target_pairs={{1,0},{2,1},{3,2},{4,3},{5,4},{6,5},{7,6},{8,7},{9,8},{10,9},{11,1... | collective-permute-start | bytes 73736 | tf_op jit(solution)/shard_map/ppermute | solution.py:499

commit v8 on v7

--- a/solution.py
+++ b/solution.py
@@ -104,7 +104,7 @@
             own_ref[base + k, 3:4, :] = weight[k : k + 1]
         return carry
 
-    lax.fori_loop(0, blocks // group, some, 0, unroll=4)
+    lax.fori_loop(0, blocks // group, some, 0, unroll=8)
     peers, cap = out_ref.shape[0], out_ref.shape[1]
 
     def send(d, carry):
@@ -112,7 +112,7 @@
             out_ref[d, c] = own_ref[send_ref[c, 0, d]]
         return carry
 
-    lax.fori_loop(0, peers, send, 0, unroll=4)
+    lax.fori_loop(0, peers, send, 0, unroll=8)
 
 
 def force_body(
@@ -338,7 +338,7 @@
         acc[...] += add_hot(spread(rows, idx, high), low_hot(idx))
         return carry
 
-    lax.fori_loop(0, blocks // group, some, 0, unroll=4)
+    lax.fori_loop(0, blocks // group, some, 0, unroll=8)
     size = 3 * high
     tot_ref[...] = ((acc[2 * size :] + acc[size : 2 * size]) + acc[:size]) + int_ref[...]
     split_table(cut, tot_ref)

time: 107 us -> 108 us (level)
  Pallas kernels: 50.8 us -> 59.9 us
  starting transfers between devices: 31.7 us -> 23 us
    all_to_all x1, starting transfers between devices: 15.1 us -> 6.39 us  [shards(): lax.all_to_all(far_force.reshape(peers, 16, -1), ('grp', 'dev'), split_ax...]
    pallas_call x1, Pallas kernels: 22.1 us -> 30.5 us  [contact_call(): pl.pallas_call(contact_body, out_shape=(struct(blocks, 3, seg), struct(pe...]
where the time goes in v8:
time: 108 us; the launch traced here: 107 us
  Pallas kernels  59.9 us (55%)
  starting transfers between devices  23 us (21%)
  waiting for transfers between devices  18 us (17%)
  local copies, waits for them, and re-layouts  5.14 us (5%)
    pallas_call x1, Pallas kernels, contact_call(): pl.pallas_call(contact_body, out_shape=(struct(blocks, 3, seg), struct(pe...  30.5 us
    pallas_call x1, Pallas kernels, force_call(): pl.pallas_call(force_body, out_shape=(struct(nodes.shape[1] // WIDTH, 16,...  10.9 us
    all_to_all x1, starting transfers between devices, shards(): lax.all_to_all(outgoing, ('grp', 'dev'), split_axis=0, concat_axis=0, til...  10.3 us
    all_to_all x1, waiting for transfers between devices, shards(): lax.all_to_all(outgoing, ('grp', 'dev'), split_axis=0, concat_axis=0, til...  8.59 us
    pallas_call x1, Pallas kernels, scatter_call(): pl.pallas_call(scatter_body, out_shape=(struct(3 * high, LOW), struct(3 *...  8.31 us
    ppermute x2, starting transfers between devices, shifted(): lax.ppermute(value, axis, [(source, source + steps) for source in range(f...  6.39 us
    all_to_all x1, starting transfers between devices, shards(): lax.all_to_all(far_force.reshape(peers, 16, -1), ('grp', 'dev'), split_ax...  6.39 us
    ppermute x2, waiting for transfers between devices, shifted(): lax.ppermute(value, axis, [(source, source + steps) for source in range(f...  5.98 us
  transfers between devices with their start and end apart: 4, of which 3 were waited for; matrix products, arithmetic and copies ran while one was open for 0% of the time, Pallas kernels for 18%

profile of v8, /device:TPU:96, one launch (start us, length us, event | category | flops | bytes accessed | tf_op | source)
XLA Modules:
  0.0 106.8 jit_solution(8131808153993083834)
XLA Ops:
  0.6 4.6 %shard_map.158 = (f32[64,4,128]{2,1,0:T(4,128)}, f32[128,5,4,128]{3,2,1,0:T(4,128)}) custom-call(s32[5,1,128]{2,1,0:T(1,128)} %bitcast.12, f32[3,8192]{1,0:T(4,128)} %disp_ref.5, f32[3,8192]{1,0:T(4,128)} %ref_ref.1, s32[64,128]{1,0:T(8,128)} %seg_ref.5, s32[64,128]{1,0:T(8,128)} %mask_ref.1), custom_call_target="tpu_custom_call" | custom-call | tf_op jit(solution)/shard_map/pallas_call | solution.py:399
  5.2 10.3 %all-to-all-start = ((f32[128,5,4,128]{3,2,1,0:T(4,128)}), f32[128,5,4,128]{3,2,1,0:T(4,128)}, u32[]{:S(2)}, u32[]{:S(2)}) async-start(f32[128,5,4,128]{3,2,1,0:T(4,128)} %get-tuple-element.17), calls=%async_computation | async-start | bytes 2621440 | tf_op jit(solution)/shard_map/all_to_all | solution.py:523
  15.5 10.9 %shard_map.159 = (f32[32,16,1024]{2,1,0:T(8,128)}, f32[1,128]{1,0:T(1,128)}) custom-call(s32[1]{0:T(128)} %bitcast.3.first_ref, f32[4]{0:T(128)} %stiff_ref.1, f32[3,8192]{1,0:T(4,128)} %disp_ref.5, f32[1,8192]{1,0:T(1,128)} %bitcast.10, s32[4,8192]{1,0:T(4,128)} %nodes_ref.3, s32[1,8192]{1,0:T(1,128)} %bitcast.15, f32[1,8192]{1,0:T(1,128)} %bitcast.16), custom_call_target="tpu_custom_call" | custom-call | tf_op jit(solution)/shard_map/pallas_call | solution.py:413
  26.4 8.6 %all-to-all-done = f32[128,5,4,128]{3,2,1,0:T(4,128)} async-done(((f32[128,5,4,128]{3,2,1,0:T(4,128)}), f32[128,5,4,128]{3,2,1,0:T(4,128)}, u32[]{:S(2)}, u32[]{:S(2)}) %all-to-all-start) | async-done | bytes 1310752 | tf_op jit(solution)/shard_map/all_to_all | solution.py:523
  35.0 30.5 %shard_map.160 = (f32[64,3,128]{2,1,0:T(4,128)}, f32[2048,128]{1,0:T(8,128)}) custom-call(s32[512]{0:T(512)} %near_ref.1, s32[512]{0:T(512)} %far_ref.1, f32[64,4,128]{2,1,0:T(4,128)} %get-tuple-element.16.own_ref, f32[640,4,128]{2,1,0:T(4,128)} %bitcast.1.recv_ref, s32[4,128]{1,0:T(4,128)} %bitcast.17, f32[1,128]{1,0:T(1,128)} %get-tuple-element.18.lim_ref), custom_call_target="tpu_custom_call" | custom-call | tf_op jit(solution)/shard_map/pallas_call | solution.py:444
  65.5 0.0 copy-start
  65.5 6.4 %all-to-all-start.1 = ((f32[128,16,128]{2,1,0:T(8,128)}), f32[128,16,128]{2,1,0:T(8,128)S(1)}, u32[]{:S(2)}, u32[]{:S(2)}) async-start(f32[128,16,128]{2,1,0:T(8,128)} %bitcast.14), calls=%async_computation.1 | async-start | bytes 2097152 | tf_op jit(solution)/shard_map/all_to_all | solution.py:543
  71.9 0.0 copy-done
  71.9 0.0 copy-start.1
  71.9 0.9 copy-done.1
  72.8 0.0 copy-start.2
  72.8 0.9 copy-done.2
  73.7 0.0 copy-start.3
  73.7 0.8 copy-done.3
  74.5 0.0 copy-start.5
  74.5 0.8 copy-done.5
  75.2 0.9 copy-done.6
  76.1 0.0 copy-start.7
  76.1 0.9 copy-done.7
  77.0 0.0 copy-start.4
  77.0 0.0 copy-start.8
  77.0 8.3 %shard_map.161 = (f32[96,256]{1,0:T(8,128)S(1)}, f32[96,256]{1,0:T(8,128)S(1)}, f32[96,256]{1,0:T(8,128)S(1)}, f32[32,256]{1,0:T(8,128)S(1)}) custom-call(s32[4,8192]{1,0:T(4,128)S(1)} %copy-done.2, f32[32,16,1024]{2,1,0:T(8,128)S(1)} %copy-done, s32[64,128]{1,0:T(8,128)S(1)} %copy-done.3, f32[64,3,128]{2,1,0:T(4,128)S(1)} %copy-done.7, ...), custom_call_target="tpu_custom_call" | custom-call | tf_op jit(solution)/shard_map/pallas_call | solution.py:428
  85.3 3.5 %all-to-all-done.1 = f32[128,16,128]{2,1,0:T(8,128)S(1)} async-done(((f32[128,16,128]{2,1,0:T(8,128)}), f32[128,16,128]{2,1,0:T(8,128)S(1)}, u32[]{:S(2)}, u32[]{:S(2)}) %all-to-all-start.1) | async-done | bytes 1048608 | tf_op jit(solution)/shard_map/all_to_all | solution.py:543
  88.8 0.0 copy-done.4
  88.8 0.0 copy-done.8
  88.8 0.0 copy-done.9
  88.8 4.0 %shard_map.162 = (f32[96,256]{1,0:T(8,128)S(1)}, f32[3,2048]{1,0:T(4,128)S(1)}, f32[3,2048]{1,0:T(4,128)S(1)}, f32[1,128]{1,0:T(1,128)S(1)}) custom-call(s32[5,1,128]{2,1,0:T(1,128)S(1)} %bitcast.13, f32[2048,128]{1,0:T(8,128)S(1)} %bitcast.9, s32[64,128]{1,0:T(8,128)S(1)} %copy-done.4, f32[96,256]{1,0:T(8,128)S(1)} %get-tuple-element.22.int_ref, ...), custom_call_target="tpu_custom_call" | custom-call | tf_op jit(solution)/shard_map/pallas_call | solution.py:468
  92.8 4.5 %collective-permute-start = (f32[3,2048]{1,0:T(4,128)S(1)}, f32[3,2048]{1,0:T(4,128)S(1)}, u32[]{:S(2)}, u32[]{:S(2)}) collective-permute-start(f32[3,2048]{1,0:T(4,128)S(1)} %get-tuple-element.25), channel_id=1, source_target_pairs={{0,1},{1,2},{2,3},{3,4},{4,5},{5,6},{6,7},{7,8},{8,9},{9,10},{10,1... | collective-permute-start | bytes 73736 | tf_op jit(solution)/shard_map/ppermute | solution.py:499
  97.3 1.9 %collective-permute-start.1 = (f32[3,2048]{1,0:T(4,128)S(1)}, f32[3,2048]{1,0:T(4,128)S(1)}, u32[]{:S(2)}, u32[]{:S(2)}) collective-permute-start(f32[3,2048]{1,0:T(4,128)S(1)} %get-tuple-element.26), channel_id=1, source_target_pairs={{1,0},{2,1},{3,2},{4,3},{5,4},{6,5},{7,6},{8,7},{9,8},{10,9},{11,1... | collective-permute-start | bytes 73736 | tf_op jit(solution)/shard_map/ppermute | solution.py:499
  99.3 0.0 collective-permute-done.low_ref
  99.3 6.0 %collective-permute-done.1.up_ref = f32[3,2048]{1,0:T(4,128)S(1)} collective-permute-done((f32[3,2048]{1,0:T(4,128)S(1)}, f32[3,2048]{1,0:T(4,128)S(1)}, u32[]{:S(2)}, u32[]{:S(2)}) %collective-permute-start.1) | collective-permute-done | bytes 24608 | tf_op jit(solution)/shard_map/ppermute | solution.py:499
  105.2 1.6 %shard_map.163 = (f32[3,8192]{1,0:T(4,128)}, f32[3,8192]{1,0:T(4,128)}) custom-call(f32[1,128]{1,0:T(1,128)S(1)} %get-tuple-element.23.lim_ref, f32[96,256]{1,0:T(8,128)S(1)} %get-tuple-element.24.tot_ref, s32[2,2048]{1,0:T(2,128)S(1)} %copy-done.8, f32[3,2048]{1,0:T(4,128)S(1)} %collective-permute-done.low_ref, ...), custom_call_target="tpu_custom_call" | custom-call | tf_op jit(solution)/shard_map/pallas_call | solution.py:486
  (2 shorter events, 0.0 us)
Async XLA Ops:
  5.2 29.8 %all-to-all-start = ((f32[128,5,4,128]{3,2,1,0:T(4,128)}), f32[128,5,4,128]{3,2,1,0:T(4,128)}, u32[]{:S(2)}, u32[]{:S(2)}) async-start(f32[128,5,4,128]{3,2,1,0:T(4,128)} %get-tuple-element.17), calls=%async_computation | async-start | bytes 2621440 | tf_op jit(solution)/shard_map/all_to_all | solution.py:523
  65.5 6.4 %copy-start = (f32[32,16,1024]{2,1,0:T(8,128)S(1)}, f32[32,16,1024]{2,1,0:T(8,128)}, u32[]{:S(2)}) copy-start(f32[32,16,1024]{2,1,0:T(8,128)} %get-tuple-element.20.force_ref) | copy-start | bytes 6291460
  65.5 23.3 %all-to-all-start.1 = ((f32[128,16,128]{2,1,0:T(8,128)}), f32[128,16,128]{2,1,0:T(8,128)S(1)}, u32[]{:S(2)}, u32[]{:S(2)}) async-start(f32[128,16,128]{2,1,0:T(8,128)} %bitcast.14), calls=%async_computation.1 | async-start | bytes 2097152 | tf_op jit(solution)/shard_map/all_to_all | solution.py:543
  71.9 0.9 copy-start.1
  72.8 0.9 copy-start.2
  73.7 0.8 copy-start.3
  74.5 0.8 copy-start.5
  75.2 0.9 copy-start.6
  76.1 0.9 copy-start.7
  77.0 11.8 %copy-start.4 = (s32[64,128]{1,0:T(8,128)S(1)}, s32[64,128]{1,0:T(8,128)}, u32[]{:S(2)}) copy-start(s32[64,128]{1,0:T(8,128)} %seg_ref.5) | copy-start | bytes 98308
  77.0 11.8 %copy-start.8 = (s32[2,2048]{1,0:T(2,128)S(1)}, s32[2,2048]{1,0:T(2,128)}, u32[]{:S(2)}) copy-start(s32[2,2048]{1,0:T(2,128)} %share_ref.3) | copy-start | bytes 49156
  77.0 11.8 %copy-start.9 = (s32[1,128,5]{1,0,2:T(1,128)S(1)}, s32[1,128,5]{1,0,2:T(1,128)}, u32[]{:S(2)}) copy-start(s32[1,128,5]{1,0,2:T(1,128)} %param.26) | copy-start | bytes 7684
  92.8 6.4 %collective-permute-start = (f32[3,2048]{1,0:T(4,128)S(1)}, f32[3,2048]{1,0:T(4,128)S(1)}, u32[]{:S(2)}, u32[]{:S(2)}) collective-permute-start(f32[3,2048]{1,0:T(4,128)S(1)} %get-tuple-element.25), channel_id=1, source_target_pairs={{0,1},{1,2},{2,3},{3,4},{4,5},{5,6},{6,7},{7,8},{8,9},{9,10},{10,1... | collective-permute-start | bytes 73736 | tf_op jit(solution)/shard_map/ppermute | solution.py:499
  97.3 7.9 %collective-permute-start.1 = (f32[3,2048]{1,0:T(4,128)S(1)}, f32[3,2048]{1,0:T(4,128)S(1)}, u32[]{:S(2)}, u32[]{:S(2)}) collective-permute-start(f32[3,2048]{1,0:T(4,128)S(1)} %get-tuple-element.26), channel_id=1, source_target_pairs={{1,0},{2,1},{3,2},{4,3},{5,4},{6,5},{7,6},{8,7},{9,8},{10,9},{11,1... | collective-permute-start | bytes 73736 | tf_op jit(solution)/shard_map/ppermute | solution.py:499

commit v9 on v8

--- a/solution.py
+++ b/solution.py
@@ -338,7 +338,7 @@
         acc[...] += add_hot(spread(rows, idx, high), low_hot(idx))
         return carry
 
-    lax.fori_loop(0, blocks // group, some, 0, unroll=8)
+    lax.fori_loop(0, blocks // group, some, 0, unroll=4)
     size = 3 * high
     tot_ref[...] = ((acc[2 * size :] + acc[size : 2 * size]) + acc[:size]) + int_ref[...]
     split_table(cut, tot_ref)

time: 108 us -> 107 us (level)
  starting transfers between devices: 23 us -> 29.5 us
  Pallas kernels: 59.9 us -> 53.5 us
    all_to_all x1, starting transfers between devices: 6.39 us -> 12.8 us  [shards(): lax.all_to_all(far_force.reshape(peers, 16, -1), ('grp', 'dev'), split_ax...]
    pallas_call x1, Pallas kernels: 30.5 us -> 25.1 us  [contact_call(): pl.pallas_call(contact_body, out_shape=(struct(blocks, 3, seg), struct(pe...]
where the time goes in v9:
time: 107 us
  Pallas kernels  53.5 us (50%)
  starting transfers between devices  29.5 us (28%)
  waiting for transfers between devices  18 us (17%)
  local copies, waits for them, and re-layouts  5.14 us (5%)
    pallas_call x1, Pallas kernels, contact_call(): pl.pallas_call(contact_body, out_shape=(struct(blocks, 3, seg), struct(pe...  25.1 us
    all_to_all x1, starting transfers between devices, shards(): lax.all_to_all(far_force.reshape(peers, 16, -1), ('grp', 'dev'), split_ax...  12.8 us
    pallas_call x1, Pallas kernels, force_call(): pl.pallas_call(force_body, out_shape=(struct(nodes.shape[1] // WIDTH, 16,...  10.9 us
    all_to_all x1, starting transfers between devices, shards(): lax.all_to_all(outgoing, ('grp', 'dev'), split_axis=0, concat_axis=0, til...  10.3 us
    all_to_all x1, waiting for transfers between devices, shards(): lax.all_to_all(outgoing, ('grp', 'dev'), split_axis=0, concat_axis=0, til...  8.59 us
    pallas_call x1, Pallas kernels, scatter_call(): pl.pallas_call(scatter_body, out_shape=(struct(3 * high, LOW), struct(3 *...  8.31 us
    ppermute x2, starting transfers between devices, shifted(): lax.ppermute(value, axis, [(source, source + steps) for source in range(f...  6.4 us
    ppermute x2, waiting for transfers between devices, shifted(): lax.ppermute(value, axis, [(source, source + steps) for source in range(f...  5.98 us
  transfers between devices with their start and end apart: 4, of which 3 were waited for; matrix products, arithmetic and copies ran while one was open for 0% of the time, Pallas kernels for 18%

profile of v9, /device:TPU:96, one launch (start us, length us, event | category | flops | bytes accessed | tf_op | source)
XLA Modules:
  0.0 106.9 jit_solution(7383901618016737354)
XLA Ops:
  0.6 4.6 %shard_map.158 = (f32[64,4,128]{2,1,0:T(4,128)}, f32[128,5,4,128]{3,2,1,0:T(4,128)}) custom-call(s32[5,1,128]{2,1,0:T(1,128)} %bitcast.12, f32[3,8192]{1,0:T(4,128)} %disp_ref.5, f32[3,8192]{1,0:T(4,128)} %ref_ref.1, s32[64,128]{1,0:T(8,128)} %seg_ref.5, s32[64,128]{1,0:T(8,128)} %mask_ref.1), custom_call_target="tpu_custom_call" | custom-call | tf_op jit(solution)/shard_map/pallas_call | solution.py:399
  5.2 10.3 %all-to-all-start = ((f32[128,5,4,128]{3,2,1,0:T(4,128)}), f32[128,5,4,128]{3,2,1,0:T(4,128)}, u32[]{:S(2)}, u32[]{:S(2)}) async-start(f32[128,5,4,128]{3,2,1,0:T(4,128)} %get-tuple-element.17), calls=%async_computation | async-start | bytes 2621440 | tf_op jit(solution)/shard_map/all_to_all | solution.py:523
  15.5 10.9 %shard_map.159 = (f32[32,16,1024]{2,1,0:T(8,128)}, f32[1,128]{1,0:T(1,128)}) custom-call(s32[1]{0:T(128)} %bitcast.3.first_ref, f32[4]{0:T(128)} %stiff_ref.1, f32[3,8192]{1,0:T(4,128)} %disp_ref.5, f32[1,8192]{1,0:T(1,128)} %bitcast.10, s32[4,8192]{1,0:T(4,128)} %nodes_ref.3, s32[1,8192]{1,0:T(1,128)} %bitcast.15, f32[1,8192]{1,0:T(1,128)} %bitcast.16), custom_call_target="tpu_custom_call" | custom-call | tf_op jit(solution)/shard_map/pallas_call | solution.py:413
  26.4 8.6 %all-to-all-done = f32[128,5,4,128]{3,2,1,0:T(4,128)} async-done(((f32[128,5,4,128]{3,2,1,0:T(4,128)}), f32[128,5,4,128]{3,2,1,0:T(4,128)}, u32[]{:S(2)}, u32[]{:S(2)}) %all-to-all-start) | async-done | bytes 1310752 | tf_op jit(solution)/shard_map/all_to_all | solution.py:523
  35.0 25.1 %shard_map.160 = (f32[64,3,128]{2,1,0:T(4,128)}, f32[2048,128]{1,0:T(8,128)}) custom-call(s32[512]{0:T(512)} %near_ref.1, s32[512]{0:T(512)} %far_ref.1, f32[64,4,128]{2,1,0:T(4,128)} %get-tuple-element.16.own_ref, f32[640,4,128]{2,1,0:T(4,128)} %bitcast.1.recv_ref, s32[4,128]{1,0:T(4,128)} %bitcast.17, f32[1,128]{1,0:T(1,128)} %get-tuple-element.18.lim_ref), custom_call_target="tpu_custom_call" | custom-call | tf_op jit(solution)/shard_map/pallas_call | solution.py:444
  60.1 0.0 copy-start
  60.1 12.8 %all-to-all-start.1 = ((f32[128,16,128]{2,1,0:T(8,128)}), f32[128,16,128]{2,1,0:T(8,128)S(1)}, u32[]{:S(2)}, u32[]{:S(2)}) async-start(f32[128,16,128]{2,1,0:T(8,128)} %bitcast.14), calls=%async_computation.1 | async-start | bytes 2097152 | tf_op jit(solution)/shard_map/all_to_all | solution.py:543
  72.9 0.0 copy-done
  72.9 0.0 copy-start.1
  72.9 0.9 copy-done.1
  73.8 0.9 copy-done.2
  74.7 0.0 copy-start.3
  74.7 0.8 copy-done.3
  75.5 0.0 copy-start.5
  75.5 0.8 copy-done.5
  76.2 0.0 copy-start.6
  76.2 0.9 copy-done.6
  77.1 0.0 copy-start.7
  77.2 0.9 copy-done.7
  78.1 0.0 copy-start.4
  78.1 0.0 copy-start.8
  78.1 8.3 %shard_map.161 = (f32[96,256]{1,0:T(8,128)S(1)}, f32[96,256]{1,0:T(8,128)S(1)}, f32[96,256]{1,0:T(8,128)S(1)}, f32[32,256]{1,0:T(8,128)S(1)}) custom-call(s32[4,8192]{1,0:T(4,128)S(1)} %copy-done.2, f32[32,16,1024]{2,1,0:T(8,128)S(1)} %copy-done, s32[64,128]{1,0:T(8,128)S(1)} %copy-done.3, f32[64,3,128]{2,1,0:T(4,128)S(1)} %copy-done.7, ...), custom_call_target="tpu_custom_call" | custom-call | tf_op jit(solution)/shard_map/pallas_call | solution.py:428
  86.4 3.5 %all-to-all-done.1 = f32[128,16,128]{2,1,0:T(8,128)S(1)} async-done(((f32[128,16,128]{2,1,0:T(8,128)}), f32[128,16,128]{2,1,0:T(8,128)S(1)}, u32[]{:S(2)}, u32[]{:S(2)}) %all-to-all-start.1) | async-done | bytes 1048608 | tf_op jit(solution)/shard_map/all_to_all | solution.py:543
  89.8 0.0 copy-done.4
  89.8 0.0 copy-done.8
  89.8 0.0 copy-done.9
  89.8 3.0 %shard_map.162 = (f32[96,256]{1,0:T(8,128)S(1)}, f32[3,2048]{1,0:T(4,128)S(1)}, f32[3,2048]{1,0:T(4,128)S(1)}, f32[1,128]{1,0:T(1,128)S(1)}) custom-call(s32[5,1,128]{2,1,0:T(1,128)S(1)} %bitcast.13, f32[2048,128]{1,0:T(8,128)S(1)} %bitcast.9, s32[64,128]{1,0:T(8,128)S(1)} %copy-done.4, f32[96,256]{1,0:T(8,128)S(1)} %get-tuple-element.22.int_ref, ...), custom_call_target="tpu_custom_call" | custom-call | tf_op jit(solution)/shard_map/pallas_call | solution.py:468
  92.9 4.5 %collective-permute-start = (f32[3,2048]{1,0:T(4,128)S(1)}, f32[3,2048]{1,0:T(4,128)S(1)}, u32[]{:S(2)}, u32[]{:S(2)}) collective-permute-start(f32[3,2048]{1,0:T(4,128)S(1)} %get-tuple-element.25), channel_id=1, source_target_pairs={{0,1},{1,2},{2,3},{3,4},{4,5},{5,6},{6,7},{7,8},{8,9},{9,10},{10,1... | collective-permute-start | bytes 73736 | tf_op jit(solution)/shard_map/ppermute | solution.py:499
  97.4 1.9 %collective-permute-start.1 = (f32[3,2048]{1,0:T(4,128)S(1)}, f32[3,2048]{1,0:T(4,128)S(1)}, u32[]{:S(2)}, u32[]{:S(2)}) collective-permute-start(f32[3,2048]{1,0:T(4,128)S(1)} %get-tuple-element.26), channel_id=1, source_target_pairs={{1,0},{2,1},{3,2},{4,3},{5,4},{6,5},{7,6},{8,7},{9,8},{10,9},{11,1... | collective-permute-start | bytes 73736 | tf_op jit(solution)/shard_map/ppermute | solution.py:499
  99.3 0.0 collective-permute-done.low_ref
  99.3 6.0 %collective-permute-done.1.up_ref = f32[3,2048]{1,0:T(4,128)S(1)} collective-permute-done((f32[3,2048]{1,0:T(4,128)S(1)}, f32[3,2048]{1,0:T(4,128)S(1)}, u32[]{:S(2)}, u32[]{:S(2)}) %collective-permute-start.1) | collective-permute-done | bytes 24608 | tf_op jit(solution)/shard_map/ppermute | solution.py:499
  105.3 1.6 %shard_map.163 = (f32[3,8192]{1,0:T(4,128)}, f32[3,8192]{1,0:T(4,128)}) custom-call(f32[1,128]{1,0:T(1,128)S(1)} %get-tuple-element.23.lim_ref, f32[96,256]{1,0:T(8,128)S(1)} %get-tuple-element.24.tot_ref, s32[2,2048]{1,0:T(2,128)S(1)} %copy-done.8, f32[3,2048]{1,0:T(4,128)S(1)} %collective-permute-done.low_ref, ...), custom_call_target="tpu_custom_call" | custom-call | tf_op jit(solution)/shard_map/pallas_call | solution.py:486
  (2 shorter events, 0.0 us)
Async XLA Ops:
  5.2 29.8 %all-to-all-start = ((f32[128,5,4,128]{3,2,1,0:T(4,128)}), f32[128,5,4,128]{3,2,1,0:T(4,128)}, u32[]{:S(2)}, u32[]{:S(2)}) async-start(f32[128,5,4,128]{3,2,1,0:T(4,128)} %get-tuple-element.17), calls=%async_computation | async-start | bytes 2621440 | tf_op jit(solution)/shard_map/all_to_all | solution.py:523
  60.1 12.8 %copy-start = (f32[32,16,1024]{2,1,0:T(8,128)S(1)}, f32[32,16,1024]{2,1,0:T(8,128)}, u32[]{:S(2)}) copy-start(f32[32,16,1024]{2,1,0:T(8,128)} %get-tuple-element.20.force_ref) | copy-start | bytes 6291460
  60.1 29.8 %all-to-all-start.1 = ((f32[128,16,128]{2,1,0:T(8,128)}), f32[128,16,128]{2,1,0:T(8,128)S(1)}, u32[]{:S(2)}, u32[]{:S(2)}) async-start(f32[128,16,128]{2,1,0:T(8,128)} %bitcast.14), calls=%async_computation.1 | async-start | bytes 2097152 | tf_op jit(solution)/shard_map/all_to_all | solution.py:543
  72.9 0.9 copy-start.1
  73.8 0.9 copy-start.2
  74.7 0.8 copy-start.3
  75.5 0.8 copy-start.5
  76.2 0.9 copy-start.6
  77.1 0.9 copy-start.7
  78.1 11.8 %copy-start.4 = (s32[64,128]{1,0:T(8,128)S(1)}, s32[64,128]{1,0:T(8,128)}, u32[]{:S(2)}) copy-start(s32[64,128]{1,0:T(8,128)} %seg_ref.5) | copy-start | bytes 98308
  78.1 11.8 %copy-start.8 = (s32[2,2048]{1,0:T(2,128)S(1)}, s32[2,2048]{1,0:T(2,128)}, u32[]{:S(2)}) copy-start(s32[2,2048]{1,0:T(2,128)} %share_ref.3) | copy-start | bytes 49156
  78.1 11.8 %copy-start.9 = (s32[1,128,5]{1,0,2:T(1,128)S(1)}, s32[1,128,5]{1,0,2:T(1,128)}, u32[]{:S(2)}) copy-start(s32[1,128,5]{1,0,2:T(1,128)} %param.26) | copy-start | bytes 7684
  92.9 6.4 %collective-permute-start = (f32[3,2048]{1,0:T(4,128)S(1)}, f32[3,2048]{1,0:T(4,128)S(1)}, u32[]{:S(2)}, u32[]{:S(2)}) collective-permute-start(f32[3,2048]{1,0:T(4,128)S(1)} %get-tuple-element.25), channel_id=1, source_target_pairs={{0,1},{1,2},{2,3},{3,4},{4,5},{5,6},{6,7},{7,8},{8,9},{9,10},{10,1... | collective-permute-start | bytes 73736 | tf_op jit(solution)/shard_map/ppermute | solution.py:499
  97.4 7.9 %collective-permute-start.1 = (f32[3,2048]{1,0:T(4,128)S(1)}, f32[3,2048]{1,0:T(4,128)S(1)}, u32[]{:S(2)}, u32[]{:S(2)}) collective-permute-start(f32[3,2048]{1,0:T(4,128)S(1)} %get-tuple-element.26), channel_id=1, source_target_pairs={{1,0},{2,1},{3,2},{4,3},{5,4},{6,5},{7,6},{8,7},{9,8},{10,9},{11,1... | collective-permute-start | bytes 73736 | tf_op jit(solution)/shard_map/ppermute | solution.py:499

commit v10 on v9

--- a/solution.py
+++ b/solution.py
@@ -112,7 +112,7 @@
             out_ref[d, c] = own_ref[send_ref[c, 0, d]]
         return carry
 
-    lax.fori_loop(0, peers, send, 0, unroll=8)
+    lax.fori_loop(0, peers, send, 0, unroll=16)
 
 
 def force_body(

time: 107 us -> 107 us (level)
  Pallas kernels: 53.5 us -> 48.2 us
  starting transfers between devices: 29.5 us -> 34.8 us
    all_to_all x1, starting transfers between devices: 12.8 us -> 18.1 us  [shards(): lax.all_to_all(far_force.reshape(peers, 16, -1), ('grp', 'dev'), split_ax...]
    pallas_call x1, Pallas kernels: 25.1 us -> 19.8 us  [contact_call(): pl.pallas_call(contact_body, out_shape=(struct(blocks, 3, seg), struct(pe...]
where the time goes in v10:
time: 107 us
  Pallas kernels  48.2 us (45%)
  starting transfers between devices  34.8 us (33%)
  waiting for transfers between devices  18 us (17%)
  local copies, waits for them, and re-layouts  5.14 us (5%)
    pallas_call x1, Pallas kernels, contact_call(): pl.pallas_call(contact_body, out_shape=(struct(blocks, 3, seg), struct(pe...  19.8 us
    all_to_all x1, starting transfers between devices, shards(): lax.all_to_all(far_force.reshape(peers, 16, -1), ('grp', 'dev'), split_ax...  18.1 us
    pallas_call x1, Pallas kernels, force_call(): pl.pallas_call(force_body, out_shape=(struct(nodes.shape[1] // WIDTH, 16,...  10.9 us
    all_to_all x1, starting transfers between devices, shards(): lax.all_to_all(outgoing, ('grp', 'dev'), split_axis=0, concat_axis=0, til...  10.3 us
    all_to_all x1, waiting for transfers between devices, shards(): lax.all_to_all(outgoing, ('grp', 'dev'), split_axis=0, concat_axis=0, til...  8.59 us
    pallas_call x1, Pallas kernels, scatter_call(): pl.pallas_call(scatter_body, out_shape=(struct(3 * high, LOW), struct(3 *...  8.32 us
    ppermute x2, starting transfers between devices, shifted(): lax.ppermute(value, axis, [(source, source + steps) for source in range(f...  6.4 us
    ppermute x2, waiting for transfers between devices, shifted(): lax.ppermute(value, axis, [(source, source + steps) for source in range(f...  5.98 us
  transfers between devices with their start and end apart: 4, of which 3 were waited for; matrix products, arithmetic and copies ran while one was open for 0% of the time, Pallas kernels for 18%

profile of v10, /device:TPU:96, one launch (start us, length us, event | category | flops | bytes accessed | tf_op | source)
XLA Modules:
  0.0 106.9 jit_solution(446798453229198107)
XLA Ops:
  0.6 4.6 %shard_map.158 = (f32[64,4,128]{2,1,0:T(4,128)}, f32[128,5,4,128]{3,2,1,0:T(4,128)}) custom-call(s32[5,1,128]{2,1,0:T(1,128)} %bitcast.12, f32[3,8192]{1,0:T(4,128)} %disp_ref.5, f32[3,8192]{1,0:T(4,128)} %ref_ref.1, s32[64,128]{1,0:T(8,128)} %seg_ref.5, s32[64,128]{1,0:T(8,128)} %mask_ref.1), custom_call_target="tpu_custom_call" | custom-call | tf_op jit(solution)/shard_map/pallas_call | solution.py:399
  5.2 10.3 %all-to-all-start = ((f32[128,5,4,128]{3,2,1,0:T(4,128)}), f32[128,5,4,128]{3,2,1,0:T(4,128)}, u32[]{:S(2)}, u32[]{:S(2)}) async-start(f32[128,5,4,128]{3,2,1,0:T(4,128)} %get-tuple-element.17), calls=%async_computation | async-start | bytes 2621440 | tf_op jit(solution)/shard_map/all_to_all | solution.py:523
  15.5 10.9 %shard_map.159 = (f32[32,16,1024]{2,1,0:T(8,128)}, f32[1,128]{1,0:T(1,128)}) custom-call(s32[1]{0:T(128)} %bitcast.3.first_ref, f32[4]{0:T(128)} %stiff_ref.1, f32[3,8192]{1,0:T(4,128)} %disp_ref.5, f32[1,8192]{1,0:T(1,128)} %bitcast.10, s32[4,8192]{1,0:T(4,128)} %nodes_ref.3, s32[1,8192]{1,0:T(1,128)} %bitcast.15, f32[1,8192]{1,0:T(1,128)} %bitcast.16), custom_call_target="tpu_custom_call" | custom-call | tf_op jit(solution)/shard_map/pallas_call | solution.py:413
  26.4 8.6 %all-to-all-done = f32[128,5,4,128]{3,2,1,0:T(4,128)} async-done(((f32[128,5,4,128]{3,2,1,0:T(4,128)}), f32[128,5,4,128]{3,2,1,0:T(4,128)}, u32[]{:S(2)}, u32[]{:S(2)}) %all-to-all-start) | async-done | bytes 1310752 | tf_op jit(solution)/shard_map/all_to_all | solution.py:523
  35.0 19.8 %shard_map.160 = (f32[64,3,128]{2,1,0:T(4,128)}, f32[2048,128]{1,0:T(8,128)}) custom-call(s32[512]{0:T(512)} %near_ref.1, s32[512]{0:T(512)} %far_ref.1, f32[64,4,128]{2,1,0:T(4,128)} %get-tuple-element.16.own_ref, f32[640,4,128]{2,1,0:T(4,128)} %bitcast.1.recv_ref, s32[4,128]{1,0:T(4,128)} %bitcast.17, f32[1,128]{1,0:T(1,128)} %get-tuple-element.18.lim_ref), custom_call_target="tpu_custom_call" | custom-call | tf_op jit(solution)/shard_map/pallas_call | solution.py:444
  54.8 0.0 copy-start
  54.8 18.1 %all-to-all-start.1 = ((f32[128,16,128]{2,1,0:T(8,128)}), f32[128,16,128]{2,1,0:T(8,128)S(1)}, u32[]{:S(2)}, u32[]{:S(2)}) async-start(f32[128,16,128]{2,1,0:T(8,128)} %bitcast.14), calls=%async_computation.1 | async-start | bytes 2097152 | tf_op jit(solution)/shard_map/all_to_all | solution.py:543
  72.9 0.0 copy-done
  72.9 0.0 copy-start.1
  73.0 0.9 copy-done.1
  73.9 0.0 copy-start.2
  73.9 0.9 copy-done.2
  74.8 0.0 copy-start.3
  74.8 0.8 copy-done.3
  75.5 0.0 copy-start.5
  75.5 0.8 copy-done.5
  76.3 0.0 copy-start.6
  76.3 0.9 copy-done.6
  77.2 0.0 copy-start.7
  77.2 0.9 copy-done.7
  78.1 0.0 copy-start.4
  78.1 8.3 %shard_map.161 = (f32[96,256]{1,0:T(8,128)S(1)}, f32[96,256]{1,0:T(8,128)S(1)}, f32[96,256]{1,0:T(8,128)S(1)}, f32[32,256]{1,0:T(8,128)S(1)}) custom-call(s32[4,8192]{1,0:T(4,128)S(1)} %copy-done.2, f32[32,16,1024]{2,1,0:T(8,128)S(1)} %copy-done, s32[64,128]{1,0:T(8,128)S(1)} %copy-done.3, f32[64,3,128]{2,1,0:T(4,128)S(1)} %copy-done.7, ...), custom_call_target="tpu_custom_call" | custom-call | tf_op jit(solution)/shard_map/pallas_call | solution.py:428
  86.4 3.4 %all-to-all-done.1 = f32[128,16,128]{2,1,0:T(8,128)S(1)} async-done(((f32[128,16,128]{2,1,0:T(8,128)}), f32[128,16,128]{2,1,0:T(8,128)S(1)}, u32[]{:S(2)}, u32[]{:S(2)}) %all-to-all-start.1) | async-done | bytes 1048608 | tf_op jit(solution)/shard_map/all_to_all | solution.py:543
  89.9 0.0 copy-done.4
  89.9 0.0 copy-done.8
  89.9 0.0 copy-done.9
  89.9 3.0 %shard_map.162 = (f32[96,256]{1,0:T(8,128)S(1)}, f32[3,2048]{1,0:T(4,128)S(1)}, f32[3,2048]{1,0:T(4,128)S(1)}, f32[1,128]{1,0:T(1,128)S(1)}) custom-call(s32[5,1,128]{2,1,0:T(1,128)S(1)} %bitcast.13, f32[2048,128]{1,0:T(8,128)S(1)} %bitcast.9, s32[64,128]{1,0:T(8,128)S(1)} %copy-done.4, f32[96,256]{1,0:T(8,128)S(1)} %get-tuple-element.22.int_ref, ...), custom_call_target="tpu_custom_call" | custom-call | tf_op jit(solution)/shard_map/pallas_call | solution.py:468
  92.9 4.5 %collective-permute-start = (f32[3,2048]{1,0:T(4,128)S(1)}, f32[3,2048]{1,0:T(4,128)S(1)}, u32[]{:S(2)}, u32[]{:S(2)}) collective-permute-start(f32[3,2048]{1,0:T(4,128)S(1)} %get-tuple-element.25), channel_id=1, source_target_pairs={{0,1},{1,2},{2,3},{3,4},{4,5},{5,6},{6,7},{7,8},{8,9},{9,10},{10,1... | collective-permute-start | bytes 73736 | tf_op jit(solution)/shard_map/ppermute | solution.py:499
  97.4 1.9 %collective-permute-start.1 = (f32[3,2048]{1,0:T(4,128)S(1)}, f32[3,2048]{1,0:T(4,128)S(1)}, u32[]{:S(2)}, u32[]{:S(2)}) collective-permute-start(f32[3,2048]{1,0:T(4,128)S(1)} %get-tuple-element.26), channel_id=1, source_target_pairs={{1,0},{2,1},{3,2},{4,3},{5,4},{6,5},{7,6},{8,7},{9,8},{10,9},{11,1... | collective-permute-start | bytes 73736 | tf_op jit(solution)/shard_map/ppermute | solution.py:499
  99.3 0.0 collective-permute-done.low_ref
  99.3 6.0 %collective-permute-done.1.up_ref = f32[3,2048]{1,0:T(4,128)S(1)} collective-permute-done((f32[3,2048]{1,0:T(4,128)S(1)}, f32[3,2048]{1,0:T(4,128)S(1)}, u32[]{:S(2)}, u32[]{:S(2)}) %collective-permute-start.1) | collective-permute-done | bytes 24608 | tf_op jit(solution)/shard_map/ppermute | solution.py:499
  105.3 1.6 %shard_map.163 = (f32[3,8192]{1,0:T(4,128)}, f32[3,8192]{1,0:T(4,128)}) custom-call(f32[1,128]{1,0:T(1,128)S(1)} %get-tuple-element.23.lim_ref, f32[96,256]{1,0:T(8,128)S(1)} %get-tuple-element.24.tot_ref, s32[2,2048]{1,0:T(2,128)S(1)} %copy-done.8, f32[3,2048]{1,0:T(4,128)S(1)} %collective-permute-done.low_ref, ...), custom_call_target="tpu_custom_call" | custom-call | tf_op jit(solution)/shard_map/pallas_call | solution.py:486
  (2 shorter events, 0.0 us)
Async XLA Ops:
  5.2 29.8 %all-to-all-start = ((f32[128,5,4,128]{3,2,1,0:T(4,128)}), f32[128,5,4,128]{3,2,1,0:T(4,128)}, u32[]{:S(2)}, u32[]{:S(2)}) async-start(f32[128,5,4,128]{3,2,1,0:T(4,128)} %get-tuple-element.17), calls=%async_computation | async-start | bytes 2621440 | tf_op jit(solution)/shard_map/all_to_all | solution.py:523
  54.8 18.2 %copy-start = (f32[32,16,1024]{2,1,0:T(8,128)S(1)}, f32[32,16,1024]{2,1,0:T(8,128)}, u32[]{:S(2)}) copy-start(f32[32,16,1024]{2,1,0:T(8,128)} %get-tuple-element.20.force_ref) | copy-start | bytes 6291460
  54.8 35.1 %all-to-all-start.1 = ((f32[128,16,128]{2,1,0:T(8,128)}), f32[128,16,128]{2,1,0:T(8,128)S(1)}, u32[]{:S(2)}, u32[]{:S(2)}) async-start(f32[128,16,128]{2,1,0:T(8,128)} %bitcast.14), calls=%async_computation.1 | async-start | bytes 2097152 | tf_op jit(solution)/shard_map/all_to_all | solution.py:543
  72.9 0.9 copy-start.1
  73.9 0.9 copy-start.2
  74.8 0.8 copy-start.3
  75.5 0.8 copy-start.5
  76.3 0.9 copy-start.6
  77.2 0.9 copy-start.7
  78.1 11.8 %copy-start.4 = (s32[64,128]{1,0:T(8,128)S(1)}, s32[64,128]{1,0:T(8,128)}, u32[]{:S(2)}) copy-start(s32[64,128]{1,0:T(8,128)} %seg_ref.5) | copy-start | bytes 98308
  78.1 11.8 %copy-start.8 = (s32[2,2048]{1,0:T(2,128)S(1)}, s32[2,2048]{1,0:T(2,128)}, u32[]{:S(2)}) copy-start(s32[2,2048]{1,0:T(2,128)} %share_ref.3) | copy-start | bytes 49156
  78.1 11.8 %copy-start.9 = (s32[1,128,5]{1,0,2:T(1,128)S(1)}, s32[1,128,5]{1,0,2:T(1,128)}, u32[]{:S(2)}) copy-start(s32[1,128,5]{1,0,2:T(1,128)} %param.26) | copy-start | bytes 7684
  92.9 6.4 %collective-permute-start = (f32[3,2048]{1,0:T(4,128)S(1)}, f32[3,2048]{1,0:T(4,128)S(1)}, u32[]{:S(2)}, u32[]{:S(2)}) collective-permute-start(f32[3,2048]{1,0:T(4,128)S(1)} %get-tuple-element.25), channel_id=1, source_target_pairs={{0,1},{1,2},{2,3},{3,4},{4,5},{5,6},{6,7},{7,8},{8,9},{9,10},{10,1... | collective-permute-start | bytes 73736 | tf_op jit(solution)/shard_map/ppermute | solution.py:499
  97.4 7.9 %collective-permute-start.1 = (f32[3,2048]{1,0:T(4,128)S(1)}, f32[3,2048]{1,0:T(4,128)S(1)}, u32[]{:S(2)}, u32[]{:S(2)}) collective-permute-start(f32[3,2048]{1,0:T(4,128)S(1)} %get-tuple-element.26), channel_id=1, source_target_pairs={{1,0},{2,1},{3,2},{4,3},{5,4},{6,5},{7,6},{8,7},{9,8},{10,9},{11,1... | collective-permute-start | bytes 73736 | tf_op jit(solution)/shard_map/ppermute | solution.py:499
